TPU v7x, 512 devices: a whole 4x8x8 slice. The times are simulated.
512 devices in a mesh: ctx: 64 (over x, z, core), head: 8 (over y).
Axes of the slice: x: 4, y: 8, z: 8, core: 2. Of those that a mesh axis runs over, the one named last changes fastest.
Arguments:
- query_rows: bfloat16 [65536, 1024], P('ctx', 'head'), may hold values from -8 to 8
- key_rows: bfloat16 [65536, 1024], P('ctx', 'head'), may hold values from -8 to 8
- value_rows: bfloat16 [65536, 1024], P('ctx', 'head'), may hold values from -6 to 6
- out_grad: bfloat16 [65536, 1024], P('ctx', 'head'), may hold values from -6 to 6
- out_weight: bfloat16 [1024, 1024], P('head'), may hold values from -0.1875 to 0.1875
- neighbours: int32 [512, 12], replicated, may hold values from 0 to 511, as said below
- counts: int32 [512], replicated, may hold values from 3 to 12, as said below
Outputs:
- query_grad: bfloat16 [65536, 1024], P('ctx', 'head')
- key_grad: bfloat16 [65536, 1024], P('ctx', 'head')
- value_grad: bfloat16 [65536, 1024], P('ctx', 'head')
- weight_grad: float32 [1024, 1024], P('head')
Inputs may be any that keep to these rules, and one draw needn't show every extreme that they name: `neighbours`: row g names block g in slot 0, then distinct blocks held by ctx indices g // 8 - 1 to g // 8 + 1; slots 1 and 2 include a block of each of the ctx indices g // 8 - 1 and g // 8 + 1 that exists; slots from counts[g] on hold g again. `counts`: block 0 uses all 12 slots.
All inputs are finite; a program needn't handle non-finite values.
Results may differ from a plain program's by a relative error of at most 0.012.
The roundings to bfloat16 on the way count: a program that leaves them out, or rounds other values in their place, can miss the bound.
Values may be sent and summed in bfloat16 or wider, within the bound.
No kernel may reach another device: no remote copies, remote signals or barrier semaphores. Data moves between devices by JAX's collectives and lax.ppermute only.
A program may use at most 64 MiB of HBM per device.

v0:
```python
import jax
import jax.numpy as jnp
from jax import lax
from jax.sharding import PartitionSpec as P

HD = 64
BS = 128


def with_halo(cells, sides, width):
    for axis, dim in sides:
        count = lax.axis_size(axis)
        ends = count - 1
        head = lax.slice_in_dim(cells, 0, width, axis=dim)
        tail = lax.slice_in_dim(cells, cells.shape[dim] - width, cells.shape[dim], axis=dim)
        cells = jnp.concatenate(
            [
                lax.ppermute(tail, axis, [(i, (i + 1) % count) for i in range(ends)]),
                cells,
                lax.ppermute(head, axis, [((i + 1) % count, i) for i in range(ends)]),
            ],
            axis=dim,
        )
    return cells


def shifted(x, axis, by):
    count = lax.axis_size(axis)
    pairs = [(i, i + by) for i in range(count) if 0 <= i + by < count]
    return lax.ppermute(x, axis, pairs)


def head_scores(query_block, key_block, factor):
    return (
        jnp.einsum("qhd,khd->hqk", query_block, key_block, preferred_element_type=jnp.float32)
        * factor
    )


def masked_scores(query_block, key_block, usable, factor):
    key_mask = jnp.repeat(usable, key_block.shape[0] // usable.shape[0])
    return jnp.where(key_mask[None, None, :], head_scores(query_block, key_block, factor), -1e30)


def padded_forward(query_block, key_block, value_block, usable, factor):
    scores = masked_scores(query_block, key_block, usable, factor)
    highest = jnp.max(scores, axis=2)
    log_total = highest + jnp.log(jnp.sum(jnp.exp(scores - highest[:, :, None]), axis=2))
    soft_weights = jnp.exp(scores - log_total[:, :, None]).astype(jnp.bfloat16)
    attended = jnp.einsum(
        "hqk,khd->qhd", soft_weights, value_block, preferred_element_type=jnp.float32
    )
    return (attended.astype(jnp.bfloat16), log_total)


def pair_backward(
    query_block, grad_block, log_total, dot_block, key_block, value_block, usable, factor
):
    scores = masked_scores(query_block, key_block, usable, factor)
    soft_full = jnp.exp(scores - log_total[:, :, None])
    grad_weights = jnp.einsum(
        "qhd,khd->hqk", grad_block, value_block, preferred_element_type=jnp.float32
    )
    grad_scores = (soft_full * (grad_weights - dot_block[:, :, None])).astype(jnp.bfloat16)
    grad_query = (
        jnp.einsum("hqk,khd->qhd", grad_scores, key_block, preferred_element_type=jnp.float32)
        * factor
    )
    grad_key = (
        jnp.einsum("hqk,qhd->khd", grad_scores, query_block, preferred_element_type=jnp.float32)
        * factor
    )
    grad_value = jnp.einsum(
        "hqk,qhd->khd",
        soft_full.astype(jnp.bfloat16),
        grad_block,
        preferred_element_type=jnp.float32,
    )
    return (grad_query, grad_key, grad_value)


def body(query_rows, key_rows, value_rows, out_grad, out_weight, neighbours, counts):
    row_count, col_count = query_rows.shape
    head_count = col_count // HD
    blocks = row_count // BS
    extent = 3 * blocks
    slot_total = neighbours.shape[1]
    block_total = counts.shape[0]
    factor = HD ** (-0.5)
    ctx_index = lax.axis_index("ctx")
    offset = (ctx_index - 1) * blocks
    packed = jnp.concatenate([key_rows, value_rows], axis=1)
    window = with_halo(packed, (("ctx", 0),), row_count)
    window = window.reshape(extent, BS, 2 * col_count)
    slot_ids = jnp.arange(slot_total, dtype=jnp.int32)
    query_blocks = query_rows.reshape(blocks, BS, head_count, HD)

    def fetch_all(places):
        picked = window[places]
        key_block = picked[:, :, :col_count].reshape(slot_total * BS, head_count, HD)
        value_block = picked[:, :, col_count:].reshape(slot_total * BS, head_count, HD)
        return (key_block, value_block)

    def slot_table(block_id):
        inside = (block_id >= 0) & (block_id < block_total)
        clamped = jnp.clip(block_id, 0, block_total - 1)
        relative = neighbours[clamped] - offset
        places = jnp.clip(relative, 0, extent - 1)
        active = jnp.where(inside, counts[clamped], 0)
        return (relative, places, active)

    def forward_block(block_index):
        relative, places, active = slot_table(ctx_index * blocks + block_index)
        query_block = query_blocks[block_index]
        key_block, value_block = fetch_all(places)
        return padded_forward(query_block, key_block, value_block, slot_ids < active, factor)

    attended_blocks, log_totals = lax.map(forward_block, jnp.arange(blocks, dtype=jnp.int32))
    attended = attended_blocks.reshape(row_count, col_count)
    shard_piece = lax.all_gather(out_grad, "head", axis=1, tiled=True)
    grad_sum = jnp.einsum("ro,jo->rj", shard_piece, out_weight, preferred_element_type=jnp.float32)
    product = jnp.einsum("rj,ro->jo", attended, shard_piece, preferred_element_type=jnp.float32)
    weight_sum = product
    grad_sum, weight_sum = (grad_sum, weight_sum)
    node_count = row_count * lax.axis_size("ctx")
    weight_grad = lax.psum(weight_sum, "ctx") * node_count ** (-0.5)
    grad_attended = grad_sum.astype(jnp.bfloat16)
    grad_blocks = grad_attended.reshape(blocks, BS, head_count, HD)
    row_dots = jnp.sum(
        grad_blocks.astype(jnp.float32) * attended_blocks.astype(jnp.float32), axis=3
    ).transpose(0, 2, 1)

    def sweep_step(totals, block_index):
        relative, places, active = slot_table(ctx_index * blocks + block_index)
        query_block = query_blocks[block_index]
        grad_block = grad_blocks[block_index]
        log_total = log_totals[block_index]
        dot_block = row_dots[block_index]
        key_block, value_block = fetch_all(places)
        grad_query, grad_key, grad_value = pair_backward(
            query_block,
            grad_block,
            log_total,
            dot_block,
            key_block,
            value_block,
            slot_ids < active,
            factor,
        )
        update = jnp.concatenate(
            [
                grad_key.reshape(slot_total, BS, col_count),
                grad_value.reshape(slot_total, BS, col_count),
            ],
            axis=2,
        )
        totals = totals.at[places].add(jnp.where((slot_ids < active)[:, None, None], update, 0.0))
        return (totals, grad_query.astype(jnp.bfloat16))

    blank_totals = jnp.zeros((extent, BS, 2 * col_count), jnp.float32)
    totals, grad_queries = lax.scan(sweep_step, blank_totals, jnp.arange(blocks, dtype=jnp.int32))
    middle = totals[blocks : 2 * blocks]
    from_right = shifted(totals[:blocks], "ctx", -1)
    from_left = shifted(totals[2 * blocks :], "ctx", 1)
    combined = middle + from_right + from_left
    query_grad = grad_queries.reshape(row_count, col_count)
    key_grad = combined[:, :, :col_count].reshape(row_count, col_count).astype(jnp.bfloat16)
    value_grad = combined[:, :, col_count:].reshape(row_count, col_count).astype(jnp.bfloat16)
    return (query_grad, key_grad, value_grad, weight_grad)


def solution(mesh):
    placed = (
        P("ctx", "head"),
        P("ctx", "head"),
        P("ctx", "head"),
        P("ctx", "head"),
        P("head", None),
        P(),
        P(),
    )
    return jax.shard_map(
        body,
        mesh=mesh,
        in_specs=placed,
        out_specs=(P("ctx", "head"), P("ctx", "head"), P("ctx", "head"), P("head", None)),
        check_vma=False,
    )
```

profile of v0, /device:TPU:1, one launch (start us, length us, event | category | flops | bytes accessed | tf_op | source)
XLA Modules:
  0.0 511.5 jit_solution(8677155265565717120)
XLA Ops:
  9.3 8.7 %collective-permute-start.1 = (bf16[1024,256]{1,0:T(8,128)(2,1)S(1)}, bf16[1024,256]{1,0:T(8,128)(2,1)S(1)}, u32[]{:S(2)}, u32[]{:S(2)}) collective-permute-start(bf16[1024,256]{1,0:T(8,128)(2,1)S(1)} %constant_dynamic-update-slice_fusion), channel_id=1, source_target_pairs={{8,0},{16,8},{24,16},{32,24},{40,32},{48,40},{56,48},{64,56},{72,6... | collective-permute-start | bytes 1572872 | tf_op jit(solution)/shard_map/ppermute | solution.py:20
  18.1 1.9 collective-permute-start
  20.1 1.6 copy.63
  23.7 2.4 collective-permute-done
  26.1 1.3 pad_maximum_fusion
  28.2 81.6 %while.30 = (s32[]{:T(128)}, bf16[8,128,2,64]{1,3,2,0:T(8,128)(2,1)}, f32[8,2,128]{2,1,0:T(2,128)S(1)}, s32[8]{0:T(128)S(1)}, s32[]{:T(128)}, /*index=5*/s32[512...) while((s32[]{:T(128)}, ...), condition=%wide.region_3.4_spmd.clone, body=%wide.region_0.3_spmd.clone.sunk | while | flops 103433040 | bytes 11877893 | solution.py:118
  35.6 1.3 fusion.85
  45.8 1.3 fusion.85
  56.0 1.3 fusion.85
  66.2 1.3 fusion.85
  76.4 1.3 fusion.85
  86.6 1.3 fusion.85
  96.8 1.3 fusion.85
  107.0 1.3 fusion.85
  109.8 2.3 convolution_convert_fusion.1
  114.0 2.0 broadcast_in_dim.88
  116.0 176.0 %while.31 = (s32[]{:T(128)}, f32[24,128,256]{2,1,0:T(8,128)}, bf16[8,128,2,64]{1,3,2,0:T(8,128)(2,1)}, s32[8]{0:T(128)S(1)}, s32[]{:T(128)}, /*index=5*/s32[512,...) while((s32[]{:T(128)}, f32[24,128,256]{2,1,0:T(8,128)}, ...), condition=%wide.region_7.8_spmd.clone, body=%wide.region_5.7_spmd.clone.sunk | while | flops 255820880 | bytes 43038368 | solution.py:161
  123.6 1.3 fusion.100
  124.8 1.2 fusion.101
  130.3 1.4 maximum_select_fusion.2
  131.8 1.7 copy.91
  133.5 4.5 scatter_fusion
  145.5 1.3 fusion.100
  146.8 1.2 fusion.101
  152.3 1.4 maximum_select_fusion.2
  153.8 1.7 copy.91
  155.5 4.5 scatter_fusion
  167.6 1.3 fusion.100
  168.8 1.2 fusion.101
  174.3 1.4 maximum_select_fusion.2
  175.8 1.7 copy.91
  177.5 4.5 scatter_fusion
  189.6 1.3 fusion.100
  190.8 1.2 fusion.101
  196.3 1.4 maximum_select_fusion.2
  197.8 1.7 copy.91
  199.5 4.4 scatter_fusion
  211.5 1.3 fusion.100
  218.2 1.4 maximum_select_fusion.2
  219.7 1.7 copy.91
  221.4 4.5 scatter_fusion
  233.4 1.3 fusion.100
  234.7 1.2 fusion.101
  240.2 1.4 maximum_select_fusion.2
  241.7 1.7 copy.91
  243.4 4.6 scatter_fusion
  255.5 1.3 fusion.100
  256.8 1.2 fusion.101
  262.3 1.4 maximum_select_fusion.2
  263.7 1.7 copy.91
  265.4 4.5 scatter_fusion
  277.5 1.3 fusion.100
  278.8 1.2 fusion.101
  284.3 1.4 maximum_select_fusion.2
  285.8 1.7 copy.91
  287.5 4.5 scatter_fusion
  292.0 3.2 fusion.46
  295.2 1.9 collective-permute-start.2
  297.1 5.0 collective-permute-start.3
  302.4 1.2 fusion.40
  303.6 1.3 copy.70
  305.9 194.5 %all-reduce.2.cloned.1.call-done = f32[128,1024]{1,0:T(8,128)} async-done(((f32[128,1024]{1,0:T(8,128)}), f32[128,1024]{1,0:T(8,128)}) %all-reduce.2.cloned.1.call-update) | async-done | bytes 524304 | tf_op jit(solution)/shard_map/psum | solution.py:126
  500.4 1.9 broadcast_multiply_fusion
  502.3 1.4 add_convert_fusion
  (343 shorter events, 124.1 us)
Async XLA Ops:
  7.2 102.6 %copy-start = (bf16[128,1024]{1,0:T(8,128)(2,1)S(1)}, bf16[128,1024]{1,0:T(8,128)(2,1)}, u32[]{:S(2)}) copy-start(bf16[128,1024]{1,0:T(8,128)(2,1)} %param.15) | copy-start | bytes 786436
  7.2 14.5 %copy-start.7 = (bf16[1024,128]{1,0:T(8,128)(2,1)S(1)}, bf16[1024,128]{1,0:T(8,128)(2,1)}, u32[]{:S(2)}) copy-start(bf16[1024,128]{1,0:T(8,128)(2,1)} %param.11) | copy-start | bytes 786436
  7.2 102.6 %all-gather.2.cloned.1.call-start = ((), (), s32[]{:S(2)}) async-start(), calls=%async_computation | async-start | bytes 2359296 | tf_op jit(solution)/shard_map/all_gather | solution.py:120
  9.3 13.6 %collective-permute-start.1 = (bf16[1024,256]{1,0:T(8,128)(2,1)S(1)}, bf16[1024,256]{1,0:T(8,128)(2,1)S(1)}, u32[]{:S(2)}, u32[]{:S(2)}) collective-permute-start(bf16[1024,256]{1,0:T(8,128)(2,1)S(1)} %constant_dynamic-update-slice_fusion), channel_id=1, source_target_pairs={{8,0},{16,8},{24,16},{32,24},{40,32},{48,40},{56,48},{64,56},{72,6... | collective-permute-start | bytes 1572872 | tf_op jit(solution)/shard_map/ppermute | solution.py:20
  18.1 8.0 %collective-permute-start = (bf16[1024,256]{1,0:T(8,128)(2,1)S(1)}, bf16[1024,256]{1,0:T(8,128)(2,1)}, u32[]{:S(2)}, u32[]{:S(2)}) collective-permute-start(bf16[1024,256]{1,0:T(8,128)(2,1)S(1)} %constant_dynamic-update-slice_fusion), channel_id=1, source_target_pairs={{0,8},{8,16},{16,24},{24,32},{32,40},{40,48},{48,56},{56,64},{64,7... | collective-permute-start | bytes 1572872 | tf_op jit(solution)/shard_map/ppermute | solution.py:18
  20.0 480.4 %all-reduce.2.cloned.1.call-start = ((), (), s32[]{:S(2)}) async-start(), calls=%async_computation.1 | async-start | bytes 1048576 | tf_op jit(solution)/shard_map/psum | solution.py:126
  22.9 5.2 %copy-start.8 = (s32[512]{0:T(512)S(1)}, s32[512]{0:T(512)}, u32[]{:S(2)}) copy-start(s32[512]{0:T(512)} %param.17) | copy-start | bytes 6148
  22.9 0.8 copy-start.6
  109.8 3.3 copy-start.4
  116.0 6.1 %copy-start.1 = (bf16[24,128,256]{2,1,0:T(8,128)(2,1)}, bf16[24,128,256]{2,1,0:T(8,128)(2,1)S(1)}, u32[]{:S(2)}) copy-start(bf16[24,128,256]{2,1,0:T(8,128)(2,1)S(1)} %get-tuple-element.755) | copy-start | bytes 4718596 | tf_op jit(solution)/shard_map/while
  133.5 4.5 copy-start.2
  138.0 6.1 %copy-start.1 = (bf16[24,128,256]{2,1,0:T(8,128)(2,1)}, bf16[24,128,256]{2,1,0:T(8,128)(2,1)S(1)}, u32[]{:S(2)}) copy-start(bf16[24,128,256]{2,1,0:T(8,128)(2,1)S(1)} %get-tuple-element.755) | copy-start | bytes 4718596 | tf_op jit(solution)/shard_map/while
  155.5 4.6 copy-start.2
  160.0 6.1 %copy-start.1 = (bf16[24,128,256]{2,1,0:T(8,128)(2,1)}, bf16[24,128,256]{2,1,0:T(8,128)(2,1)S(1)}, u32[]{:S(2)}) copy-start(bf16[24,128,256]{2,1,0:T(8,128)(2,1)S(1)} %get-tuple-element.755) | copy-start | bytes 4718596 | tf_op jit(solution)/shard_map/while
  177.5 4.5 copy-start.2
  182.0 6.1 %copy-start.1 = (bf16[24,128,256]{2,1,0:T(8,128)(2,1)}, bf16[24,128,256]{2,1,0:T(8,128)(2,1)S(1)}, u32[]{:S(2)}) copy-start(bf16[24,128,256]{2,1,0:T(8,128)(2,1)S(1)} %get-tuple-element.755) | copy-start | bytes 4718596 | tf_op jit(solution)/shard_map/while
  199.5 4.4 copy-start.2
  203.9 6.1 %copy-start.1 = (bf16[24,128,256]{2,1,0:T(8,128)(2,1)}, bf16[24,128,256]{2,1,0:T(8,128)(2,1)S(1)}, u32[]{:S(2)}) copy-start(bf16[24,128,256]{2,1,0:T(8,128)(2,1)S(1)} %get-tuple-element.755) | copy-start | bytes 4718596 | tf_op jit(solution)/shard_map/while
  221.4 4.5 copy-start.2
  225.9 6.1 %copy-start.1 = (bf16[24,128,256]{2,1,0:T(8,128)(2,1)}, bf16[24,128,256]{2,1,0:T(8,128)(2,1)S(1)}, u32[]{:S(2)}) copy-start(bf16[24,128,256]{2,1,0:T(8,128)(2,1)S(1)} %get-tuple-element.755) | copy-start | bytes 4718596 | tf_op jit(solution)/shard_map/while
  243.4 4.6 copy-start.2
  248.0 6.1 %copy-start.1 = (bf16[24,128,256]{2,1,0:T(8,128)(2,1)}, bf16[24,128,256]{2,1,0:T(8,128)(2,1)S(1)}, u32[]{:S(2)}) copy-start(bf16[24,128,256]{2,1,0:T(8,128)(2,1)S(1)} %get-tuple-element.755) | copy-start | bytes 4718596 | tf_op jit(solution)/shard_map/while
  265.4 4.5 copy-start.2
  270.0 6.1 %copy-start.1 = (bf16[24,128,256]{2,1,0:T(8,128)(2,1)}, bf16[24,128,256]{2,1,0:T(8,128)(2,1)S(1)}, u32[]{:S(2)}) copy-start(bf16[24,128,256]{2,1,0:T(8,128)(2,1)S(1)} %get-tuple-element.755) | copy-start | bytes 4718596 | tf_op jit(solution)/shard_map/while
  287.5 4.5 copy-start.2
  292.0 10.2 %copy-start.5 = (bf16[8,128,2,64]{1,3,2,0:T(8,128)(2,1)S(1)}, bf16[8,128,2,64]{1,3,2,0:T(8,128)(2,1)}, u32[]{:S(2)}) copy-start(bf16[8,128,2,64]{1,3,2,0:T(8,128)(2,1)} %get-tuple-element.294) | copy-start | bytes 786436
  292.0 10.4 %copy-start.3 = (bf16[1024,1024]{1,0:T(8,128)(2,1)S(1)}, bf16[1024,1024]{1,0:T(8,128)(2,1)}, u32[]{:S(2)}) copy-start(bf16[1024,1024]{1,0:T(8,128)(2,1)} %all-gather.2.cloned.1.call-done) | copy-start | bytes 6291460
  295.2 207.0 %collective-permute-start.2 = (f32[8,128,256]{2,1,0:T(8,128)}, f32[8,128,256]{2,1,0:T(8,128)S(1)}, u32[]{:S(2)}, u32[]{:S(2)}) collective-permute-start(f32[8,128,256]{2,1,0:T(8,128)} %get-tuple-element.505), channel_id=1, source_target_pairs={{8,0},{16,8},{24,16},{32,24},{40,32},{48,40},{56,48},{64,56},{72,6... | collective-permute-start | bytes 3145736 | tf_op jit(solution)/shard_map/ppermute | solution.py:30
  297.1 205.1 %collective-permute-start.3 = (f32[8,128,256]{2,1,0:T(8,128)}, f32[8,128,256]{2,1,0:T(8,128)S(1)}, u32[]{:S(2)}, u32[]{:S(2)}) collective-permute-start(f32[8,128,256]{2,1,0:T(8,128)} %get-tuple-element.506), channel_id=1, source_target_pairs={{0,8},{8,16},{16,24},{24,32},{32,40},{40,48},{48,56},{56,64},{64,7... | collective-permute-start | bytes 3145736 | tf_op jit(solution)/shard_map/ppermute | solution.py:30
Sparse Core Ops, SparseCore 0:
  20.1 47.4 all-gather.1
  303.8 196.5 all-reduce.1
where the time goes:
time: 518 us; the launch traced here: 511 us
  waiting for transfers between devices  197 us (38%)
  local copies, waits for them, and re-layouts  96.8 us (19%)
  other arithmetic  66.9 us (13%)
  matrix products  66.1 us (13%)
  loops' own time  52.9 us (10%)
  starting transfers between devices  17.7 us (3%)
  between operations  14.2 us (3%)
    psum x1, waiting for transfers between devices, body(): weight_grad = lax.psum(weight_sum, 'ctx') * node_count ** (-0.5)  195 us
    scatter-add x8, other arithmetic, sweep_step(): totals.at[places]  36.1 us
    another operation x1, loops' own time, body(): lax.map(forward_block, jnp.arange(blocks, dtype=jnp.int32))  26.5 us
    another operation x1, loops' own time, body(): lax.scan(sweep_step, blank_totals, jnp.arange(blocks, dtype=jnp.int32))  26.4 us
    dot_general x16, matrix products, head_scores(): jnp.einsum('qhd,khd->hqk', query_block, key_block, preferred_element_type...  20.1 us
    select_n x8, local copies, waits for them, and re-layouts, sweep_step(): jnp.where((slot_ids < active)[:, None, None], update, 0.0)  13.6 us
    select_n x8, other arithmetic, sweep_step(): jnp.where((slot_ids < active)[:, None, None], update, 0.0)  11.5 us
  transfers between devices with their start and end apart: 6, of which 2 were waited for; matrix products, arithmetic and copies ran while one was open for 13% of the time, Pallas kernels for 0%

commit v1 on v0

v1 whole, which is shorter than its diff:
```python
import jax
import jax.numpy as jnp
from jax import lax
from jax.experimental import pallas as pl
from jax.experimental.pallas import tpu as pltpu
from jax.sharding import PartitionSpec as P

HD = 64
BS = 128
SIZES = (4, 6, 8, 10, 12)


def by_size(active, run):
    low = 0
    for size in SIZES:
        pl.when((active > low) & (active <= size))(lambda size=size: run(size))
        low = size


def spread_columns(rows_t):
    blank = jnp.zeros((HD, BS), rows_t.dtype)
    upper = jnp.concatenate([rows_t[:HD], blank], axis=1)
    lower = jnp.concatenate([blank, rows_t[HD:]], axis=1)
    return jnp.concatenate([upper, lower], axis=0)


def spread_rows(rows):
    lane = lax.broadcasted_iota(jnp.int32, rows.shape, 1)
    blank = jnp.zeros_like(rows)
    return jnp.concatenate(
        [jnp.where(lane < HD, rows, blank), jnp.where(lane >= HD, rows, blank)], axis=0
    )


def own_heads(both):
    return jnp.concatenate([both[:HD, :BS], both[HD:, BS:]], axis=0)


def dot(a, b):
    return jnp.dot(a, b, preferred_element_type=jnp.float32)


def forward_kernel(
    places, active, q_ref, mid_k, mid_v, left, right, att_ref, p_ref, kt_ref, v_ref, k_scr, vt_scr, s_scr
):
    step = pl.program_id(0)
    blocks = pl.num_programs(0)
    factor = HD ** (-0.5)

    @pl.when(step == 0)
    def _():
        count = mid_k.shape[0] // BS
        for b in range(3 * count):
            side, at = divmod(b, count)
            rows = pl.ds(at * BS, BS)
            if side == 1:
                k, v = mid_k[rows, :], mid_v[rows, :]
            else:
                source = left if side == 0 else right
                k, v = source[rows, :BS], source[rows, BS:]
            k_scr[b] = k
            kt_ref[b] = k.T
            v_ref[b] = v
            vt_scr[b] = v.T

    query = spread_columns(q_ref[...].T * factor)

    def run(size):
        highest = None
        for s in range(size):
            scores = dot(k_scr[places[step, s]], query)
            if s == size - 1:
                scores = jnp.where(s < active[step], scores, -1e30)
            s_scr[pl.ds(s * BS, BS), :] = scores
            part = jnp.max(scores.reshape(BS // 8, 8, 2 * BS), axis=0)
            highest = part if highest is None else jnp.maximum(highest, part)
        highest = jnp.max(highest, axis=0, keepdims=True)
        total = None
        for s in range(size):
            grown = jnp.exp(s_scr[pl.ds(s * BS, BS), :] - highest)
            s_scr[pl.ds(s * BS, BS), :] = grown
            part = jnp.sum(grown.reshape(BS // 8, 8, 2 * BS), axis=0)
            total = part if total is None else total + part
        inverse = 1.0 / jnp.sum(total, axis=0, keepdims=True)
        attended = None
        for s in range(size):
            weights = s_scr[pl.ds(s * BS, BS), :] * inverse
            p_ref[0, pl.ds(s * BS, BS), :] = weights
            term = dot(vt_scr[places[step, s]], weights.astype(jnp.bfloat16))
            attended = term if attended is None else attended + term
        att_ref[...] = own_heads(attended).astype(jnp.bfloat16)

    by_size(active[step], run)


def forward(places, active, query_rows, key_rows, value_rows, left, right):
    blocks, slots = places.shape
    rows, cols = query_rows.shape
    extent = 3 * blocks
    whole = lambda *shape: pl.BlockSpec(shape, lambda i, *_: (0,) * len(shape))
    window = jax.ShapeDtypeStruct((extent, BS, cols), jnp.bfloat16)
    return pl.pallas_call(
        forward_kernel,
        grid_spec=pltpu.PrefetchScalarGridSpec(
            num_scalar_prefetch=2,
            grid=(blocks,),
            in_specs=[
                pl.BlockSpec((BS, cols), lambda i, *_: (i, 0)),
                whole(rows, cols),
                whole(rows, cols),
                whole(rows, 2 * cols),
                whole(rows, 2 * cols),
            ],
            out_specs=[
                pl.BlockSpec((cols, BS), lambda i, *_: (0, i)),
                pl.BlockSpec((1, slots * BS, 2 * BS), lambda i, *_: (i, 0, 0)),
                whole(extent, BS, cols),
                whole(extent, BS, cols),
            ],
            scratch_shapes=[
                pltpu.VMEM((extent, BS, cols), jnp.bfloat16),
                pltpu.VMEM((extent, BS, cols), jnp.bfloat16),
                pltpu.VMEM((slots * BS, 2 * BS), jnp.float32),
            ],
        ),
        out_shape=[
            jax.ShapeDtypeStruct((cols, rows), jnp.bfloat16),
            jax.ShapeDtypeStruct((blocks, slots * BS, 2 * BS), jnp.float32),
            window,
            window,
        ],
        compiler_params=pltpu.CompilerParams(dimension_semantics=("arbitrary",)),
        name="forward",
    )(places, active, query_rows, key_rows, value_rows, left, right)


def backward_kernel(
    places, active, q_ref, ga_ref, att_ref, p_ref, kt_ref, v_ref, dq_ref, mid_ref, left_ref, right_ref, dk, dv
):
    step = pl.program_id(0)
    factor = HD ** (-0.5)

    @pl.when(step == 0)
    def _():
        dk[...] = jnp.zeros_like(dk)
        dv[...] = jnp.zeros_like(dv)

    grad = ga_ref[...]
    grad_t = grad.T
    products = grad_t.astype(jnp.float32) * att_ref[...].astype(jnp.float32)
    dots = jnp.concatenate(
        [
            jnp.sum(products[:HD], axis=0, keepdims=True),
            jnp.sum(products[HD:], axis=0, keepdims=True),
        ],
        axis=1,
    )
    grad_wide = spread_columns(grad_t)
    grad_tall = spread_rows(grad)
    query_tall = spread_rows(q_ref[...] * factor)

    def run(size):
        total = None
        for s in range(size):
            place = places[step, s]
            weights = p_ref[0, pl.ds(s * BS, BS), :]
            change = weights * (dot(v_ref[place], grad_wide) - dots)
            change = change.astype(jnp.bfloat16)
            term = dot(kt_ref[place], change)
            total = term if total is None else total + term
            dk[place] += dot(change, query_tall)
            dv[place] += dot(weights.astype(jnp.bfloat16), grad_tall)
        dq_ref[...] = (own_heads(total) * factor).T.astype(jnp.bfloat16)

    by_size(active[step], run)

    @pl.when(step == pl.num_programs(0) - 1)
    def _():
        count = mid_ref.shape[0] // BS
        for b in range(3 * count):
            side, at = divmod(b, count)
            target = (left_ref, mid_ref, right_ref)[side]
            rows = pl.ds(at * BS, BS)
            target[rows, :BS] = dk[b].astype(target.dtype)
            target[rows, BS:] = dv[b].astype(target.dtype)


def backward(places, active, query_rows, grad_attended, att_t, weights, keys_t, values):
    blocks, slots = places.shape
    rows, cols = query_rows.shape
    extent = 3 * blocks
    whole = lambda *shape: pl.BlockSpec(shape, lambda i, *_: (0,) * len(shape))
    one = pl.BlockSpec((BS, cols), lambda i, *_: (i, 0))
    return pl.pallas_call(
        backward_kernel,
        grid_spec=pltpu.PrefetchScalarGridSpec(
            num_scalar_prefetch=2,
            grid=(blocks,),
            in_specs=[
                one,
                one,
                pl.BlockSpec((cols, BS), lambda i, *_: (0, i)),
                pl.BlockSpec((1, slots * BS, 2 * BS), lambda i, *_: (i, 0, 0)),
                whole(extent, BS, cols),
                whole(extent, BS, cols),
            ],
            out_specs=[one, whole(rows, 2 * cols), whole(rows, 2 * cols), whole(rows, 2 * cols)],
            scratch_shapes=[
                pltpu.VMEM((extent, BS, cols), jnp.float32),
                pltpu.VMEM((extent, BS, cols), jnp.float32),
            ],
        ),
        out_shape=[
            jax.ShapeDtypeStruct((rows, cols), jnp.bfloat16),
            jax.ShapeDtypeStruct((rows, 2 * cols), jnp.float32),
            jax.ShapeDtypeStruct((rows, 2 * cols), jnp.bfloat16),
            jax.ShapeDtypeStruct((rows, 2 * cols), jnp.bfloat16),
        ],
        compiler_params=pltpu.CompilerParams(dimension_semantics=("arbitrary",)),
        name="backward",
    )(places, active, query_rows, grad_attended, att_t, weights, keys_t, values)


def shifted(x, axis, by):
    count = lax.axis_size(axis)
    return lax.ppermute(x, axis, [(i, (i + by) % count) for i in range(count)])


def body(query_rows, key_rows, value_rows, out_grad, out_weight, neighbours, counts):
    row_count, col_count = query_rows.shape
    blocks = row_count // BS
    extent = 3 * blocks
    ctx_index = lax.axis_index("ctx")
    packed = jnp.concatenate([key_rows, value_rows], axis=1)
    left = shifted(packed, "ctx", 1)
    right = shifted(packed, "ctx", -1)
    first = ctx_index * blocks
    places = lax.dynamic_slice_in_dim(neighbours, first, blocks, axis=0)
    places = jnp.clip(places - (first - blocks), 0, extent - 1)
    active = lax.dynamic_slice_in_dim(counts, first, blocks, axis=0)
    att_t, weights, keys_t, values = forward(
        places, active, query_rows, key_rows, value_rows, left, right
    )
    gathered = lax.all_gather(out_grad, "head", axis=1, tiled=True)
    grad_attended = jnp.einsum(
        "ro,jo->rj", gathered, out_weight, preferred_element_type=jnp.float32
    ).astype(jnp.bfloat16)
    product = jnp.einsum("jr,ro->jo", att_t, gathered, preferred_element_type=jnp.float32)
    node_count = row_count * lax.axis_size("ctx")
    weight_grad = lax.psum(product, "ctx") * node_count ** (-0.5)
    query_grad, middle, to_left, to_right = backward(
        places, active, query_rows, grad_attended, att_t, weights, keys_t, values
    )
    from_right = shifted(to_left, "ctx", -1)
    from_left = shifted(to_right, "ctx", 1)
    combined = middle + from_right.astype(jnp.float32) + from_left.astype(jnp.float32)
    key_grad = combined[:, :col_count].astype(jnp.bfloat16)
    value_grad = combined[:, col_count:].astype(jnp.bfloat16)
    return (query_grad, key_grad, value_grad, weight_grad)


def solution(mesh):
    placed = (
        P("ctx", "head"),
        P("ctx", "head"),
        P("ctx", "head"),
        P("ctx", "head"),
        P("head", None),
        P(),
        P(),
    )
    return jax.shard_map(
        body,
        mesh=mesh,
        in_specs=placed,
        out_specs=(P("ctx", "head"), P("ctx", "head"), P("ctx", "head"), P("head", None)),
        check_vma=False,
    )
```

time: 518 us -> 301 us (0.58); the launches traced: 511 us -> 300 us
  local copies, waits for them, and re-layouts: 96.8 us -> 5.77 us
  other arithmetic: 66.9 us -> 4.02 us
  matrix products: 66.1 us -> 4.25 us
  loops' own time: 52.9 us -> 0 us
  Pallas kernels: 0 us -> 30.9 us
  waiting for transfers between devices: 197 us -> 219 us
    dot_general x58 -> x2, matrix products: 66.1 us -> 4.25 us  [the longest x1 3.01 us: body(): jnp.einsum('ro,jo->rj', gathered, out_weight, preferred_element_type=jnp....]
    another operation x2 -> x0, loops' own time: 52.9 us -> none  [the longest x1 26.5 us: body(): lax.map(forward_block, jnp.arange(blocks, dtype=jnp.int32))]
    scatter-add x8 -> x0, other arithmetic: 36.1 us -> none  [sweep_step(): totals.at[places]]
    pallas_call x0 -> x2, Pallas kernels: none -> 30.9 us  [the longest x1 17.7 us: backward(): pl.pallas_call(backward_kernel, grid_spec=pltpu.PrefetchScalarGridSpec(nu...]
    select_n x24 -> x0, other arithmetic: 22.8 us -> none  [the longest x8 11.5 us: sweep_step(): jnp.where((slot_ids < active)[:, None, None], update, 0.0)]
    slice x50 -> x1, local copies, waits for them, and re-layouts: 21.1 us -> 0.83 us  [body(): value_grad = combined[:, col_count:].astype(jnp.bfloat16)]
    all_gather x1, waiting for transfers between devices: 0.01 us -> 19.4 us  [body(): gathered = lax.all_gather(out_grad, 'head', axis=1, tiled=True)]
    reshape x49 -> x0, local copies, waits for them, and re-layouts: 19.1 us -> none  [the longest x8 9 us: sweep_step(): grad_value.reshape(slot_total, BS, col_count)]
  transfers between devices with their start and end apart: 6 -> 6, of which waited for: 2 -> 3; matrix products, arithmetic and copies ran while one was open for 13% -> 3% of each run, Pallas kernels for 0% -> 4%
where the time goes in v1:
time: 301 us; the launch traced here: 300 us
  waiting for transfers between devices  219 us (73%)
  Pallas kernels  30.9 us (10%)
  starting transfers between devices  22.7 us (8%)
  between operations  14.1 us (5%)
  local copies, waits for them, and re-layouts  5.77 us (2%)
  matrix products  4.25 us (1%)
  other arithmetic  4.02 us (1%)
    psum x1, waiting for transfers between devices, body(): weight_grad = lax.psum(product, 'ctx') * node_count ** (-0.5)  195 us
    ppermute x4, starting transfers between devices, shifted(): return lax.ppermute(x, axis, [(i, (i + by) % count) for i in range(count)])  22.6 us
    all_gather x1, waiting for transfers between devices, body(): gathered = lax.all_gather(out_grad, 'head', axis=1, tiled=True)  19.4 us
    pallas_call x1, Pallas kernels, backward(): pl.pallas_call(backward_kernel, grid_spec=pltpu.PrefetchScalarGridSpec(nu...  17.7 us
    pallas_call x1, Pallas kernels, forward(): pl.pallas_call(forward_kernel, grid_spec=pltpu.PrefetchScalarGridSpec(num...  13.1 us
  transfers between devices with their start and end apart: 6, of which 3 were waited for; matrix products, arithmetic and copies ran while one was open for 3% of the time, Pallas kernels for 4%

profile of v1, /device:TPU:1, one launch (start us, length us, event | category | flops | bytes accessed | tf_op | source)
XLA Modules:
  0.0 300.3 jit_solution(8682349472490382944)
XLA Ops:
  7.2 0.0 copy-start
  7.2 0.0 all-gather.2.cloned.1.call-start
  7.2 0.7 all-gather.2.cloned.1.call-update
  7.9 0.0 all-reduce.2.cloned.1.call-start
  8.0 1.0 constant_dynamic-update-slice_fusion.1
  9.0 1.0 constant_dynamic-update-slice_fusion
  10.0 8.7 %collective-permute-start.1 = (bf16[1024,256]{1,0:T(8,128)(2,1)S(1)}, bf16[1024,256]{1,0:T(8,128)(2,1)S(1)}, u32[]{:S(2)}, u32[]{:S(2)}) collective-permute-start(bf16[1024,256]{1,0:T(8,128)(2,1)S(1)} %constant_dynamic-update-slice_fusion), channel_id=1, source_target_pairs={{0,504},{8,0},{16,8},{24,16},{32,24},{40,32},{48,40},{56,48},{64,5... | collective-permute-start | bytes 1572872 | tf_op jit(solution)/shard_map/ppermute | solution.py:226
  18.7 1.9 collective-permute-start
  20.7 1.3 dynamic_slice.7.active
  21.9 0.8 constant_dynamic-slice_fusion
  22.7 0.1 copy.12
  22.8 0.6 subtract_clamp_fusion.places
  23.4 0.0 collective-permute-done.1.right
  23.4 0.0 copy-start.3
  23.4 4.0 %collective-permute-done.left = bf16[1024,256]{1,0:T(8,128)(2,1)S(1)} collective-permute-done((bf16[1024,256]{1,0:T(8,128)(2,1)S(1)}, bf16[1024,256]{1,0:T(8,128)(2,1)S(1)}, u32[]{:S(2)}, u32[]{:S(2)}) %collective-permute-start) | collective-permute-done | bytes 524320 | tf_op jit(solution)/shard_map/ppermute | solution.py:226
  27.4 0.0 copy-done.3
  27.4 0.0 copy-start.4
  27.4 0.8 copy-done.4
  28.2 13.1 %forward.1 = (bf16[128,1024]{1,0:T(8,128)(2,1)}, f32[8,1536,256]{2,1,0:T(8,128)}, bf16[24,128,128]{2,1,0:T(8,128)(2,1)}, bf16[24,128,128]{2,1,0:T(8,128)(2,1)}) custom-call(s32[8,12]{1,0:T(8,128)} %subtract_clamp_fusion.places, s32[8]{0:T(128)} %dynamic_slice.7.active, bf16[1024,128]{1,0:T(8,128)(2,1)} %q_ref.3, bf16[1024,128]{1,0:T(8,128)(2,1)} %mid_k.1, ...), custom_call_target="tpu_custom_call" | custom-call | tf_op jit(solution)/shard_map/forward/pallas_call | solution.py:102
  41.3 19.4 %all-gather.2.cloned.1.call-done = bf16[1024,1024]{1,0:T(8,128)(2,1)} async-done(((bf16[1024,128]{1,0:T(8,128)(2,1)}), bf16[1024,1024]{1,0:T(8,128)(2,1)}) %all-gather.2.cloned.1.call-update) | async-done | bytes 2097168 | tf_op jit(solution)/shard_map/all_gather | solution.py:244
  60.7 0.0 copy-done
  60.7 3.0 %convolution_convert_fusion.ga_ref = bf16[1024,128]{1,0:T(8,128)(2,1)} fusion(bf16[1024,1024]{1,0:T(8,128)(2,1)} %all-gather.2.cloned.1.call-done, bf16[128,1024]{1,0:T(8,128)(2,1)S(1)} %copy-done), kind=kOutput, calls=%fused_computation | convolution fusion | flops 268566528 | bytes 2621440 | tf_op jit(solution)/shard_map/ro,jo->rj/dot_general | solution.py:245
  63.7 0.0 copy-start.1
  63.7 0.0 copy-start.2
  63.7 17.7 %backward.1 = (bf16[1024,128]{1,0:T(8,128)(2,1)}, f32[1024,256]{1,0:T(8,128)}, bf16[1024,256]{1,0:T(8,128)(2,1)}, bf16[1024,256]{1,0:T(8,128)(2,1)}) custom-call(s32[8,12]{1,0:T(8,128)} %subtract_clamp_fusion.places, s32[8]{0:T(128)} %dynamic_slice.7.active, bf16[1024,128]{1,0:T(8,128)(2,1)} %q_ref.3, bf16[1024,128]{1,0:T(8,128)(2,1)} %convolution_convert_fusion.ga_ref, ...), custom_call_target="tpu_custom_call" | custom-call | tf_op jit(solution)/shard_map/backward/pallas_call | solution.py:194
  81.4 10.0 %collective-permute-start.2 = (bf16[1024,256]{1,0:T(8,128)(2,1)}, bf16[1024,256]{1,0:T(8,128)(2,1)S(1)}, u32[]{:S(2)}, u32[]{:S(2)}) collective-permute-start(bf16[1024,256]{1,0:T(8,128)(2,1)} %get-tuple-element.18), channel_id=1, source_target_pairs={{0,504},{8,0},{16,8},{24,16},{32,24},{40,32},{48,40},{56,48},{64,5... | collective-permute-start | bytes 1572872 | tf_op jit(solution)/shard_map/ppermute | solution.py:226
  91.5 1.9 collective-permute-start.3
  93.4 0.0 copy-done.1
  93.4 0.0 copy-done.2
  93.4 1.2 fusion.1
  94.6 0.0 all-reduce.2.cloned.1.call-update
  94.7 194.6 %all-reduce.2.cloned.1.call-done = f32[128,1024]{1,0:T(8,128)} async-done(((f32[128,1024]{1,0:T(8,128)}), f32[128,1024]{1,0:T(8,128)}) %all-reduce.2.cloned.1.call-update) | async-done | bytes 524304 | tf_op jit(solution)/shard_map/psum | solution.py:250
  289.2 1.9 broadcast_multiply_fusion
  291.1 0.0 collective-permute-done.2
  291.1 0.0 collective-permute-done.3
  291.1 1.5 add_convert_fusion
  292.7 0.8 fusion
Async XLA Ops:
  7.2 53.5 %copy-start = (bf16[128,1024]{1,0:T(8,128)(2,1)S(1)}, bf16[128,1024]{1,0:T(8,128)(2,1)}, u32[]{:S(2)}) copy-start(bf16[128,1024]{1,0:T(8,128)(2,1)} %param.11) | copy-start | bytes 786436
  7.2 53.5 %all-gather.2.cloned.1.call-start = ((), (), s32[]{:S(2)}) async-start(), calls=%async_computation | async-start | bytes 2359296 | tf_op jit(solution)/shard_map/all_gather | solution.py:244
  7.9 281.3 %all-reduce.2.cloned.1.call-start = ((), (), s32[]{:S(2)}) async-start(), calls=%async_computation.1 | async-start | bytes 1048576 | tf_op jit(solution)/shard_map/psum | solution.py:250
  10.0 13.4 %collective-permute-start.1 = (bf16[1024,256]{1,0:T(8,128)(2,1)S(1)}, bf16[1024,256]{1,0:T(8,128)(2,1)S(1)}, u32[]{:S(2)}, u32[]{:S(2)}) collective-permute-start(bf16[1024,256]{1,0:T(8,128)(2,1)S(1)} %constant_dynamic-update-slice_fusion), channel_id=1, source_target_pairs={{0,504},{8,0},{16,8},{24,16},{32,24},{40,32},{48,40},{56,48},{64,5... | collective-permute-start | bytes 1572872 | tf_op jit(solution)/shard_map/ppermute | solution.py:226
  18.7 8.6 %collective-permute-start = (bf16[1024,256]{1,0:T(8,128)(2,1)S(1)}, bf16[1024,256]{1,0:T(8,128)(2,1)S(1)}, u32[]{:S(2)}, u32[]{:S(2)}) collective-permute-start(bf16[1024,256]{1,0:T(8,128)(2,1)S(1)} %constant_dynamic-update-slice_fusion), channel_id=1, source_target_pairs={{0,8},{8,16},{16,24},{24,32},{32,40},{40,48},{48,56},{56,64},{64,7... | collective-permute-start | bytes 1572872 | tf_op jit(solution)/shard_map/ppermute | solution.py:226
  23.4 4.0 %copy-start.3 = (bf16[1024,256]{1,0:T(8,128)(2,1)}, bf16[1024,256]{1,0:T(8,128)(2,1)S(1)}, u32[]{:S(2)}) copy-start(bf16[1024,256]{1,0:T(8,128)(2,1)S(1)} %collective-permute-done.1.right) | copy-start | bytes 1572868
  27.4 0.8 copy-start.4
  63.7 29.7 %copy-start.1 = (bf16[1024,1024]{1,0:T(8,128)(2,1)S(1)}, bf16[1024,1024]{1,0:T(8,128)(2,1)}, u32[]{:S(2)}) copy-start(bf16[1024,1024]{1,0:T(8,128)(2,1)} %all-gather.2.cloned.1.call-done) | copy-start | bytes 6291460
  63.7 29.7 %copy-start.2 = (bf16[128,1024]{1,0:T(8,128)(2,1)S(1)}, bf16[128,1024]{1,0:T(8,128)(2,1)}, u32[]{:S(2)}) copy-start(bf16[128,1024]{1,0:T(8,128)(2,1)} %get-tuple-element.12.att_ref) | copy-start | bytes 786436
  81.4 209.7 %collective-permute-start.2 = (bf16[1024,256]{1,0:T(8,128)(2,1)}, bf16[1024,256]{1,0:T(8,128)(2,1)S(1)}, u32[]{:S(2)}, u32[]{:S(2)}) collective-permute-start(bf16[1024,256]{1,0:T(8,128)(2,1)} %get-tuple-element.18), channel_id=1, source_target_pairs={{0,504},{8,0},{16,8},{24,16},{32,24},{40,32},{48,40},{56,48},{64,5... | collective-permute-start | bytes 1572872 | tf_op jit(solution)/shard_map/ppermute | solution.py:226
  91.5 199.7 %collective-permute-start.3 = (bf16[1024,256]{1,0:T(8,128)(2,1)}, bf16[1024,256]{1,0:T(8,128)(2,1)}, u32[]{:S(2)}, u32[]{:S(2)}) collective-permute-start(bf16[1024,256]{1,0:T(8,128)(2,1)} %get-tuple-element.19), channel_id=1, source_target_pairs={{0,8},{8,16},{16,24},{24,32},{32,40},{40,48},{48,56},{56,64},{64,7... | collective-permute-start | bytes 1572872 | tf_op jit(solution)/shard_map/ppermute | solution.py:226
Sparse Core Ops, SparseCore 0:
  10.0 50.6 all-gather.1
  94.8 194.4 all-reduce.1

commit v2 on v1

--- a/solution.py
+++ b/solution.py
@@ -226,6 +226,87 @@
     return lax.ppermute(x, axis, [(i, (i + by) % count) for i in range(count)])
 
 
+def project_kernel(head, own, r1, l1, r2, l2, r3, l3, upper, lower, w_ref, att_ref, ga_ref, wg_ref):
+    count = wg_ref.shape[0]
+    half = upper.shape[0]
+    chunks = {0: own, -1: r1, 1: l1, -2: r2, 2: l2, -3: r3, 3: l3}
+    att = att_ref[...]
+    total = None
+    for first, second in ((0, 1), (-1, 2), (-2, 3), (-3, 4)):
+        sides, parts = [], []
+        for k in (first, second):
+            at = lax.rem(head[0] + k + count, count)
+            sides.append(w_ref[:, pl.ds(pl.multiple_of(at * BS, BS), BS)])
+            if k == 4:
+                parts.append(jnp.concatenate([upper[...], lower[...]], axis=0))
+            else:
+                parts.append(chunks[k][...])
+        side = jnp.concatenate(sides, axis=1)
+        part = jnp.concatenate(parts, axis=1)
+        term = lax.dot_general(
+            part, side, (((1,), (1,)), ((), ())), preferred_element_type=jnp.float32
+        )
+        total = term if total is None else total + term
+        grad = dot(att, part)
+        wg_ref[first % count] = grad[:, :BS].astype(wg_ref.dtype)
+        wg_ref[second % count] = grad[:, BS:].astype(wg_ref.dtype)
+    ga_ref[...] = total.astype(jnp.bfloat16)
+
+
+def project(head, parts, out_weight, att_t):
+    rows = parts[0].shape[0]
+    cols, width = out_weight.shape
+    return pl.pallas_call(
+        project_kernel,
+        in_specs=[pl.BlockSpec(memory_space=pltpu.SMEM)]
+        + [pl.BlockSpec(memory_space=pltpu.VMEM)] * (len(parts) + 2),
+        out_shape=[
+            jax.ShapeDtypeStruct((rows, cols), jnp.bfloat16),
+            jax.ShapeDtypeStruct((width // BS, cols, BS), jnp.bfloat16),
+        ],
+        name="project",
+    )(head, *parts, out_weight, att_t)
+
+
+def place_kernel(head, sum_ref, out_ref):
+    count = sum_ref.shape[0]
+    for k in range(count):
+        at = lax.rem(head[0] + k, count)
+        out_ref[:, pl.ds(pl.multiple_of(at * BS, BS), BS)] = sum_ref[k].astype(jnp.float32)
+
+
+def place(head, sums):
+    count, cols, width = sums.shape
+    return pl.pallas_call(
+        place_kernel,
+        in_specs=[pl.BlockSpec(memory_space=pltpu.SMEM), pl.BlockSpec(memory_space=pltpu.VMEM)],
+        out_shape=jax.ShapeDtypeStruct((cols, count * width), jnp.float32),
+        name="place",
+    )(head, sums)
+
+
+def head_ring(own):
+    half = own.shape[0] // 2
+    parts = [own]
+    r, l = own, own
+    for _ in range(3):
+        r, l = shifted(r, "head", 1), shifted(l, "head", -1)
+        parts += [r, l]
+    parts += [shifted(r[:half], "head", 1), shifted(l[half:], "head", -1)]
+    return parts
+
+
+def total_over(partial, axis, scale):
+    members = lax.axis_size(axis)
+    shape = partial.shape
+    pieces = partial.reshape(members, -1, shape[-1])
+    pieces = lax.all_to_all(pieces, axis, 0, 0)
+    piece = jnp.sum(pieces.astype(jnp.float32), axis=0) * scale
+    piece = piece.astype(partial.dtype)
+    pieces = lax.all_to_all(jnp.broadcast_to(piece[None], pieces.shape), axis, 0, 0)
+    return pieces.reshape(shape)
+
+
 def body(query_rows, key_rows, value_rows, out_grad, out_weight, neighbours, counts):
     row_count, col_count = query_rows.shape
     blocks = row_count // BS
@@ -241,18 +322,16 @@
     att_t, weights, keys_t, values = forward(
         places, active, query_rows, key_rows, value_rows, left, right
     )
-    gathered = lax.all_gather(out_grad, "head", axis=1, tiled=True)
-    grad_attended = jnp.einsum(
-        "ro,jo->rj", gathered, out_weight, preferred_element_type=jnp.float32
-    ).astype(jnp.bfloat16)
-    product = jnp.einsum("jr,ro->jo", att_t, gathered, preferred_element_type=jnp.float32)
+    head = lax.axis_index("head").reshape(1)
+    grad_attended, partial = project(head, head_ring(out_grad), out_weight, att_t)
     node_count = row_count * lax.axis_size("ctx")
-    weight_grad = lax.psum(product, "ctx") * node_count ** (-0.5)
     query_grad, middle, to_left, to_right = backward(
         places, active, query_rows, grad_attended, att_t, weights, keys_t, values
     )
     from_right = shifted(to_left, "ctx", -1)
     from_left = shifted(to_right, "ctx", 1)
+    weight_sum = total_over(partial, "ctx", node_count ** (-0.5))
+    weight_grad = place(head, weight_sum)
     combined = middle + from_right.astype(jnp.float32) + from_left.astype(jnp.float32)
     key_grad = combined[:, :col_count].astype(jnp.bfloat16)
     value_grad = combined[:, col_count:].astype(jnp.bfloat16)

time: 301 us -> 134 us (0.45)
  waiting for transfers between devices: 219 us -> 12.1 us
  starting transfers between devices: 22.7 us -> 75.6 us
  between operations: 14.1 us -> 0.97 us
  matrix products: 4.25 us -> 0 us
  local copies, waits for them, and re-layouts: 5.77 us -> 9.39 us
    psum x1 -> x0, waiting for transfers between devices: 195 us -> none  [body(): weight_grad = lax.psum(product, 'ctx') * node_count ** (-0.5)]
    ppermute x4 -> x12, starting transfers between devices: 22.6 us -> 49.3 us  [shifted(): return lax.ppermute(x, axis, [(i, (i + by) % count) for i in range(count)])]
    all_to_all x0 -> x2, starting transfers between devices: none -> 26.3 us  [the longest x1 17.1 us: total_over(): pieces = lax.all_to_all(pieces, axis, 0, 0)]
    all_gather x1 -> x0, waiting for transfers between devices: 19.4 us -> none  [body(): gathered = lax.all_gather(out_grad, 'head', axis=1, tiled=True)]
    all_to_all x0 -> x2, waiting for transfers between devices: none -> 9.74 us  [the longest x1 9.73 us: total_over(): lax.all_to_all(jnp.broadcast_to(piece[None], pieces.shape), axis, 0, 0)]
    pallas_call x0 -> x2, Pallas kernels: none -> 5.26 us  [the longest x1 3.47 us: project(): pl.pallas_call(project_kernel, in_specs=[pl.BlockSpec(memory_space=pltpu....]
    dot_general x2 -> x0, matrix products: 4.25 us -> none  [the longest x1 3.01 us: body(): jnp.einsum('ro,jo->rj', gathered, out_weight, preferred_element_type=jnp....]
    pallas_call x1, Pallas kernels: 17.7 us -> 14.6 us  [backward(): pl.pallas_call(backward_kernel, grid_spec=pltpu.PrefetchScalarGridSpec(nu...]
  transfers between devices with their start and end apart: 6 -> 14, of which waited for: 3 -> 3; matrix products, arithmetic and copies ran while one was open for 3% -> 6% of each run, Pallas kernels for 4% -> 20%
where the time goes in v2:
time: 134 us; the launch traced here: 132 us
  starting transfers between devices  75.6 us (56%)
  Pallas kernels  31.7 us (24%)
  waiting for transfers between devices  12.1 us (9%)
  local copies, waits for them, and re-layouts  9.39 us (7%)
  other arithmetic  2.06 us (2%)
    ppermute x12, starting transfers between devices, shifted(): return lax.ppermute(x, axis, [(i, (i + by) % count) for i in range(count)])  49.3 us
    all_to_all x1, starting transfers between devices, total_over(): pieces = lax.all_to_all(pieces, axis, 0, 0)  17.1 us
    pallas_call x1, Pallas kernels, backward(): pl.pallas_call(backward_kernel, grid_spec=pltpu.PrefetchScalarGridSpec(nu...  14.6 us
    pallas_call x1, Pallas kernels, forward(): pl.pallas_call(forward_kernel, grid_spec=pltpu.PrefetchScalarGridSpec(num...  11.9 us
    all_to_all x1, waiting for transfers between devices, total_over(): lax.all_to_all(jnp.broadcast_to(piece[None], pieces.shape), axis, 0, 0)  9.73 us
    all_to_all x1, starting transfers between devices, total_over(): lax.all_to_all(jnp.broadcast_to(piece[None], pieces.shape), axis, 0, 0)  9.16 us
    unnamed x26, local copies, waits for them, and re-layouts  4.06 us
    pallas_call x1, Pallas kernels, project(): pl.pallas_call(project_kernel, in_specs=[pl.BlockSpec(memory_space=pltpu....  3.47 us
  transfers between devices with their start and end apart: 14, of which 3 were waited for; matrix products, arithmetic and copies ran while one was open for 6% of the time, Pallas kernels for 20%

profile of v2, /device:TPU:1, one launch (start us, length us, event | category | flops | bytes accessed | tf_op | source)
XLA Modules:
  0.0 131.8 jit_solution(5532378576991986920)
XLA Ops:
  0.6 0.0 copy-start
  0.6 4.0 %collective-permute-start = (bf16[1024,128]{1,0:T(8,128)(2,1)}, bf16[1024,128]{1,0:T(8,128)(2,1)S(1)}, u32[]{:S(2)}, u32[]{:S(2)}) collective-permute-start(bf16[1024,128]{1,0:T(8,128)(2,1)} %own.1), channel_id=1, source_target_pairs={{0,1},{1,2},{2,3},{3,4},{4,5},{5,6},{6,7},{7,0},{8,9},{9,10},{10,1... | collective-permute-start | bytes 786440 | tf_op jit(solution)/shard_map/ppermute | solution.py:226
  4.7 3.8 %collective-permute-start.1 = (bf16[1024,128]{1,0:T(8,128)(2,1)}, bf16[1024,128]{1,0:T(8,128)(2,1)S(1)}, u32[]{:S(2)}, u32[]{:S(2)}) collective-permute-start(bf16[1024,128]{1,0:T(8,128)(2,1)} %own.1), channel_id=1, source_target_pairs={{0,7},{1,0},{2,1},{3,2},{4,3},{5,4},{6,5},{7,6},{8,15},{9,8},{10,9... | collective-permute-start | bytes 786440 | tf_op jit(solution)/shard_map/ppermute | solution.py:226
  8.5 2.0 %collective-permute-done.r1 = bf16[1024,128]{1,0:T(8,128)(2,1)S(1)} collective-permute-done((bf16[1024,128]{1,0:T(8,128)(2,1)}, bf16[1024,128]{1,0:T(8,128)(2,1)S(1)}, u32[]{:S(2)}, u32[]{:S(2)}) %collective-permute-start) | collective-permute-done | bytes 262176 | tf_op jit(solution)/shard_map/ppermute | solution.py:226
  10.5 0.0 copy-start.6
  10.5 2.9 %collective-permute-start.2 = (bf16[1024,128]{1,0:T(8,128)(2,1)S(1)}, bf16[1024,128]{1,0:T(8,128)(2,1)S(1)}, u32[]{:S(2)}, u32[]{:S(2)}) collective-permute-start(bf16[1024,128]{1,0:T(8,128)(2,1)S(1)} %collective-permute-done.r1), channel_id=1, source_target_pairs={{0,1},{1,2},{2,3},{3,4},{4,5},{5,6},{6,7},{7,0},{8,9},{9,10},{10,1... | collective-permute-start | bytes 786440 | tf_op jit(solution)/shard_map/ppermute | solution.py:226
  13.4 0.0 collective-permute-done.1.l1
  13.4 0.0 copy-start.7
  13.5 4.3 %collective-permute-start.3 = (bf16[1024,128]{1,0:T(8,128)(2,1)S(1)}, bf16[1024,128]{1,0:T(8,128)(2,1)S(1)}, u32[]{:S(2)}, u32[]{:S(2)}) collective-permute-start(bf16[1024,128]{1,0:T(8,128)(2,1)S(1)} %collective-permute-done.1.l1), channel_id=1, source_target_pairs={{0,7},{1,0},{2,1},{3,2},{4,3},{5,4},{6,5},{7,6},{8,15},{9,8},{10,9... | collective-permute-start | bytes 786440 | tf_op jit(solution)/shard_map/ppermute | solution.py:226
  17.8 1.0 constant_dynamic-update-slice_fusion.1
  18.8 1.0 constant_dynamic-update-slice_fusion
  19.8 8.4 %collective-permute-start.9 = (bf16[1024,256]{1,0:T(8,128)(2,1)S(1)}, bf16[1024,256]{1,0:T(8,128)(2,1)S(1)}, u32[]{:S(2)}, u32[]{:S(2)}) collective-permute-start(bf16[1024,256]{1,0:T(8,128)(2,1)S(1)} %constant_dynamic-update-slice_fusion), channel_id=1, source_target_pairs={{0,504},{8,0},{16,8},{24,16},{32,24},{40,32},{48,40},{56,48},{64,5... | collective-permute-start | bytes 1572872 | tf_op jit(solution)/shard_map/ppermute | solution.py:226
  28.2 1.9 %collective-permute-start.8 = (bf16[1024,256]{1,0:T(8,128)(2,1)S(1)}, bf16[1024,256]{1,0:T(8,128)(2,1)S(1)}, u32[]{:S(2)}, u32[]{:S(2)}) collective-permute-start(bf16[1024,256]{1,0:T(8,128)(2,1)S(1)} %constant_dynamic-update-slice_fusion), channel_id=1, source_target_pairs={{0,8},{8,16},{16,24},{24,32},{32,40},{40,48},{48,56},{56,64},{64,7... | collective-permute-start | bytes 1572872 | tf_op jit(solution)/shard_map/ppermute | solution.py:226
  30.1 0.0 collective-permute-done.2.r2
  30.1 0.0 copy-start.8
  30.1 1.9 %collective-permute-start.4 = (bf16[1024,128]{1,0:T(8,128)(2,1)S(1)}, bf16[1024,128]{1,0:T(8,128)(2,1)S(1)}, u32[]{:S(2)}, u32[]{:S(2)}) collective-permute-start(bf16[1024,128]{1,0:T(8,128)(2,1)S(1)} %collective-permute-done.2.r2), channel_id=1, source_target_pairs={{0,1},{1,2},{2,3},{3,4},{4,5},{5,6},{6,7},{7,0},{8,9},{9,10},{10,1... | collective-permute-start | bytes 786440 | tf_op jit(solution)/shard_map/ppermute | solution.py:226
  32.1 0.0 collective-permute-done.3.l2
  32.1 0.0 copy-start.9
  32.1 4.6 %collective-permute-start.5 = (bf16[1024,128]{1,0:T(8,128)(2,1)S(1)}, bf16[1024,128]{1,0:T(8,128)(2,1)S(1)}, u32[]{:S(2)}, u32[]{:S(2)}) collective-permute-start(bf16[1024,128]{1,0:T(8,128)(2,1)S(1)} %collective-permute-done.3.l2), channel_id=1, source_target_pairs={{0,7},{1,0},{2,1},{3,2},{4,3},{5,4},{6,5},{7,6},{8,15},{9,8},{10,9... | collective-permute-start | bytes 786440 | tf_op jit(solution)/shard_map/ppermute | solution.py:226
  36.7 1.3 dynamic_slice.7.active
  38.0 0.0 copy-done
  38.0 0.1 constant_dynamic-slice_fusion
  38.0 0.1 copy.12
  38.1 0.3 collective-permute-done.4.r3
  38.5 0.7 slice.18
  39.2 1.9 %collective-permute-start.6 = (bf16[512,128]{1,0:T(8,128)(2,1)}, bf16[512,128]{1,0:T(8,128)(2,1)S(1)}, u32[]{:S(2)}, u32[]{:S(2)}) collective-permute-start(bf16[512,128]{1,0:T(8,128)(2,1)} %slice.18), channel_id=1, source_target_pairs={{0,1},{1,2},{2,3},{3,4},{4,5},{5,6},{6,7},{7,0},{8,9},{9,10},{10,1... | collective-permute-start | bytes 393224 | tf_op jit(solution)/shard_map/ppermute | solution.py:226
  41.1 0.0 collective-permute-done.5.l3
  41.1 0.0 copy-start.3
  41.1 0.7 slice.19
  41.8 4.6 %collective-permute-start.7 = (bf16[512,128]{1,0:T(8,128)(2,1)}, bf16[512,128]{1,0:T(8,128)(2,1)S(1)}, u32[]{:S(2)}, u32[]{:S(2)}) collective-permute-start(bf16[512,128]{1,0:T(8,128)(2,1)} %slice.19), channel_id=1, source_target_pairs={{0,7},{1,0},{2,1},{3,2},{4,3},{5,4},{6,5},{7,6},{8,15},{9,8},{10,9... | collective-permute-start | bytes 393224 | tf_op jit(solution)/shard_map/ppermute | solution.py:226
  46.4 0.6 subtract_clamp_fusion.places
  47.0 0.0 collective-permute-done.9.right
  47.0 0.0 collective-permute-done.8.left
  47.0 0.8 copy-done.4
  47.8 0.8 copy-done.5
  48.6 11.9 %forward.1 = (bf16[128,1024]{1,0:T(8,128)(2,1)}, f32[8,1536,256]{2,1,0:T(8,128)}, bf16[24,128,128]{2,1,0:T(8,128)(2,1)}, bf16[24,128,128]{2,1,0:T(8,128)(2,1)}) custom-call(s32[8,12]{1,0:T(8,128)} %subtract_clamp_fusion.places, s32[8]{0:T(128)} %dynamic_slice.7.active, bf16[1024,128]{1,0:T(8,128)(2,1)} %q_ref.3, bf16[1024,128]{1,0:T(8,128)(2,1)} %mid_k.1, ...), custom_call_target="tpu_custom_call" | custom-call | tf_op jit(solution)/shard_map/forward/pallas_call | solution.py:102
  60.5 0.0 collective-permute-done.6.upper
  60.5 0.0 copy-start.10
  60.5 0.0 collective-permute-done.7.lower
  60.6 0.0 copy-start.11
  60.6 0.0 copy-done.6
  60.6 0.0 copy-done.7
  60.6 0.0 copy-done.8
  60.6 0.0 copy-done.9
  60.6 0.0 copy-done.2
  60.6 0.0 copy-done.3
  60.6 0.6 copy-done.10
  61.2 0.0 copy-done.11
  61.2 3.5 %project.1 = (bf16[1024,128]{1,0:T(8,128)(2,1)}, bf16[8,128,128]{2,1,0:T(8,128)(2,1)}) custom-call(s32[1]{0:T(128)} %bitcast.head, bf16[1024,128]{1,0:T(8,128)(2,1)} %own.1, bf16[1024,128]{1,0:T(8,128)(2,1)} %copy-done.6, bf16[1024,128]{1,0:T(8,128)(2,1)} %copy-done.7, bf16[1024,128]{1,0:T(8,128)(2,1)} %copy-done.8, bf16[1024,128]{1,0:T(8,128)(2,1)} %copy-done.9, ...), custom_call_target="tpu_custom_call" | custom-call | tf_op jit(solution)/shard_map/project/pallas_call | solution.py:259
  64.7 17.1 %all-to-all-start = ((bf16[64,16,128]{2,1,0:T(8,128)(2,1)}), bf16[64,16,128]{2,1,0:T(8,128)(2,1)S(1)}, u32[]{:S(2)}, u32[]{:S(2)}) async-start(bf16[64,16,128]{2,1,0:T(8,128)(2,1)} %bitcast.4), calls=%async_computation | async-start | bytes 524288 | tf_op jit(solution)/shard_map/all_to_all | solution.py:303
  81.8 14.6 %backward.1 = (bf16[1024,128]{1,0:T(8,128)(2,1)}, f32[1024,256]{1,0:T(8,128)}, bf16[1024,256]{1,0:T(8,128)(2,1)}, bf16[1024,256]{1,0:T(8,128)(2,1)}) custom-call(s32[8,12]{1,0:T(8,128)} %subtract_clamp_fusion.places, s32[8]{0:T(128)} %dynamic_slice.7.active, bf16[1024,128]{1,0:T(8,128)(2,1)} %q_ref.3, bf16[1024,128]{1,0:T(8,128)(2,1)} %get-tuple-element.15.ga_ref, ...), custom_call_target="tpu_custom_call" | custom-call | tf_op jit(solution)/shard_map/backward/pallas_call | solution.py:194
  96.3 9.1 %collective-permute-start.10 = (bf16[1024,256]{1,0:T(8,128)(2,1)}, bf16[1024,256]{1,0:T(8,128)(2,1)S(1)}, u32[]{:S(2)}, u32[]{:S(2)}) collective-permute-start(bf16[1024,256]{1,0:T(8,128)(2,1)} %get-tuple-element.21), channel_id=1, source_target_pairs={{0,504},{8,0},{16,8},{24,16},{32,24},{40,32},{48,40},{56,48},{64,5... | collective-permute-start | bytes 1572872 | tf_op jit(solution)/shard_map/ppermute | solution.py:226
  105.4 1.9 %collective-permute-start.11 = (bf16[1024,256]{1,0:T(8,128)(2,1)}, bf16[1024,256]{1,0:T(8,128)(2,1)S(1)}, u32[]{:S(2)}, u32[]{:S(2)}) collective-permute-start(bf16[1024,256]{1,0:T(8,128)(2,1)} %get-tuple-element.22), channel_id=1, source_target_pairs={{0,8},{8,16},{16,24},{24,32},{32,40},{40,48},{48,56},{56,64},{64,7... | collective-permute-start | bytes 1572872 | tf_op jit(solution)/shard_map/ppermute | solution.py:226
  107.4 0.0 all-to-all-done
  107.4 0.1 convert_reduce_fusion
  107.5 0.7 broadcast_in_dim.2
  108.2 9.2 %all-to-all-start.1 = ((bf16[64,16,128]{2,1,0:T(8,128)(2,1)}), bf16[64,16,128]{2,1,0:T(8,128)(2,1)S(1)}, u32[]{:S(2)}, u32[]{:S(2)}) async-start(bf16[64,16,128]{2,1,0:T(8,128)(2,1)} %broadcast_in_dim.2), calls=%async_computation.1 | async-start | bytes 524288 | tf_op jit(solution)/shard_map/all_to_all | solution.py:306
  117.4 0.0 collective-permute-done.10
  117.4 0.0 collective-permute-done.11
  117.4 1.4 %add_convert_fusion = bf16[1024,256]{1,0:T(8,128)(2,1)S(1)} fusion(bf16[1024,256]{1,0:T(8,128)(2,1)S(1)} %collective-permute-done.11, f32[1024,256]{1,0:T(8,128)} %get-tuple-element.20, bf16[1024,256]{1,0:T(8,128)(2,1)S(1)} %collective-permute-done.10), kind=kLoop, calls=%fused_computation | loop fusion | flops 1310720 | bytes 2621440 | tf_op jit(solution)/shard_map/convert.1
  118.8 0.8 fusion
  119.6 9.7 %all-to-all-done.1 = bf16[64,16,128]{2,1,0:T(8,128)(2,1)S(1)} async-done(((bf16[64,16,128]{2,1,0:T(8,128)(2,1)}), bf16[64,16,128]{2,1,0:T(8,128)(2,1)S(1)}, u32[]{:S(2)}, u32[]{:S(2)}) %all-to-all-start.1) | async-done | bytes 262176 | tf_op jit(solution)/shard_map/all_to_all | solution.py:306
  129.4 0.7 copy-done.1
  130.1 1.8 %place.1 = f32[128,1024]{1,0:T(8,128)} custom-call(s32[1]{0:T(128)} %bitcast.head, bf16[8,128,128]{2,1,0:T(8,128)(2,1)} %bitcast.3), custom_call_target="tpu_custom_call" | custom-call | tf_op jit(solution)/shard_map/place/pallas_call | solution.py:280
  (5 shorter events, 0.0 us)
Async XLA Ops:
  0.6 37.3 %copy-start = (s32[512,12]{0,1:T(8,128)S(1)}, s32[512,12]{0,1:T(8,128)}, u32[]{:S(2)}) copy-start(s32[512,12]{0,1:T(8,128)} %param.12) | copy-start | bytes 73732
  0.6 9.9 %collective-permute-start = (bf16[1024,128]{1,0:T(8,128)(2,1)}, bf16[1024,128]{1,0:T(8,128)(2,1)S(1)}, u32[]{:S(2)}, u32[]{:S(2)}) collective-permute-start(bf16[1024,128]{1,0:T(8,128)(2,1)} %own.1), channel_id=1, source_target_pairs={{0,1},{1,2},{2,3},{3,4},{4,5},{5,6},{6,7},{7,0},{8,9},{9,10},{10,1... | collective-permute-start | bytes 786440 | tf_op jit(solution)/shard_map/ppermute | solution.py:226
  4.7 8.8 %collective-permute-start.1 = (bf16[1024,128]{1,0:T(8,128)(2,1)}, bf16[1024,128]{1,0:T(8,128)(2,1)S(1)}, u32[]{:S(2)}, u32[]{:S(2)}) collective-permute-start(bf16[1024,128]{1,0:T(8,128)(2,1)} %own.1), channel_id=1, source_target_pairs={{0,7},{1,0},{2,1},{3,2},{4,3},{5,4},{6,5},{7,6},{8,15},{9,8},{10,9... | collective-permute-start | bytes 786440 | tf_op jit(solution)/shard_map/ppermute | solution.py:226
  10.5 50.0 %copy-start.6 = (bf16[1024,128]{1,0:T(8,128)(2,1)}, bf16[1024,128]{1,0:T(8,128)(2,1)S(1)}, u32[]{:S(2)}) copy-start(bf16[1024,128]{1,0:T(8,128)(2,1)S(1)} %collective-permute-done.r1) | copy-start | bytes 786436
  10.5 19.6 %collective-permute-start.2 = (bf16[1024,128]{1,0:T(8,128)(2,1)S(1)}, bf16[1024,128]{1,0:T(8,128)(2,1)S(1)}, u32[]{:S(2)}, u32[]{:S(2)}) collective-permute-start(bf16[1024,128]{1,0:T(8,128)(2,1)S(1)} %collective-permute-done.r1), channel_id=1, source_target_pairs={{0,1},{1,2},{2,3},{3,4},{4,5},{5,6},{6,7},{7,0},{8,9},{9,10},{10,1... | collective-permute-start | bytes 786440 | tf_op jit(solution)/shard_map/ppermute | solution.py:226
  13.4 47.1 %copy-start.7 = (bf16[1024,128]{1,0:T(8,128)(2,1)}, bf16[1024,128]{1,0:T(8,128)(2,1)S(1)}, u32[]{:S(2)}) copy-start(bf16[1024,128]{1,0:T(8,128)(2,1)S(1)} %collective-permute-done.1.l1) | copy-start | bytes 786436
  13.5 18.6 %collective-permute-start.3 = (bf16[1024,128]{1,0:T(8,128)(2,1)S(1)}, bf16[1024,128]{1,0:T(8,128)(2,1)S(1)}, u32[]{:S(2)}, u32[]{:S(2)}) collective-permute-start(bf16[1024,128]{1,0:T(8,128)(2,1)S(1)} %collective-permute-done.1.l1), channel_id=1, source_target_pairs={{0,7},{1,0},{2,1},{3,2},{4,3},{5,4},{6,5},{7,6},{8,15},{9,8},{10,9... | collective-permute-start | bytes 786440 | tf_op jit(solution)/shard_map/ppermute | solution.py:226
  19.8 27.2 %collective-permute-start.9 = (bf16[1024,256]{1,0:T(8,128)(2,1)S(1)}, bf16[1024,256]{1,0:T(8,128)(2,1)S(1)}, u32[]{:S(2)}, u32[]{:S(2)}) collective-permute-start(bf16[1024,256]{1,0:T(8,128)(2,1)S(1)} %constant_dynamic-update-slice_fusion), channel_id=1, source_target_pairs={{0,504},{8,0},{16,8},{24,16},{32,24},{40,32},{48,40},{56,48},{64,5... | collective-permute-start | bytes 1572872 | tf_op jit(solution)/shard_map/ppermute | solution.py:226
  28.2 18.8 %collective-permute-start.8 = (bf16[1024,256]{1,0:T(8,128)(2,1)S(1)}, bf16[1024,256]{1,0:T(8,128)(2,1)S(1)}, u32[]{:S(2)}, u32[]{:S(2)}) collective-permute-start(bf16[1024,256]{1,0:T(8,128)(2,1)S(1)} %constant_dynamic-update-slice_fusion), channel_id=1, source_target_pairs={{0,8},{8,16},{16,24},{24,32},{32,40},{40,48},{48,56},{56,64},{64,7... | collective-permute-start | bytes 1572872 | tf_op jit(solution)/shard_map/ppermute | solution.py:226
  30.1 30.5 %copy-start.8 = (bf16[1024,128]{1,0:T(8,128)(2,1)}, bf16[1024,128]{1,0:T(8,128)(2,1)S(1)}, u32[]{:S(2)}) copy-start(bf16[1024,128]{1,0:T(8,128)(2,1)S(1)} %collective-permute-done.2.r2) | copy-start | bytes 786436
  30.1 8.3 %collective-permute-start.4 = (bf16[1024,128]{1,0:T(8,128)(2,1)S(1)}, bf16[1024,128]{1,0:T(8,128)(2,1)S(1)}, u32[]{:S(2)}, u32[]{:S(2)}) collective-permute-start(bf16[1024,128]{1,0:T(8,128)(2,1)S(1)} %collective-permute-done.2.r2), channel_id=1, source_target_pairs={{0,1},{1,2},{2,3},{3,4},{4,5},{5,6},{6,7},{7,0},{8,9},{9,10},{10,1... | collective-permute-start | bytes 786440 | tf_op jit(solution)/shard_map/ppermute | solution.py:226
  32.1 28.5 %copy-start.9 = (bf16[1024,128]{1,0:T(8,128)(2,1)}, bf16[1024,128]{1,0:T(8,128)(2,1)S(1)}, u32[]{:S(2)}) copy-start(bf16[1024,128]{1,0:T(8,128)(2,1)S(1)} %collective-permute-done.3.l2) | copy-start | bytes 786436
  32.1 9.0 %collective-permute-start.5 = (bf16[1024,128]{1,0:T(8,128)(2,1)S(1)}, bf16[1024,128]{1,0:T(8,128)(2,1)S(1)}, u32[]{:S(2)}, u32[]{:S(2)}) collective-permute-start(bf16[1024,128]{1,0:T(8,128)(2,1)S(1)} %collective-permute-done.3.l2), channel_id=1, source_target_pairs={{0,7},{1,0},{2,1},{3,2},{4,3},{5,4},{6,5},{7,6},{8,15},{9,8},{10,9... | collective-permute-start | bytes 786440 | tf_op jit(solution)/shard_map/ppermute | solution.py:226
  38.5 22.1 %copy-start.2 = (bf16[1024,128]{1,0:T(8,128)(2,1)}, bf16[1024,128]{1,0:T(8,128)(2,1)S(1)}, u32[]{:S(2)}) copy-start(bf16[1024,128]{1,0:T(8,128)(2,1)S(1)} %collective-permute-done.4.r3) | copy-start | bytes 786436
  39.2 21.4 %collective-permute-start.6 = (bf16[512,128]{1,0:T(8,128)(2,1)}, bf16[512,128]{1,0:T(8,128)(2,1)S(1)}, u32[]{:S(2)}, u32[]{:S(2)}) collective-permute-start(bf16[512,128]{1,0:T(8,128)(2,1)} %slice.18), channel_id=1, source_target_pairs={{0,1},{1,2},{2,3},{3,4},{4,5},{5,6},{6,7},{7,0},{8,9},{9,10},{10,1... | collective-permute-start | bytes 393224 | tf_op jit(solution)/shard_map/ppermute | solution.py:226
  41.1 19.5 %copy-start.3 = (bf16[1024,128]{1,0:T(8,128)(2,1)}, bf16[1024,128]{1,0:T(8,128)(2,1)S(1)}, u32[]{:S(2)}) copy-start(bf16[1024,128]{1,0:T(8,128)(2,1)S(1)} %collective-permute-done.5.l3) | copy-start | bytes 786436
  41.8 18.7 %collective-permute-start.7 = (bf16[512,128]{1,0:T(8,128)(2,1)}, bf16[512,128]{1,0:T(8,128)(2,1)S(1)}, u32[]{:S(2)}, u32[]{:S(2)}) collective-permute-start(bf16[512,128]{1,0:T(8,128)(2,1)} %slice.19), channel_id=1, source_target_pairs={{0,7},{1,0},{2,1},{3,2},{4,3},{5,4},{6,5},{7,6},{8,15},{9,8},{10,9... | collective-permute-start | bytes 393224 | tf_op jit(solution)/shard_map/ppermute | solution.py:226
  47.0 0.8 copy-start.4
  47.8 0.8 copy-start.5
  60.5 0.7 copy-start.10
  60.6 0.7 copy-start.11
  64.7 42.7 %all-to-all-start = ((bf16[64,16,128]{2,1,0:T(8,128)(2,1)}), bf16[64,16,128]{2,1,0:T(8,128)(2,1)S(1)}, u32[]{:S(2)}, u32[]{:S(2)}) async-start(bf16[64,16,128]{2,1,0:T(8,128)(2,1)} %bitcast.4), calls=%async_computation | async-start | bytes 524288 | tf_op jit(solution)/shard_map/all_to_all | solution.py:303
  96.3 21.0 %collective-permute-start.10 = (bf16[1024,256]{1,0:T(8,128)(2,1)}, bf16[1024,256]{1,0:T(8,128)(2,1)S(1)}, u32[]{:S(2)}, u32[]{:S(2)}) collective-permute-start(bf16[1024,256]{1,0:T(8,128)(2,1)} %get-tuple-element.21), channel_id=1, source_target_pairs={{0,504},{8,0},{16,8},{24,16},{32,24},{40,32},{48,40},{56,48},{64,5... | collective-permute-start | bytes 1572872 | tf_op jit(solution)/shard_map/ppermute | solution.py:226
  105.4 12.0 %collective-permute-start.11 = (bf16[1024,256]{1,0:T(8,128)(2,1)}, bf16[1024,256]{1,0:T(8,128)(2,1)S(1)}, u32[]{:S(2)}, u32[]{:S(2)}) collective-permute-start(bf16[1024,256]{1,0:T(8,128)(2,1)} %get-tuple-element.22), channel_id=1, source_target_pairs={{0,8},{8,16},{16,24},{24,32},{32,40},{40,48},{48,56},{56,64},{64,7... | collective-permute-start | bytes 1572872 | tf_op jit(solution)/shard_map/ppermute | solution.py:226
  108.2 21.1 %all-to-all-start.1 = ((bf16[64,16,128]{2,1,0:T(8,128)(2,1)}), bf16[64,16,128]{2,1,0:T(8,128)(2,1)S(1)}, u32[]{:S(2)}, u32[]{:S(2)}) async-start(bf16[64,16,128]{2,1,0:T(8,128)(2,1)} %broadcast_in_dim.2), calls=%async_computation.1 | async-start | bytes 524288 | tf_op jit(solution)/shard_map/all_to_all | solution.py:306
  129.4 0.7 copy-start.1

commit v3 on v1

v3 whole, which is shorter than its diff:
```python
import functools

import jax
import jax.numpy as jnp
from jax import lax
from jax.experimental import pallas as pl
from jax.experimental.pallas import tpu as pltpu
from jax.sharding import PartitionSpec as P


HD = 64
BS = 128
SIZES = (4, 6, 8, 10, 12)


def by_size(active, run):
    low = 0
    for size in SIZES:
        pl.when((active > low) & (active <= size))(lambda size=size: run(size))
        low = size


def cost(steps):
    return pl.CostEstimate(flops=2 * steps * 10**9, bytes_accessed=steps * 10**6, transcendentals=0)


def spread_columns(rows_t):
    blank = jnp.zeros((HD, BS), rows_t.dtype)
    upper = jnp.concatenate([rows_t[:HD], blank], axis=1)
    lower = jnp.concatenate([blank, rows_t[HD:]], axis=1)
    return jnp.concatenate([upper, lower], axis=0)


def spread_rows(rows):
    lane = lax.broadcasted_iota(jnp.int32, rows.shape, 1)
    blank = jnp.zeros_like(rows)
    return jnp.concatenate(
        [jnp.where(lane < HD, rows, blank), jnp.where(lane >= HD, rows, blank)], axis=0
    )


def own_heads(both):
    return jnp.concatenate([both[:HD, :BS], both[HD:, BS:]], axis=0)


def dot(a, b):
    return jnp.dot(a, b, preferred_element_type=jnp.float32)


def forward_kernel(skip, places, active, q_ref, *rest):
    factor = HD ** (-0.5)
    if skip:
        (k_ref, vt_ref, _, _, att_ref, p_ref, s_scr) = rest
    else:
        (mid_k, mid_v, left, right, att_ref, p_ref, kt_ref, v_ref, k_ref, vt_ref, s_scr) = rest

        @pl.when(pl.program_id(0) == 0)
        def _():
            count = mid_k.shape[0] // BS
            for b in range(3 * count):
                side, at = divmod(b, count)
                rows = pl.ds(at * BS, BS)
                if side == 1:
                    k, v = mid_k[rows, :], mid_v[rows, :]
                else:
                    source = left if side == 0 else right
                    k, v = source[rows, :BS], source[rows, BS:]
                k_ref[b] = k
                kt_ref[b] = k.T
                v_ref[b] = v
                vt_ref[b] = v.T

    step = pl.program_id(0) + skip
    query = spread_columns(q_ref[...].T * factor)

    def run(size):
        highest = None
        for s in range(size):
            scores = dot(k_ref[places[step, s]], query)
            if s == size - 1:
                scores = jnp.where(s < active[step], scores, -1e30)
            s_scr[pl.ds(s * BS, BS), :] = scores
            part = jnp.max(scores.reshape(BS // 8, 8, 2 * BS), axis=0)
            highest = part if highest is None else jnp.maximum(highest, part)
        highest = jnp.max(highest, axis=0, keepdims=True)
        total = None
        for s in range(size):
            grown = jnp.exp(s_scr[pl.ds(s * BS, BS), :] - highest)
            s_scr[pl.ds(s * BS, BS), :] = grown
            part = jnp.sum(grown.reshape(BS // 8, 8, 2 * BS), axis=0)
            total = part if total is None else total + part
        inverse = 1.0 / jnp.sum(total, axis=0, keepdims=True)
        attended = None
        for s in range(0, size, 2):
            weights = s_scr[pl.ds(s * BS, 2 * BS), :] * inverse
            p_ref[0, pl.ds(s * BS, 2 * BS), :] = weights
            pair = jnp.concatenate([vt_ref[places[step, s]], vt_ref[places[step, s + 1]]], axis=1)
            term = dot(pair, weights.astype(jnp.bfloat16))
            attended = term if attended is None else attended + term
        att_ref[...] = own_heads(attended).astype(jnp.bfloat16)

    by_size(active[step], run)


def forward(places, active, query_rows, skip, steps, sources, carried):
    blocks, slots = places.shape
    rows, cols = query_rows.shape
    extent = 3 * blocks
    whole = lambda *shape: pl.BlockSpec(shape, lambda i, *_: (0,) * len(shape))
    window = jax.ShapeDtypeStruct((extent, BS, cols), jnp.bfloat16)
    count = 0 if skip else 4
    in_specs = [pl.BlockSpec((BS, cols), lambda i, *_: (i + skip, 0))]
    in_specs += [whole(*x.shape) for x in sources]
    in_specs += [pl.BlockSpec(memory_space=pl.ANY)] * len(carried)
    return pl.pallas_call(
        functools.partial(forward_kernel, skip),
        grid_spec=pltpu.PrefetchScalarGridSpec(
            num_scalar_prefetch=2,
            grid=(steps,),
            in_specs=in_specs,
            out_specs=[
                pl.BlockSpec((cols, BS), lambda i, *_: (0, i + skip)),
                pl.BlockSpec((1, slots * BS, 2 * BS), lambda i, *_: (i + skip, 0, 0)),
            ]
            + [whole(extent, BS, cols)] * count,
            scratch_shapes=[pltpu.VMEM((slots * BS, 2 * BS), jnp.float32)],
        ),
        out_shape=[
            jax.ShapeDtypeStruct((cols, rows), jnp.bfloat16),
            jax.ShapeDtypeStruct((blocks, slots * BS, 2 * BS), jnp.float32),
        ]
        + [window] * count,
        input_output_aliases={5: 0, 6: 1} if skip else {},
        compiler_params=pltpu.CompilerParams(dimension_semantics=("arbitrary",)),
        cost_estimate=cost(steps),
        name="forward",
    )(places, active, query_rows, *sources, *carried)


def backward_kernel(first, last, places, active, q_ref, ga_ref, att_ref, p_ref, kt_ref, v_ref, *rest):
    if first:
        (dq_ref, dk, dv) = rest
    elif last:
        (_, dk_base, dv_base, dq_ref, mid_ref, left_ref, right_ref, dk, dv) = rest
    here = pl.program_id(0)
    factor = HD ** (-0.5)

    @pl.when(here == 0)
    def _():
        if first:
            dk[...] = jnp.zeros_like(dk)
            dv[...] = jnp.zeros_like(dv)
        else:
            dk[...] = dk_base[...]
            dv[...] = dv_base[...]

    step = here if first else here + pl.num_programs(0)
    grad = ga_ref[...]
    grad_t = grad.T
    products = grad_t.astype(jnp.float32) * att_ref[...].astype(jnp.float32)
    dots = jnp.concatenate(
        [
            jnp.sum(products[:HD], axis=0, keepdims=True),
            jnp.sum(products[HD:], axis=0, keepdims=True),
        ],
        axis=1,
    )
    grad_wide = spread_columns(grad_t)
    grad_tall = spread_rows(grad)
    query_tall = spread_rows(q_ref[...] * factor)

    def run(size):
        total = None
        for s in range(0, size, 2):
            changes, pair = [], []
            for j in range(2):
                place = places[step, s + j]
                weights = p_ref[0, pl.ds((s + j) * BS, BS), :]
                change = weights * (dot(v_ref[place], grad_wide) - dots)
                change = change.astype(jnp.bfloat16)
                changes.append(change)
                pair.append(kt_ref[place])
                dk[place] += dot(change, query_tall)
                dv[place] += dot(weights.astype(jnp.bfloat16), grad_tall)
            term = dot(jnp.concatenate(pair, axis=1), jnp.concatenate(changes, axis=0))
            total = term if total is None else total + term
        dq_ref[...] = (own_heads(total) * factor).T.astype(jnp.bfloat16)

    by_size(active[step], run)

    if last:

        @pl.when(here == pl.num_programs(0) - 1)
        def _():
            count = mid_ref.shape[0] // BS
            for b in range(3 * count):
                side, at = divmod(b, count)
                target = (left_ref, mid_ref, right_ref)[side]
                rows = pl.ds(at * BS, BS)
                target[rows, :BS] = dk[b].astype(target.dtype)
                target[rows, BS:] = dv[b].astype(target.dtype)


def backward(places, active, query_rows, grad_attended, att_t, weights, keys_t, values, base):
    blocks, slots = places.shape
    rows, cols = query_rows.shape
    extent = 3 * blocks
    steps = blocks // 2
    first = not base
    skip = 0 if first else steps
    whole = lambda *shape: pl.BlockSpec(shape, lambda i, *_: (0,) * len(shape))
    one = pl.BlockSpec((BS, cols), lambda i, *_: (i + skip, 0))
    sums = jax.ShapeDtypeStruct((extent, BS, cols), jnp.float32)
    in_specs = [
        one,
        one,
        pl.BlockSpec((cols, BS), lambda i, *_: (0, i + skip)),
        pl.BlockSpec((1, slots * BS, 2 * BS), lambda i, *_: (i + skip, 0, 0)),
        whole(extent, BS, cols),
        whole(extent, BS, cols),
    ]
    out_shape = [jax.ShapeDtypeStruct((rows, cols), jnp.bfloat16)]
    if first:
        out_specs = [one, whole(*sums.shape), whole(*sums.shape)]
        out_shape += [sums, sums]
        scratch, aliases = [], {}
    else:
        in_specs += [pl.BlockSpec(memory_space=pl.ANY), whole(*sums.shape), whole(*sums.shape)]
        out_specs = [one] + [whole(rows, 2 * cols)] * 3
        out_shape += [
            jax.ShapeDtypeStruct((rows, 2 * cols), kind)
            for kind in (jnp.float32, jnp.bfloat16, jnp.bfloat16)
        ]
        scratch = [pltpu.VMEM(sums.shape, jnp.float32)] * 2
        aliases = {len(in_specs) - 3 + 2: 0}
    return pl.pallas_call(
        functools.partial(backward_kernel, first, not first),
        grid_spec=pltpu.PrefetchScalarGridSpec(
            num_scalar_prefetch=2,
            grid=(steps,),
            in_specs=in_specs,
            out_specs=out_specs,
            scratch_shapes=scratch,
        ),
        out_shape=out_shape,
        input_output_aliases=aliases,
        compiler_params=pltpu.CompilerParams(dimension_semantics=("arbitrary",)),
        cost_estimate=cost(2 * steps),
        name="backward",
    )(places, active, query_rows, grad_attended, att_t, weights, keys_t, values, *base)


def shifted(x, axis, by):
    count = lax.axis_size(axis)
    return lax.ppermute(x, axis, [(i, (i + by) % count) for i in range(count)])


def project_kernel(skip, order, *refs):
    w_ref, att_ref = refs[:2]
    ga_ref, wg_ref = refs[-2:]
    chunks = refs[2:-2]
    total = None
    if skip:
        total = chunks[0][...]
        wg_ref[...] = chunks[1][...]
        chunks = chunks[2:]
    att = att_ref[...]
    for k in range(0, len(chunks), 2):
        places = [order[skip + k + j] for j in range(2)]
        part = jnp.concatenate([chunks[k][...], chunks[k + 1][...]], axis=1)
        sides = [w_ref[:, pl.ds(pl.multiple_of(at * BS, BS), BS)] for at in places]
        term = lax.dot_general(
            part,
            jnp.concatenate(sides, axis=1),
            (((1,), (1,)), ((), ())),
            preferred_element_type=jnp.float32,
        )
        total = term if total is None else total + term
        grad = dot(att, part)
        for j in range(2):
            wg_ref[places[j]] = grad[:, j * BS : (j + 1) * BS].astype(wg_ref.dtype)
    ga_ref[...] = total.astype(ga_ref.dtype)


def project(order, chunks, out_weight, att_t, base):
    rows = chunks[0].shape[0]
    cols, width = out_weight.shape
    count = width // BS
    return pl.pallas_call(
        functools.partial(project_kernel, count - len(chunks) if base else 0),
        in_specs=[pl.BlockSpec(memory_space=pltpu.SMEM)]
        + [pl.BlockSpec(memory_space=pltpu.VMEM)] * (len(chunks) + len(base) + 2),
        out_shape=[
            jax.ShapeDtypeStruct((rows, cols), jnp.bfloat16 if base else jnp.float32),
            jax.ShapeDtypeStruct((count, cols, BS), jnp.bfloat16),
        ],
        cost_estimate=cost(1),
        name="project",
    )(order, out_weight, att_t, *base, *chunks)


def place_kernel(sum_ref, out_ref):
    for k in range(sum_ref.shape[0]):
        out_ref[:, k * BS : (k + 1) * BS] = sum_ref[k].astype(jnp.float32)


def place(sums):
    count, cols, width = sums.shape
    return pl.pallas_call(
        place_kernel,
        out_shape=jax.ShapeDtypeStruct((cols, count * width), jnp.float32),
        name="place",
    )(sums)


def next_head(x):
    rings, count = lax.axis_size("ctx"), lax.axis_size("head")
    pairs = []
    for c in range(rings):
        by = 1 - 2 * (c % 2)
        pairs += [(c * count + h, c * count + (h + by) % count) for h in range(count)]
    return lax.ppermute(x, ("ctx", "head"), pairs)


def total_piece(partial, axis, scale):
    members = lax.axis_size(axis)
    pieces = partial.reshape(members, -1, partial.shape[-1])
    pieces = lax.all_to_all(pieces, axis, 0, 0)
    piece = jnp.sum(pieces.astype(jnp.float32), axis=0) * scale
    copies = jnp.broadcast_to(piece.astype(partial.dtype)[None], pieces.shape)
    return copies


def ring_order():
    count = lax.axis_size("head")
    by = 1 - 2 * (lax.axis_index("ctx") % 2)
    return (lax.axis_index("head") - by * jnp.arange(count, dtype=jnp.int32)) % count


def body(query_rows, key_rows, value_rows, out_grad, out_weight, neighbours, counts):
    row_count, col_count = query_rows.shape
    blocks = row_count // BS
    extent = 3 * blocks
    ctx_index = lax.axis_index("ctx")
    packed = jnp.concatenate([key_rows, value_rows], axis=1)
    left = shifted(packed, "ctx", 1)
    right = shifted(packed, "ctx", -1)
    first = ctx_index * blocks
    places = lax.dynamic_slice_in_dim(neighbours, first, blocks, axis=0)
    places = jnp.clip(places - (first - blocks), 0, extent - 1)
    active = lax.dynamic_slice_in_dim(counts, first, blocks, axis=0)
    order = ring_order()
    chunks = [out_grad]
    for _ in range(2):
        chunks.append(next_head(chunks[-1]))
    sources, carried = (key_rows, value_rows, left, right), ()
    for at in range(0, blocks, 2):
        chunks.append(next_head(chunks[-1]))
        outs = forward(places, active, query_rows, at, 2, sources, carried)
        att_t, weights = outs[:2]
        chunks[-1], att_t = lax.optimization_barrier((chunks[-1], att_t))
        if at == 0:
            keys_t, values, *sources = outs[2:]
        carried = (att_t, weights)
    last = next_head(chunks[-1])
    base = project(order, chunks[:6], out_weight, att_t, ())
    last, *base = lax.optimization_barrier((last, *base))
    grad_attended, partial = project(order, [chunks[6], last], out_weight, att_t, base)
    node_count = row_count * lax.axis_size("ctx")
    shared = (att_t, weights, keys_t, values)
    carried = backward(places, active, query_rows, grad_attended, *shared, ())
    copies = total_piece(partial, "ctx", node_count ** (-0.5))
    copies, *carried = lax.optimization_barrier((copies, *carried))
    query_grad, middle, to_left, to_right = backward(
        places, active, query_rows, grad_attended, *shared, carried
    )
    from_right = shifted(to_left, "ctx", -1)
    from_left = shifted(to_right, "ctx", 1)
    weight_sum = lax.all_to_all(copies, "ctx", 0, 0)
    weight_grad = place(weight_sum.reshape(partial.shape))
    combined = middle + from_right.astype(jnp.float32) + from_left.astype(jnp.float32)
    key_grad = combined[:, :col_count].astype(jnp.bfloat16)
    value_grad = combined[:, col_count:].astype(jnp.bfloat16)
    return (query_grad, key_grad, value_grad, weight_grad)


def solution(mesh):
    placed = (
        P("ctx", "head"),
        P("ctx", "head"),
        P("ctx", "head"),
        P("ctx", "head"),
        P("head", None),
        P(),
        P(),
    )
    return jax.shard_map(
        body,
        mesh=mesh,
        in_specs=placed,
        out_specs=(P("ctx", "head"), P("ctx", "head"), P("ctx", "head"), P("head", None)),
        check_vma=False,
    )
```

time: 301 us -> 145 us (0.48)
  waiting for transfers between devices: 219 us -> 3.53 us
  starting transfers between devices: 22.7 us -> 56 us
  Pallas kernels: 30.9 us -> 53.9 us
  blocking collectives: 0 us -> 19.9 us
  between operations: 14.1 us -> 0.88 us
  matrix products: 4.25 us -> 0 us
    psum x1 -> x0, waiting for transfers between devices: 195 us -> none  [body(): weight_grad = lax.psum(product, 'ctx') * node_count ** (-0.5)]
    ppermute x0 -> x7, starting transfers between devices: none -> 26.5 us  [next_head(): return lax.ppermute(x, ('ctx', 'head'), pairs)]
    pallas_call x2 -> x9, Pallas kernels: 30.9 us -> 53.9 us  [the longest x4 23.2 us: forward(): pl.pallas_call(functools.partial(forward_kernel, skip), grid_spec=pltpu.P...]
    all_to_all x0 -> x1, blocking collectives: none -> 19.9 us  [body(): weight_sum = lax.all_to_all(copies, 'ctx', 0, 0)]
    all_gather x1 -> x0, waiting for transfers between devices: 19.4 us -> none  [body(): gathered = lax.all_gather(out_grad, 'head', axis=1, tiled=True)]
    all_to_all x0 -> x1, starting transfers between devices: none -> 17.3 us  [total_piece(): pieces = lax.all_to_all(pieces, axis, 0, 0)]
    ppermute x4, starting transfers between devices: 22.6 us -> 12.2 us  [shifted(): return lax.ppermute(x, axis, [(i, (i + by) % count) for i in range(count)])]
    dot_general x2 -> x0, matrix products: 4.25 us -> none  [the longest x1 3.01 us: body(): jnp.einsum('ro,jo->rj', gathered, out_weight, preferred_element_type=jnp....]
  transfers between devices with their start and end apart: 6 -> 12, of which waited for: 3 -> 4; matrix products, arithmetic and copies ran while one was open for 3% -> 3% of each run, Pallas kernels for 4% -> 27%
where the time goes in v3:
time: 145 us; the launch traced here: 144 us
  starting transfers between devices  56 us (39%)
  Pallas kernels  53.9 us (37%)
  blocking collectives  19.9 us (14%)
  local copies, waits for them, and re-layouts  6.64 us (5%)
  waiting for transfers between devices  3.53 us (2%)
  other arithmetic  2.59 us (2%)
    ppermute x7, starting transfers between devices, next_head(): return lax.ppermute(x, ('ctx', 'head'), pairs)  26.5 us
    pallas_call x4, Pallas kernels, forward(): pl.pallas_call(functools.partial(forward_kernel, skip), grid_spec=pltpu.P...  23.2 us
    pallas_call x2, Pallas kernels, backward(): pl.pallas_call(functools.partial(backward_kernel, first, not first), grid...  23.1 us
    all_to_all x1, blocking collectives, body(): weight_sum = lax.all_to_all(copies, 'ctx', 0, 0)  19.9 us
    all_to_all x1, starting transfers between devices, total_piece(): pieces = lax.all_to_all(pieces, axis, 0, 0)  17.3 us
    ppermute x4, starting transfers between devices, shifted(): return lax.ppermute(x, axis, [(i, (i + by) % count) for i in range(count)])  12.2 us
    pallas_call x2, Pallas kernels, project(): pl.pallas_call(functools.partial(project_kernel, count - len(chunks) if b...  5.81 us
    unnamed x22, local copies, waits for them, and re-layouts  3.4 us
  transfers between devices with their start and end apart: 12, of which 4 were waited for; matrix products, arithmetic and copies ran while one was open for 3% of the time, Pallas kernels for 27%

profile of v3, /device:TPU:1, one launch (start us, length us, event | category | flops | bytes accessed | tf_op | source)
XLA Modules:
  0.0 143.5 jit_solution(1539759827374941207)
XLA Ops:
  0.6 0.0 copy-start
  0.6 5.9 %collective-permute-start = (bf16[1024,128]{1,0:T(8,128)(2,1)}, bf16[1024,128]{1,0:T(8,128)(2,1)S(1)}, u32[]{:S(2)}, u32[]{:S(2)}) collective-permute-start(bf16[1024,128]{1,0:T(8,128)(2,1)} %refs_2_.1), channel_id=1, source_target_pairs={{0,1},{1,2},{2,3},{3,4},{4,5},{5,6},{6,7},{7,0},{8,15},{9,8},{10,9... | collective-permute-start | bytes 786440 | tf_op jit(solution)/shard_map/ppermute | solution.py:322
  6.6 1.0 constant_dynamic-update-slice_fusion.1
  7.6 1.0 constant_dynamic-update-slice_fusion
  8.6 4.8 %collective-permute-start.4 = (bf16[1024,256]{1,0:T(8,128)(2,1)S(1)}, bf16[1024,256]{1,0:T(8,128)(2,1)S(1)}, u32[]{:S(2)}, u32[]{:S(2)}) collective-permute-start(bf16[1024,256]{1,0:T(8,128)(2,1)S(1)} %constant_dynamic-update-slice_fusion), channel_id=1, source_target_pairs={{0,504},{8,0},{16,8},{24,16},{32,24},{40,32},{48,40},{56,48},{64,5... | collective-permute-start | bytes 1572872 | tf_op jit(solution)/shard_map/ppermute | solution.py:255
  13.3 1.9 %collective-permute-start.3 = (bf16[1024,256]{1,0:T(8,128)(2,1)S(1)}, bf16[1024,256]{1,0:T(8,128)(2,1)S(1)}, u32[]{:S(2)}, u32[]{:S(2)}) collective-permute-start(bf16[1024,256]{1,0:T(8,128)(2,1)S(1)} %constant_dynamic-update-slice_fusion), channel_id=1, source_target_pairs={{0,8},{8,16},{16,24},{24,32},{32,40},{40,48},{48,56},{56,64},{64,7... | collective-permute-start | bytes 1572872 | tf_op jit(solution)/shard_map/ppermute | solution.py:255
  15.3 0.0 collective-permute-done.refs_3_
  15.3 0.0 copy-start.3
  15.3 4.9 %collective-permute-start.1 = (bf16[1024,128]{1,0:T(8,128)(2,1)S(1)}, bf16[1024,128]{1,0:T(8,128)(2,1)S(1)}, u32[]{:S(2)}, u32[]{:S(2)}) collective-permute-start(bf16[1024,128]{1,0:T(8,128)(2,1)S(1)} %collective-permute-done.refs_3_), channel_id=1, source_target_pairs={{0,1},{1,2},{2,3},{3,4},{4,5},{5,6},{6,7},{7,0},{8,15},{9,8},{10,9... | collective-permute-start | bytes 786440 | tf_op jit(solution)/shard_map/ppermute | solution.py:322
  20.2 0.0 copy-done
  20.2 0.1 constant_dynamic-slice_fusion
  20.3 1.3 dynamic_slice.7.active
  21.5 0.1 copy.19
  21.6 0.6 subtract_clamp_fusion.places
  22.2 1.2 collective-permute-done.1.refs_4_
  23.5 0.0 copy-start.4
  23.5 5.0 %collective-permute-start.2 = (bf16[1024,128]{1,0:T(8,128)(2,1)S(1)}, bf16[1024,128]{1,0:T(8,128)(2,1)S(1)}, u32[]{:S(2)}, u32[]{:S(2)}) collective-permute-start(bf16[1024,128]{1,0:T(8,128)(2,1)S(1)} %collective-permute-done.1.refs_4_), channel_id=1, source_target_pairs={{0,1},{1,2},{2,3},{3,4},{4,5},{5,6},{6,7},{7,0},{8,15},{9,8},{10,9... | collective-permute-start | bytes 786440 | tf_op jit(solution)/shard_map/ppermute | solution.py:322
  28.5 0.0 collective-permute-done.4.rest_3_
  28.5 0.0 copy-start.1
  28.5 0.0 collective-permute-done.3.rest_2_
  28.5 0.8 copy-done.1
  29.3 0.0 copy-start.2
  29.3 0.8 copy-done.2
  30.1 6.7 %forward.4 = (bf16[128,1024]{1,0:T(8,128)(2,1)}, f32[8,1536,256]{2,1,0:T(8,128)}, bf16[24,128,128]{2,1,0:T(8,128)(2,1)}, bf16[24,128,128]{2,1,0:T(8,128)(2,1)}, ...) custom-call(s32[8,12]{1,0:T(8,128)} %subtract_clamp_fusion.places, s32[8]{0:T(128)} %dynamic_slice.7.active, ...), custom_call_target="tpu_custom_call" | custom-call | flops 4000000000 | bytes 2000000 | tf_op jit(solution)/shard_map/forward/pallas_call | solution.py:115
  36.8 0.0 collective-permute-done.2.refs_5_
  36.8 0.0 copy-start.5
  36.9 1.9 %collective-permute-start.5 = (bf16[1024,128]{1,0:T(8,128)(2,1)S(1)}, bf16[1024,128]{1,0:T(8,128)(2,1)S(1)}, u32[]{:S(2)}, u32[]{:S(2)}) collective-permute-start(bf16[1024,128]{1,0:T(8,128)(2,1)S(1)} %collective-permute-done.2.refs_5_), channel_id=1, source_target_pairs={{0,1},{1,2},{2,3},{3,4},{4,5},{5,6},{6,7},{7,0},{8,15},{9,8},{10,9... | collective-permute-start | bytes 786440 | tf_op jit(solution)/shard_map/ppermute | solution.py:322
  38.8 5.0 %forward.5 = (bf16[128,1024]{1,0:T(8,128)(2,1)}, f32[8,1536,256]{2,1,0:T(8,128)}) custom-call(s32[8,12]{1,0:T(8,128)} %subtract_clamp_fusion.places, s32[8]{0:T(128)} %dynamic_slice.7.active, bf16[1024,128]{1,0:T(8,128)(2,1)} %q_ref.11, bf16[24,128,128]{2,1,0:T(8,128)(2,1)} %get-tuple-element.44.rest_0_, ...), custom_call_target="tpu_custom_call", output_to_operand_aliasing={{0}: (5, {}), {1}: (6, {})} | custom-call | flops 4000000000 | bytes 2000000 | tf_op jit(solution)/shard_map/forward/pallas_call | solution.py:115
  43.8 0.2 collective-permute-done.5.refs_6_
  44.0 0.0 copy-start.6
  44.0 3.1 %collective-permute-start.6 = (bf16[1024,128]{1,0:T(8,128)(2,1)S(1)}, bf16[1024,128]{1,0:T(8,128)(2,1)S(1)}, u32[]{:S(2)}, u32[]{:S(2)}) collective-permute-start(bf16[1024,128]{1,0:T(8,128)(2,1)S(1)} %collective-permute-done.5.refs_6_), channel_id=1, source_target_pairs={{0,1},{1,2},{2,3},{3,4},{4,5},{5,6},{6,7},{7,0},{8,15},{9,8},{10,9... | collective-permute-start | bytes 786440 | tf_op jit(solution)/shard_map/ppermute | solution.py:322
  47.1 5.9 %forward.6 = (bf16[128,1024]{1,0:T(8,128)(2,1)}, f32[8,1536,256]{2,1,0:T(8,128)}) custom-call(s32[8,12]{1,0:T(8,128)} %subtract_clamp_fusion.places, s32[8]{0:T(128)} %dynamic_slice.7.active, bf16[1024,128]{1,0:T(8,128)(2,1)} %q_ref.11, bf16[24,128,128]{2,1,0:T(8,128)(2,1)} %get-tuple-element.44.rest_0_, ...), custom_call_target="tpu_custom_call", output_to_operand_aliasing={{0}: (5, {}), {1}: (6, {})} | custom-call | flops 4000000000 | bytes 2000000 | tf_op jit(solution)/shard_map/forward/pallas_call | solution.py:115
  53.0 0.0 copy-done.5
  53.0 0.0 collective-permute-done.6.refs_7_
  53.0 0.0 copy-start.7
  53.0 2.6 %collective-permute-start.7 = (bf16[1024,128]{1,0:T(8,128)(2,1)S(1)}, bf16[1024,128]{1,0:T(8,128)(2,1)S(1)}, u32[]{:S(2)}, u32[]{:S(2)}) collective-permute-start(bf16[1024,128]{1,0:T(8,128)(2,1)S(1)} %collective-permute-done.6.refs_7_), channel_id=1, source_target_pairs={{0,1},{1,2},{2,3},{3,4},{4,5},{5,6},{6,7},{7,0},{8,15},{9,8},{10,9... | collective-permute-start | bytes 786440 | tf_op jit(solution)/shard_map/ppermute | solution.py:322
  55.6 5.6 %forward.7 = (bf16[128,1024]{1,0:T(8,128)(2,1)}, f32[8,1536,256]{2,1,0:T(8,128)}) custom-call(s32[8,12]{1,0:T(8,128)} %subtract_clamp_fusion.places, s32[8]{0:T(128)} %dynamic_slice.7.active, bf16[1024,128]{1,0:T(8,128)(2,1)} %q_ref.11, bf16[24,128,128]{2,1,0:T(8,128)(2,1)} %get-tuple-element.44.rest_0_, ...), custom_call_target="tpu_custom_call", output_to_operand_aliasing={{0}: (5, {}), {1}: (6, {})} | custom-call | flops 4000000000 | bytes 2000000 | tf_op jit(solution)/shard_map/forward/pallas_call | solution.py:115
  61.2 0.0 copy-done.6
  61.2 0.0 collective-permute-done.7.refs_4_
  61.2 0.0 copy-start.8
  61.2 3.1 %collective-permute-start.8 = (bf16[1024,128]{1,0:T(8,128)(2,1)S(1)}, bf16[1024,128]{1,0:T(8,128)(2,1)S(1)}, u32[]{:S(2)}, u32[]{:S(2)}) collective-permute-start(bf16[1024,128]{1,0:T(8,128)(2,1)S(1)} %collective-permute-done.7.refs_4_), channel_id=1, source_target_pairs={{0,1},{1,2},{2,3},{3,4},{4,5},{5,6},{6,7},{7,0},{8,15},{9,8},{10,9... | collective-permute-start | bytes 786440 | tf_op jit(solution)/shard_map/ppermute | solution.py:322
  64.3 0.5 and_select_fusion.order
  64.8 0.0 copy-done.3
  64.8 0.0 copy-done.4
  64.8 0.0 copy-done.7
  64.8 3.2 %project.2 = (f32[1024,128]{1,0:T(8,128)}, bf16[8,128,128]{2,1,0:T(8,128)(2,1)}) custom-call(s32[8]{0:T(128)} %and_select_fusion.order, bf16[128,1024]{1,0:T(8,128)(2,1)} %refs_0_.3, bf16[128,1024]{1,0:T(8,128)(2,1)} %get-tuple-element.57.refs_1_.att_ref, bf16[1024,128]{1,0:T(8,128)(2,1)} %refs_2_.1, bf16[1024,128]{1,0:T(8,128)(2,1)} %copy-done.3, ...), custom_call_target="tpu_custom_call" | custom-call | flops 2000000000 | bytes 1000000 | tf_op jit(solution)/shard_map/project/pallas_call | solution.py:289
  68.0 0.3 collective-permute-done.8.refs_5_
  68.3 0.0 copy-start.9
  68.3 0.0 copy-done.8
  68.3 0.7 copy-done.9
  69.0 2.6 %project.3 = (bf16[1024,128]{1,0:T(8,128)(2,1)}, bf16[8,128,128]{2,1,0:T(8,128)(2,1)}) custom-call(s32[8]{0:T(128)} %and_select_fusion.order, bf16[128,1024]{1,0:T(8,128)(2,1)} %refs_0_.3, bf16[128,1024]{1,0:T(8,128)(2,1)} %get-tuple-element.57.refs_1_.att_ref, f32[1024,128]{1,0:T(8,128)} %get-tuple-element.61.refs_2_, ...), custom_call_target="tpu_custom_call" | custom-call | flops 2000000000 | bytes 1000000 | tf_op jit(solution)/shard_map/project/pallas_call | solution.py:289
  71.6 17.3 %all-to-all-start = ((bf16[64,16,128]{2,1,0:T(8,128)(2,1)}), bf16[64,16,128]{2,1,0:T(8,128)(2,1)S(1)}, u32[]{:S(2)}, u32[]{:S(2)}) async-start(bf16[64,16,128]{2,1,0:T(8,128)(2,1)} %bitcast.3), calls=%async_computation | async-start | bytes 524288 | tf_op jit(solution)/shard_map/all_to_all | solution.py:328
  89.0 10.2 %backward.2 = (bf16[1024,128]{1,0:T(8,128)(2,1)}, f32[24,128,128]{2,1,0:T(8,128)}, f32[24,128,128]{2,1,0:T(8,128)}) custom-call(s32[8,12]{1,0:T(8,128)} %subtract_clamp_fusion.places, s32[8]{0:T(128)} %dynamic_slice.7.active, bf16[1024,128]{1,0:T(8,128)(2,1)} %q_ref.11, bf16[1024,128]{1,0:T(8,128)(2,1)} %get-tuple-element.64.ga_ref, ...), custom_call_target="tpu_custom_call" | custom-call | flops 16000000000 | bytes 8000000 | tf_op jit(solution)/shard_map/backward/pallas_call | solution.py:236
  99.2 1.8 %all-to-all-done = bf16[64,16,128]{2,1,0:T(8,128)(2,1)S(1)} async-done(((bf16[64,16,128]{2,1,0:T(8,128)(2,1)}), bf16[64,16,128]{2,1,0:T(8,128)(2,1)S(1)}, u32[]{:S(2)}, u32[]{:S(2)}) %all-to-all-start) | async-done | bytes 262176 | tf_op jit(solution)/shard_map/all_to_all | solution.py:328
  101.0 0.1 convert_reduce_fusion
  101.1 12.9 %backward.3 = (bf16[1024,128]{1,0:T(8,128)(2,1)}, f32[1024,256]{1,0:T(8,128)}, bf16[1024,256]{1,0:T(8,128)(2,1)}, bf16[1024,256]{1,0:T(8,128)(2,1)}) custom-call(s32[8,12]{1,0:T(8,128)} %subtract_clamp_fusion.places, s32[8]{0:T(128)} %dynamic_slice.7.active, bf16[1024,128]{1,0:T(8,128)(2,1)} %q_ref.11, ...), custom_call_target="tpu_custom_call", output_to_operand_aliasing={{0}: (8, {})} | custom-call | flops 16000000000 | bytes 8000000 | tf_op jit(solution)/shard_map/backward/pallas_call | solution.py:236
  114.0 1.9 %collective-permute-start.9 = (bf16[1024,256]{1,0:T(8,128)(2,1)}, bf16[1024,256]{1,0:T(8,128)(2,1)S(1)}, u32[]{:S(2)}, u32[]{:S(2)}) collective-permute-start(bf16[1024,256]{1,0:T(8,128)(2,1)} %get-tuple-element.77), channel_id=1, source_target_pairs={{0,504},{8,0},{16,8},{24,16},{32,24},{40,32},{48,40},{56,48},{64,5... | collective-permute-start | bytes 1572872 | tf_op jit(solution)/shard_map/ppermute | solution.py:255
  115.9 3.6 %collective-permute-start.10 = (bf16[1024,256]{1,0:T(8,128)(2,1)}, bf16[1024,256]{1,0:T(8,128)(2,1)S(1)}, u32[]{:S(2)}, u32[]{:S(2)}) collective-permute-start(bf16[1024,256]{1,0:T(8,128)(2,1)} %get-tuple-element.78), channel_id=1, source_target_pairs={{0,8},{8,16},{16,24},{24,32},{32,40},{40,48},{48,56},{56,64},{64,7... | collective-permute-start | bytes 1572872 | tf_op jit(solution)/shard_map/ppermute | solution.py:255
  119.6 19.9 %all_to_all.10 = bf16[64,16,128]{2,1,0:T(8,128)(2,1)} all-to-all(bf16[64,16,128]{2,1,0:T(8,128)(2,1)S(1)} %broadcast_in_dim.2), channel_id=1, replica_groups=mesh['ctx'=64,'head'=8] {'ctx'}, dimensions={0} | all-to-all | bytes 524288 | tf_op jit(solution)/shard_map/all_to_all | solution.py:379
  139.5 1.8 %place.1 = f32[128,1024]{1,0:T(8,128)} custom-call(bf16[8,128,128]{2,1,0:T(8,128)(2,1)} %bitcast.2), custom_call_target="tpu_custom_call" | custom-call | tf_op jit(solution)/shard_map/place/pallas_call | solution.py:309
  141.3 0.0 collective-permute-done.9
  141.3 0.0 collective-permute-done.10
  141.3 1.4 add_convert_fusion
  142.7 0.8 fusion.1
  (2 shorter events, 0.0 us)
Async XLA Ops:
  0.6 19.5 %copy-start = (s32[512,12]{0,1:T(8,128)S(1)}, s32[512,12]{0,1:T(8,128)}, u32[]{:S(2)}) copy-start(s32[512,12]{0,1:T(8,128)} %param.12) | copy-start | bytes 73732
  0.6 14.6 %collective-permute-start = (bf16[1024,128]{1,0:T(8,128)(2,1)}, bf16[1024,128]{1,0:T(8,128)(2,1)S(1)}, u32[]{:S(2)}, u32[]{:S(2)}) collective-permute-start(bf16[1024,128]{1,0:T(8,128)(2,1)} %refs_2_.1), channel_id=1, source_target_pairs={{0,1},{1,2},{2,3},{3,4},{4,5},{5,6},{6,7},{7,0},{8,15},{9,8},{10,9... | collective-permute-start | bytes 786440 | tf_op jit(solution)/shard_map/ppermute | solution.py:322
  8.6 19.9 %collective-permute-start.4 = (bf16[1024,256]{1,0:T(8,128)(2,1)S(1)}, bf16[1024,256]{1,0:T(8,128)(2,1)S(1)}, u32[]{:S(2)}, u32[]{:S(2)}) collective-permute-start(bf16[1024,256]{1,0:T(8,128)(2,1)S(1)} %constant_dynamic-update-slice_fusion), channel_id=1, source_target_pairs={{0,504},{8,0},{16,8},{24,16},{32,24},{40,32},{48,40},{56,48},{64,5... | collective-permute-start | bytes 1572872 | tf_op jit(solution)/shard_map/ppermute | solution.py:255
  13.3 15.2 %collective-permute-start.3 = (bf16[1024,256]{1,0:T(8,128)(2,1)S(1)}, bf16[1024,256]{1,0:T(8,128)(2,1)S(1)}, u32[]{:S(2)}, u32[]{:S(2)}) collective-permute-start(bf16[1024,256]{1,0:T(8,128)(2,1)S(1)} %constant_dynamic-update-slice_fusion), channel_id=1, source_target_pairs={{0,8},{8,16},{16,24},{24,32},{32,40},{40,48},{48,56},{56,64},{64,7... | collective-permute-start | bytes 1572872 | tf_op jit(solution)/shard_map/ppermute | solution.py:255
  15.3 49.5 %copy-start.3 = (bf16[1024,128]{1,0:T(8,128)(2,1)}, bf16[1024,128]{1,0:T(8,128)(2,1)S(1)}, u32[]{:S(2)}) copy-start(bf16[1024,128]{1,0:T(8,128)(2,1)S(1)} %collective-permute-done.refs_3_) | copy-start | bytes 786436
  15.3 8.2 %collective-permute-start.1 = (bf16[1024,128]{1,0:T(8,128)(2,1)S(1)}, bf16[1024,128]{1,0:T(8,128)(2,1)S(1)}, u32[]{:S(2)}, u32[]{:S(2)}) collective-permute-start(bf16[1024,128]{1,0:T(8,128)(2,1)S(1)} %collective-permute-done.refs_3_), channel_id=1, source_target_pairs={{0,1},{1,2},{2,3},{3,4},{4,5},{5,6},{6,7},{7,0},{8,15},{9,8},{10,9... | collective-permute-start | bytes 786440 | tf_op jit(solution)/shard_map/ppermute | solution.py:322
  23.5 41.4 %copy-start.4 = (bf16[1024,128]{1,0:T(8,128)(2,1)}, bf16[1024,128]{1,0:T(8,128)(2,1)S(1)}, u32[]{:S(2)}) copy-start(bf16[1024,128]{1,0:T(8,128)(2,1)S(1)} %collective-permute-done.1.refs_4_) | copy-start | bytes 786436
  23.5 13.4 %collective-permute-start.2 = (bf16[1024,128]{1,0:T(8,128)(2,1)S(1)}, bf16[1024,128]{1,0:T(8,128)(2,1)S(1)}, u32[]{:S(2)}, u32[]{:S(2)}) collective-permute-start(bf16[1024,128]{1,0:T(8,128)(2,1)S(1)} %collective-permute-done.1.refs_4_), channel_id=1, source_target_pairs={{0,1},{1,2},{2,3},{3,4},{4,5},{5,6},{6,7},{7,0},{8,15},{9,8},{10,9... | collective-permute-start | bytes 786440 | tf_op jit(solution)/shard_map/ppermute | solution.py:322
  28.5 0.8 copy-start.1
  29.3 0.8 copy-start.2
  36.8 16.2 %copy-start.5 = (bf16[1024,128]{1,0:T(8,128)(2,1)}, bf16[1024,128]{1,0:T(8,128)(2,1)S(1)}, u32[]{:S(2)}) copy-start(bf16[1024,128]{1,0:T(8,128)(2,1)S(1)} %collective-permute-done.2.refs_5_) | copy-start | bytes 786436
  36.9 7.1 %collective-permute-start.5 = (bf16[1024,128]{1,0:T(8,128)(2,1)S(1)}, bf16[1024,128]{1,0:T(8,128)(2,1)S(1)}, u32[]{:S(2)}, u32[]{:S(2)}) collective-permute-start(bf16[1024,128]{1,0:T(8,128)(2,1)S(1)} %collective-permute-done.2.refs_5_), channel_id=1, source_target_pairs={{0,1},{1,2},{2,3},{3,4},{4,5},{5,6},{6,7},{7,0},{8,15},{9,8},{10,9... | collective-permute-start | bytes 786440 | tf_op jit(solution)/shard_map/ppermute | solution.py:322
  44.0 17.2 %copy-start.6 = (bf16[1024,128]{1,0:T(8,128)(2,1)}, bf16[1024,128]{1,0:T(8,128)(2,1)S(1)}, u32[]{:S(2)}) copy-start(bf16[1024,128]{1,0:T(8,128)(2,1)S(1)} %collective-permute-done.5.refs_6_) | copy-start | bytes 786436
  44.0 9.1 %collective-permute-start.6 = (bf16[1024,128]{1,0:T(8,128)(2,1)S(1)}, bf16[1024,128]{1,0:T(8,128)(2,1)S(1)}, u32[]{:S(2)}, u32[]{:S(2)}) collective-permute-start(bf16[1024,128]{1,0:T(8,128)(2,1)S(1)} %collective-permute-done.5.refs_6_), channel_id=1, source_target_pairs={{0,1},{1,2},{2,3},{3,4},{4,5},{5,6},{6,7},{7,0},{8,15},{9,8},{10,9... | collective-permute-start | bytes 786440 | tf_op jit(solution)/shard_map/ppermute | solution.py:322
  53.0 11.8 %copy-start.7 = (bf16[1024,128]{1,0:T(8,128)(2,1)}, bf16[1024,128]{1,0:T(8,128)(2,1)S(1)}, u32[]{:S(2)}) copy-start(bf16[1024,128]{1,0:T(8,128)(2,1)S(1)} %collective-permute-done.6.refs_7_) | copy-start | bytes 786436
  53.0 8.1 %collective-permute-start.7 = (bf16[1024,128]{1,0:T(8,128)(2,1)S(1)}, bf16[1024,128]{1,0:T(8,128)(2,1)S(1)}, u32[]{:S(2)}, u32[]{:S(2)}) collective-permute-start(bf16[1024,128]{1,0:T(8,128)(2,1)S(1)} %collective-permute-done.6.refs_7_), channel_id=1, source_target_pairs={{0,1},{1,2},{2,3},{3,4},{4,5},{5,6},{6,7},{7,0},{8,15},{9,8},{10,9... | collective-permute-start | bytes 786440 | tf_op jit(solution)/shard_map/ppermute | solution.py:322
  61.2 7.1 %copy-start.8 = (bf16[1024,128]{1,0:T(8,128)(2,1)}, bf16[1024,128]{1,0:T(8,128)(2,1)S(1)}, u32[]{:S(2)}) copy-start(bf16[1024,128]{1,0:T(8,128)(2,1)S(1)} %collective-permute-done.7.refs_4_) | copy-start | bytes 786436
  61.2 7.1 %collective-permute-start.8 = (bf16[1024,128]{1,0:T(8,128)(2,1)S(1)}, bf16[1024,128]{1,0:T(8,128)(2,1)S(1)}, u32[]{:S(2)}, u32[]{:S(2)}) collective-permute-start(bf16[1024,128]{1,0:T(8,128)(2,1)S(1)} %collective-permute-done.7.refs_4_), channel_id=1, source_target_pairs={{0,1},{1,2},{2,3},{3,4},{4,5},{5,6},{6,7},{7,0},{8,15},{9,8},{10,9... | collective-permute-start | bytes 786440 | tf_op jit(solution)/shard_map/ppermute | solution.py:322
  68.3 0.7 copy-start.9
  71.6 29.4 %all-to-all-start = ((bf16[64,16,128]{2,1,0:T(8,128)(2,1)}), bf16[64,16,128]{2,1,0:T(8,128)(2,1)S(1)}, u32[]{:S(2)}, u32[]{:S(2)}) async-start(bf16[64,16,128]{2,1,0:T(8,128)(2,1)} %bitcast.3), calls=%async_computation | async-start | bytes 524288 | tf_op jit(solution)/shard_map/all_to_all | solution.py:328
  114.0 27.3 %collective-permute-start.9 = (bf16[1024,256]{1,0:T(8,128)(2,1)}, bf16[1024,256]{1,0:T(8,128)(2,1)S(1)}, u32[]{:S(2)}, u32[]{:S(2)}) collective-permute-start(bf16[1024,256]{1,0:T(8,128)(2,1)} %get-tuple-element.77), channel_id=1, source_target_pairs={{0,504},{8,0},{16,8},{24,16},{32,24},{40,32},{48,40},{56,48},{64,5... | collective-permute-start | bytes 1572872 | tf_op jit(solution)/shard_map/ppermute | solution.py:255
  115.9 25.4 %collective-permute-start.10 = (bf16[1024,256]{1,0:T(8,128)(2,1)}, bf16[1024,256]{1,0:T(8,128)(2,1)S(1)}, u32[]{:S(2)}, u32[]{:S(2)}) collective-permute-start(bf16[1024,256]{1,0:T(8,128)(2,1)} %get-tuple-element.78), channel_id=1, source_target_pairs={{0,8},{8,16},{16,24},{24,32},{32,40},{40,48},{48,56},{56,64},{64,7... | collective-permute-start | bytes 1572872 | tf_op jit(solution)/shard_map/ppermute | solution.py:255

commit v4 on v1

--- a/solution.py
+++ b/solution.py
@@ -1,3 +1,5 @@
+import functools
+
 import jax
 import jax.numpy as jnp
 from jax import lax
@@ -5,16 +7,21 @@
 from jax.experimental.pallas import tpu as pltpu
 from jax.sharding import PartitionSpec as P
 
+
 HD = 64
 BS = 128
-SIZES = (4, 6, 8, 10, 12)
+SIZES = (2, 4, 6, 8, 10, 12)
 
 
 def by_size(active, run):
-    low = 0
+    low = -1
     for size in SIZES:
         pl.when((active > low) & (active <= size))(lambda size=size: run(size))
         low = size
+
+
+def cost(steps):
+    return pl.CostEstimate(flops=2 * steps * 10**9, bytes_accessed=steps * 10**6, transcendentals=0)
 
 
 def spread_columns(rows_t):
@@ -44,7 +51,6 @@
     places, active, q_ref, mid_k, mid_v, left, right, att_ref, p_ref, kt_ref, v_ref, k_scr, vt_scr, s_scr
 ):
     step = pl.program_id(0)
-    blocks = pl.num_programs(0)
     factor = HD ** (-0.5)
 
     @pl.when(step == 0)
@@ -83,10 +89,11 @@
             total = part if total is None else total + part
         inverse = 1.0 / jnp.sum(total, axis=0, keepdims=True)
         attended = None
-        for s in range(size):
-            weights = s_scr[pl.ds(s * BS, BS), :] * inverse
-            p_ref[0, pl.ds(s * BS, BS), :] = weights
-            term = dot(vt_scr[places[step, s]], weights.astype(jnp.bfloat16))
+        for s in range(0, size, 2):
+            weights = s_scr[pl.ds(s * BS, 2 * BS), :] * inverse
+            p_ref[0, pl.ds(s * BS, 2 * BS), :] = weights
+            pair = jnp.concatenate([vt_scr[places[step, s]], vt_scr[places[step, s + 1]]], axis=1)
+            term = dot(pair, weights.astype(jnp.bfloat16))
             attended = term if attended is None else attended + term
         att_ref[...] = own_heads(attended).astype(jnp.bfloat16)
 
@@ -130,14 +137,19 @@
             window,
         ],
         compiler_params=pltpu.CompilerParams(dimension_semantics=("arbitrary",)),
+        cost_estimate=cost(blocks),
         name="forward",
     )(places, active, query_rows, key_rows, value_rows, left, right)
 
 
-def backward_kernel(
-    places, active, q_ref, ga_ref, att_ref, p_ref, kt_ref, v_ref, dq_ref, mid_ref, left_ref, right_ref, dk, dv
-):
+def backward_kernel(own, places, active, halo, q_ref, ga_ref, att_ref, p_ref, kt_ref, v_ref, *rest):
+    if own:
+        base_ref, dq_ref, dk, dv = rest
+    else:
+        dq_ref, left_ref, right_ref, dk, dv = rest
     step = pl.program_id(0)
+    slots = p_ref.shape[1] // BS
+    blocks = v_ref.shape[0] // 3
     factor = HD ** (-0.5)
 
     @pl.when(step == 0)
@@ -158,67 +170,94 @@
     grad_wide = spread_columns(grad_t)
     grad_tall = spread_rows(grad)
     query_tall = spread_rows(q_ref[...] * factor)
+    begin = halo[step] if own else 0
+    used = active[step] - halo[step] if own else halo[step]
 
     def run(size):
         total = None
-        for s in range(size):
-            place = places[step, s]
-            weights = p_ref[0, pl.ds(s * BS, BS), :]
-            change = weights * (dot(v_ref[place], grad_wide) - dots)
-            change = change.astype(jnp.bfloat16)
-            term = dot(kt_ref[place], change)
+        for s in range(0, size, 2):
+            changes, pair = [], []
+            for j in range(2):
+                slot = begin + s + j
+                final = s + j == size - 1
+                if final:
+                    slot = jnp.minimum(slot, slots - 1)
+                place = places[step, slot]
+                rows = pl.ds(pl.multiple_of(slot * BS, BS), BS)
+                weights = p_ref[0, rows, :]
+                if final:
+                    weights = jnp.where(s + j < used, weights, 0.0)
+                change = weights * (dot(v_ref[place], grad_wide) - dots)
+                change = change.astype(jnp.bfloat16)
+                changes.append(change)
+                pair.append(kt_ref[place])
+                at = place - blocks if own else jnp.where(place < blocks, place, place - blocks)
+                at = jnp.clip(at, 0, dk.shape[0] - 1)
+                dk[at] += dot(change, query_tall)
+                dv[at] += dot(weights.astype(jnp.bfloat16), grad_tall)
+            term = dot(jnp.concatenate(pair, axis=1), jnp.concatenate(changes, axis=0))
             total = term if total is None else total + term
-            dk[place] += dot(change, query_tall)
-            dv[place] += dot(weights.astype(jnp.bfloat16), grad_tall)
-        dq_ref[...] = (own_heads(total) * factor).T.astype(jnp.bfloat16)
-
-    by_size(active[step], run)
-
-    @pl.when(step == pl.num_programs(0) - 1)
-    def _():
-        count = mid_ref.shape[0] // BS
-        for b in range(3 * count):
-            side, at = divmod(b, count)
-            target = (left_ref, mid_ref, right_ref)[side]
-            rows = pl.ds(at * BS, BS)
-            target[rows, :BS] = dk[b].astype(target.dtype)
-            target[rows, BS:] = dv[b].astype(target.dtype)
-
-
-def backward(places, active, query_rows, grad_attended, att_t, weights, keys_t, values):
-    blocks, slots = places.shape
+        total = own_heads(total)
+        if own:
+            dq_ref[...] = ((total + base_ref[...]) * factor).T.astype(jnp.bfloat16)
+        else:
+            dq_ref[...] = total
+
+    by_size(used, run)
+
+    if not own:
+
+        @pl.when(step == pl.num_programs(0) - 1)
+        def _():
+            for b in range(2 * blocks):
+                side, at = divmod(b, blocks)
+                target = (left_ref, right_ref)[side]
+                rows = pl.ds(at * BS, BS)
+                target[rows, :BS] = dk[b].astype(target.dtype)
+                target[rows, BS:] = dv[b].astype(target.dtype)
+
+
+def backward(tables, query_rows, grad_attended, att_t, weights, keys_t, values, base):
+    blocks, slots = tables[0].shape
     rows, cols = query_rows.shape
     extent = 3 * blocks
+    own = bool(base)
     whole = lambda *shape: pl.BlockSpec(shape, lambda i, *_: (0,) * len(shape))
     one = pl.BlockSpec((BS, cols), lambda i, *_: (i, 0))
+    one_t = pl.BlockSpec((cols, BS), lambda i, *_: (0, i))
+    in_specs = [
+        one,
+        one,
+        one_t,
+        pl.BlockSpec((1, slots * BS, 2 * BS), lambda i, *_: (i, 0, 0)),
+        whole(extent, BS, cols),
+        whole(extent, BS, cols),
+    ]
+    if own:
+        in_specs.append(one_t)
+        out_specs = [one] + [whole(blocks, BS, cols)] * 2
+        out_shape = [jax.ShapeDtypeStruct((rows, cols), jnp.bfloat16)]
+        out_shape += [jax.ShapeDtypeStruct((blocks, BS, cols), jnp.float32)] * 2
+        scratch = []
+    else:
+        out_specs = [one_t] + [whole(rows, 2 * cols)] * 2
+        out_shape = [jax.ShapeDtypeStruct((cols, rows), jnp.float32)]
+        out_shape += [jax.ShapeDtypeStruct((rows, 2 * cols), jnp.bfloat16)] * 2
+        scratch = [pltpu.VMEM((2 * blocks, BS, cols), jnp.float32)] * 2
     return pl.pallas_call(
-        backward_kernel,
+        functools.partial(backward_kernel, own),
         grid_spec=pltpu.PrefetchScalarGridSpec(
-            num_scalar_prefetch=2,
+            num_scalar_prefetch=3,
             grid=(blocks,),
-            in_specs=[
-                one,
-                one,
-                pl.BlockSpec((cols, BS), lambda i, *_: (0, i)),
-                pl.BlockSpec((1, slots * BS, 2 * BS), lambda i, *_: (i, 0, 0)),
-                whole(extent, BS, cols),
-                whole(extent, BS, cols),
-            ],
-            out_specs=[one, whole(rows, 2 * cols), whole(rows, 2 * cols), whole(rows, 2 * cols)],
-            scratch_shapes=[
-                pltpu.VMEM((extent, BS, cols), jnp.float32),
-                pltpu.VMEM((extent, BS, cols), jnp.float32),
-            ],
+            in_specs=in_specs,
+            out_specs=out_specs,
+            scratch_shapes=scratch,
         ),
-        out_shape=[
-            jax.ShapeDtypeStruct((rows, cols), jnp.bfloat16),
-            jax.ShapeDtypeStruct((rows, 2 * cols), jnp.float32),
-            jax.ShapeDtypeStruct((rows, 2 * cols), jnp.bfloat16),
-            jax.ShapeDtypeStruct((rows, 2 * cols), jnp.bfloat16),
-        ],
+        out_shape=out_shape,
         compiler_params=pltpu.CompilerParams(dimension_semantics=("arbitrary",)),
+        cost_estimate=cost(blocks),
         name="backward",
-    )(places, active, query_rows, grad_attended, att_t, weights, keys_t, values)
+    )(*tables, query_rows, grad_attended, att_t, weights, keys_t, values, *base)
 
 
 def shifted(x, axis, by):
@@ -226,36 +265,105 @@
     return lax.ppermute(x, axis, [(i, (i + by) % count) for i in range(count)])
 
 
+def project_kernel(g_ref, w_ref, att_ref, ga_ref, wg_ref):
+    count = g_ref.shape[0]
+    att = att_ref[...]
+    total = None
+    for k in range(0, count, 2):
+        part = jnp.concatenate([g_ref[k], g_ref[k + 1]], axis=1)
+        side = w_ref[:, k * BS : (k + 2) * BS]
+        term = lax.dot_general(
+            part, side, (((1,), (1,)), ((), ())), preferred_element_type=jnp.float32
+        )
+        total = term if total is None else total + term
+        grad = dot(att, part)
+        for j in range(2):
+            wg_ref[k + j] = grad[:, j * BS : (j + 1) * BS].astype(wg_ref.dtype)
+    ga_ref[...] = total.astype(jnp.bfloat16)
+
+
+def project(gathered, out_weight, att_t):
+    count, rows, width = gathered.shape
+    cols = out_weight.shape[0]
+    return pl.pallas_call(
+        project_kernel,
+        in_specs=[pl.BlockSpec(memory_space=pltpu.VMEM)] * 3,
+        out_shape=[
+            jax.ShapeDtypeStruct((rows, cols), jnp.bfloat16),
+            jax.ShapeDtypeStruct((count, cols, width), jnp.bfloat16),
+        ],
+        cost_estimate=cost(2),
+        name="project",
+    )(gathered, out_weight, att_t)
+
+
+def place_kernel(sum_ref, out_ref):
+    for k in range(sum_ref.shape[0]):
+        out_ref[:, k * BS : (k + 1) * BS] = sum_ref[k].astype(jnp.float32)
+
+
+def place(sums):
+    count, cols, width = sums.shape
+    return pl.pallas_call(
+        place_kernel,
+        out_shape=jax.ShapeDtypeStruct((cols, count * width), jnp.float32),
+        name="place",
+    )(sums)
+
+
+def gather_heads(rows):
+    copies = jnp.broadcast_to(rows[None], (lax.axis_size("head"),) + rows.shape)
+    return lax.all_to_all(copies, "head", 0, 0)
+
+
+def slot_tables(neighbours, counts, blocks):
+    first = lax.axis_index("ctx") * blocks
+    places = lax.dynamic_slice_in_dim(neighbours, first, blocks, axis=0)
+    places = jnp.clip(places - (first - blocks), 0, 3 * blocks - 1)
+    active = lax.dynamic_slice_in_dim(counts, first, blocks, axis=0)
+    slots = jnp.arange(places.shape[1], dtype=jnp.int32)
+    own = (places >= blocks) & (places < 2 * blocks)
+    kind = jnp.where(slots < active[:, None], own.astype(jnp.int32), 2)
+    key = kind * places.shape[1] + slots
+    rank = jnp.sum((key[:, :, None] > key[:, None, :]).astype(jnp.int32), axis=2)
+    chosen = rank[:, :, None] == slots
+    ordered = jnp.sum(jnp.where(chosen, places[:, :, None], 0), axis=1)
+    halo = jnp.sum((kind == 0).astype(jnp.int32), axis=1)
+    return ordered, active, halo
+
+
 def body(query_rows, key_rows, value_rows, out_grad, out_weight, neighbours, counts):
     row_count, col_count = query_rows.shape
     blocks = row_count // BS
-    extent = 3 * blocks
-    ctx_index = lax.axis_index("ctx")
+    node_count = row_count * lax.axis_size("ctx")
+    gathered = gather_heads(out_grad)
     packed = jnp.concatenate([key_rows, value_rows], axis=1)
     left = shifted(packed, "ctx", 1)
     right = shifted(packed, "ctx", -1)
-    first = ctx_index * blocks
-    places = lax.dynamic_slice_in_dim(neighbours, first, blocks, axis=0)
-    places = jnp.clip(places - (first - blocks), 0, extent - 1)
-    active = lax.dynamic_slice_in_dim(counts, first, blocks, axis=0)
+    tables = slot_tables(neighbours, counts, blocks)
     att_t, weights, keys_t, values = forward(
-        places, active, query_rows, key_rows, value_rows, left, right
-    )
-    gathered = lax.all_gather(out_grad, "head", axis=1, tiled=True)
-    grad_attended = jnp.einsum(
-        "ro,jo->rj", gathered, out_weight, preferred_element_type=jnp.float32
-    ).astype(jnp.bfloat16)
-    product = jnp.einsum("jr,ro->jo", att_t, gathered, preferred_element_type=jnp.float32)
-    node_count = row_count * lax.axis_size("ctx")
-    weight_grad = lax.psum(product, "ctx") * node_count ** (-0.5)
-    query_grad, middle, to_left, to_right = backward(
-        places, active, query_rows, grad_attended, att_t, weights, keys_t, values
-    )
+        *tables[:2], query_rows, key_rows, value_rows, left, right
+    )
+    grad_attended, partial = project(gathered, out_weight, att_t)
+    shared = (query_rows, grad_attended, att_t, weights, keys_t, values)
+    members = lax.axis_size("ctx")
+    pieces = partial.reshape(members, -1, partial.shape[-1])
+    pieces = lax.all_to_all(pieces, "ctx", 0, 0)
+    query_part, to_left, to_right = backward(tables, *shared, ())
     from_right = shifted(to_left, "ctx", -1)
     from_left = shifted(to_right, "ctx", 1)
-    combined = middle + from_right.astype(jnp.float32) + from_left.astype(jnp.float32)
-    key_grad = combined[:, :col_count].astype(jnp.bfloat16)
-    value_grad = combined[:, col_count:].astype(jnp.bfloat16)
+    piece = jnp.sum(pieces.astype(jnp.float32), axis=0) * node_count ** (-0.5)
+    copies = jnp.broadcast_to(piece.astype(partial.dtype)[None], pieces.shape)
+    weight_sum = lax.all_to_all(copies, "ctx", 0, 0)
+    query_grad, key_own, value_own = backward(tables, *shared, (query_part,))
+    weight_grad = place(weight_sum.reshape(partial.shape))
+    sides = [
+        own.reshape(row_count, col_count)
+        + from_right[:, at : at + col_count].astype(jnp.float32)
+        + from_left[:, at : at + col_count].astype(jnp.float32)
+        for own, at in ((key_own, 0), (value_own, col_count))
+    ]
+    key_grad, value_grad = [side.astype(jnp.bfloat16) for side in sides]
     return (query_grad, key_grad, value_grad, weight_grad)
 
 

time: 301 us -> 132 us (0.44)
  waiting for transfers between devices: 219 us -> 28.1 us
  starting transfers between devices: 22.7 us -> 44.2 us
  Pallas kernels: 30.9 us -> 46.8 us
  between operations: 14.1 us -> 0.76 us
  matrix products: 4.25 us -> 0 us
    psum x1 -> x0, waiting for transfers between devices: 195 us -> none  [body(): weight_grad = lax.psum(product, 'ctx') * node_count ** (-0.5)]
    all_to_all x0 -> x3, starting transfers between devices: none -> 33.1 us  [the longest x1 13.8 us: body(): pieces = lax.all_to_all(pieces, 'ctx', 0, 0)]
    all_to_all x0 -> x3, waiting for transfers between devices: none -> 22.4 us  [the longest x1 22.3 us: gather_heads(): return lax.all_to_all(copies, 'head', 0, 0)]
    all_gather x1 -> x0, waiting for transfers between devices: 19.4 us -> none  [body(): gathered = lax.all_gather(out_grad, 'head', axis=1, tiled=True)]
    pallas_call x1 -> x4, Pallas kernels: 17.7 us -> 33.4 us  [the longest x2 28.1 us: backward(): pl.pallas_call(functools.partial(backward_kernel, own), grid_spec=pltpu.P...]
    ppermute x4, starting transfers between devices: 22.6 us -> 11.1 us  [shifted(): return lax.ppermute(x, axis, [(i, (i + by) % count) for i in range(count)])]
    dot_general x2 -> x0, matrix products: 4.25 us -> none  [the longest x1 3.01 us: body(): jnp.einsum('ro,jo->rj', gathered, out_weight, preferred_element_type=jnp....]
    broadcast_in_dim x0 -> x2, local copies, waits for them, and re-layouts: none -> 3.27 us  [the longest x1 2.55 us: gather_heads(): copies = jnp.broadcast_to(rows[None], (lax.axis_size('head'),) + rows.shape)]
  transfers between devices with their start and end apart: 6 -> 7, of which waited for: 3 -> 3; matrix products, arithmetic and copies ran while one was open for 3% -> 5% of each run, Pallas kernels for 4% -> 32%
where the time goes in v4:
time: 132 us; the launch traced here: 131 us
  Pallas kernels  46.8 us (35%)
  starting transfers between devices  44.2 us (33%)
  waiting for transfers between devices  28.1 us (21%)
  local copies, waits for them, and re-layouts  6.26 us (5%)
  other arithmetic  4.61 us (3%)
    pallas_call x2, Pallas kernels, backward(): pl.pallas_call(functools.partial(backward_kernel, own), grid_spec=pltpu.P...  28.1 us
    all_to_all x1, waiting for transfers between devices, gather_heads(): return lax.all_to_all(copies, 'head', 0, 0)  22.3 us
    all_to_all x1, starting transfers between devices, body(): pieces = lax.all_to_all(pieces, 'ctx', 0, 0)  13.8 us
    pallas_call x1, Pallas kernels, forward(): pl.pallas_call(forward_kernel, grid_spec=pltpu.PrefetchScalarGridSpec(num...  13.4 us
    all_to_all x1, starting transfers between devices, body(): weight_sum = lax.all_to_all(copies, 'ctx', 0, 0)  11.5 us
    ppermute x4, starting transfers between devices, shifted(): return lax.ppermute(x, axis, [(i, (i + by) % count) for i in range(count)])  11.1 us
    all_to_all x1, starting transfers between devices, gather_heads(): return lax.all_to_all(copies, 'head', 0, 0)  7.77 us
    ppermute x4, waiting for transfers between devices, shifted(): return lax.ppermute(x, axis, [(i, (i + by) % count) for i in range(count)])  5.75 us
  transfers between devices with their start and end apart: 7, of which 3 were waited for; matrix products, arithmetic and copies ran while one was open for 5% of the time, Pallas kernels for 32%

profile of v4, /device:TPU:1, one launch (start us, length us, event | category | flops | bytes accessed | tf_op | source)
XLA Modules:
  0.0 130.8 jit_solution(3161221176392240811)
XLA Ops:
  0.6 2.6 %broadcast_in_dim.23 = bf16[8,1024,128]{2,1,0:T(8,128)(2,1)} broadcast(bf16[1024,128]{1,0:T(8,128)(2,1)} %param.10), dimensions={1,2} | broadcast | bytes 2359296 | tf_op jit(solution)/shard_map/broadcast_in_dim | solution.py:315
  3.2 0.0 copy-start.2
  3.2 0.0 copy-start.3
  3.2 7.8 %all-to-all-start = ((bf16[8,1024,128]{2,1,0:T(8,128)(2,1)}), bf16[8,1024,128]{2,1,0:T(8,128)(2,1)S(1)}, u32[]{:S(2)}, u32[]{:S(2)}) async-start(bf16[8,1024,128]{2,1,0:T(8,128)(2,1)} %broadcast_in_dim.23), calls=%async_computation | async-start | bytes 4194304 | tf_op jit(solution)/shard_map/all_to_all | solution.py:316
  11.0 0.0 copy-done.2
  11.0 0.0 copy-done.3
  11.0 0.1 constant_dynamic-update-slice_fusion
  11.1 4.8 %collective-permute-start = (bf16[1024,256]{1,0:T(8,128)(2,1)S(1)}, bf16[1024,256]{1,0:T(8,128)(2,1)}, u32[]{:S(2)}, u32[]{:S(2)}) collective-permute-start(bf16[1024,256]{1,0:T(8,128)(2,1)S(1)} %constant_dynamic-update-slice_fusion), channel_id=1, source_target_pairs={{0,8},{8,16},{16,24},{24,32},{32,40},{40,48},{48,56},{56,64},{64,7... | collective-permute-start | bytes 1572872 | tf_op jit(solution)/shard_map/ppermute | solution.py:265
  15.9 1.9 %collective-permute-start.1 = (bf16[1024,256]{1,0:T(8,128)(2,1)S(1)}, bf16[1024,256]{1,0:T(8,128)(2,1)}, u32[]{:S(2)}, u32[]{:S(2)}) collective-permute-start(bf16[1024,256]{1,0:T(8,128)(2,1)S(1)} %constant_dynamic-update-slice_fusion), channel_id=1, source_target_pairs={{0,504},{8,0},{16,8},{24,16},{32,24},{40,32},{48,40},{56,48},{64,5... | collective-permute-start | bytes 1572872 | tf_op jit(solution)/shard_map/ppermute | solution.py:265
  17.9 0.8 dynamic_slice.6.active
  18.6 0.0 copy-start.4
  18.6 1.3 %convert_reduce_fusion.2 = (s32[8]{0:T(128)}, pred[8,12]{0,1:T(8,128)(4,1)S(1)}, s32[8,12]{0,1:T(8,128)S(1)}) fusion(s32[8]{0:T(128)S(1)} %dynamic_slice.6.active, s32[]{:T(128)S(6)} %sub.9, s32[512,12]{0,1:T(8,128)} %param.12, s32[]{:T(128)S(6)} %select_n.12), kind=kLoop, calls=%fused_computation.11 | loop fusion | flops 1048 | bytes 936 | tf_op jit(solution)/shard_map/reduce_sum | solution.py:331
  20.0 0.1 copy.14
  20.1 0.3 convert_reduce_fusion.1
  20.4 0.7 select_reduce_fusion.places
  21.1 0.9 collective-permute-done.left
  22.1 4.8 %collective-permute-done.1.right = bf16[1024,256]{1,0:T(8,128)(2,1)} collective-permute-done((bf16[1024,256]{1,0:T(8,128)(2,1)S(1)}, bf16[1024,256]{1,0:T(8,128)(2,1)}, u32[]{:S(2)}, u32[]{:S(2)}) %collective-permute-start.1) | collective-permute-done | bytes 524320 | tf_op jit(solution)/shard_map/ppermute | solution.py:265
  26.9 0.0 copy-done.4
  26.9 13.4 %forward.1 = (bf16[128,1024]{1,0:T(8,128)(2,1)}, f32[8,1536,256]{2,1,0:T(8,128)}, bf16[24,128,128]{2,1,0:T(8,128)(2,1)}, bf16[24,128,128]{2,1,0:T(8,128)(2,1)}) custom-call(s32[8,12]{1,0:T(8,128)} %select_reduce_fusion.places, s32[8]{0:T(128)} %copy-done.4, bf16[1024,128]{1,0:T(8,128)(2,1)} %q_ref.5, bf16[1024,128]{1,0:T(8,128)(2,1)} %mid_k.1, ...), custom_call_target="tpu_custom_call" | custom-call | flops 16000000000 | bytes 8000000 | tf_op jit(solution)/shard_map/forward/pallas_call | solution.py:109
  40.3 22.3 %all-to-all-done.g_ref = bf16[8,1024,128]{2,1,0:T(8,128)(2,1)S(1)} async-done(((bf16[8,1024,128]{2,1,0:T(8,128)(2,1)}), bf16[8,1024,128]{2,1,0:T(8,128)(2,1)S(1)}, u32[]{:S(2)}, u32[]{:S(2)}) %all-to-all-start) | async-done | bytes 2097184 | tf_op jit(solution)/shard_map/all_to_all | solution.py:316
  62.6 0.0 copy-start
  62.6 1.3 %copy-done = bf16[8,1024,128]{2,1,0:T(8,128)(2,1)} copy-done((bf16[8,1024,128]{2,1,0:T(8,128)(2,1)}, bf16[8,1024,128]{2,1,0:T(8,128)(2,1)S(1)}, u32[]{:S(2)}) %copy-start) | copy-done | bytes 2097176
  64.0 3.5 %project.1 = (bf16[1024,128]{1,0:T(8,128)(2,1)}, bf16[8,128,128]{2,1,0:T(8,128)(2,1)}) custom-call(bf16[8,1024,128]{2,1,0:T(8,128)(2,1)} %copy-done, bf16[128,1024]{1,0:T(8,128)(2,1)} %w_ref.1, bf16[128,1024]{1,0:T(8,128)(2,1)} %get-tuple-element.16.att_ref), custom_call_target="tpu_custom_call" | custom-call | flops 4000000000 | bytes 2000000 | tf_op jit(solution)/shard_map/project/pallas_call | solution.py:288
  67.4 13.8 %all-to-all-start.1 = ((bf16[64,16,128]{2,1,0:T(8,128)(2,1)}), bf16[64,16,128]{2,1,0:T(8,128)(2,1)S(1)}, u32[]{:S(2)}, u32[]{:S(2)}) async-start(bf16[64,16,128]{2,1,0:T(8,128)(2,1)} %bitcast.15), calls=%async_computation.1 | async-start | bytes 524288 | tf_op jit(solution)/shard_map/all_to_all | solution.py:351
  81.3 14.5 %backward.2 = (f32[128,1024]{1,0:T(8,128)}, bf16[1024,256]{1,0:T(8,128)(2,1)}, bf16[1024,256]{1,0:T(8,128)(2,1)}) custom-call(s32[8,12]{1,0:T(8,128)} %select_reduce_fusion.places, s32[8]{0:T(128)} %copy-done.4, s32[8]{0:T(128)} %get-tuple-element.28.halo, bf16[1024,128]{1,0:T(8,128)(2,1)} %q_ref.5, bf16[1024,128]{1,0:T(8,128)(2,1)} %get-tuple-element.17.ga_ref, ...), custom_call_target="tpu_custom_call" | custom-call | flops 16000000000 | bytes 8000000 | tf_op jit(solution)/shard_map/backward/pallas_call | solution.py:247
  95.7 1.9 %collective-permute-start.3 = (bf16[1024,256]{1,0:T(8,128)(2,1)}, bf16[1024,256]{1,0:T(8,128)(2,1)S(1)}, u32[]{:S(2)}, u32[]{:S(2)}) collective-permute-start(bf16[1024,256]{1,0:T(8,128)(2,1)} %get-tuple-element.25), channel_id=1, source_target_pairs={{0,8},{8,16},{16,24},{24,32},{32,40},{40,48},{48,56},{56,64},{64,7... | collective-permute-start | bytes 1572872 | tf_op jit(solution)/shard_map/ppermute | solution.py:265
  97.7 2.4 %collective-permute-start.2 = (bf16[1024,256]{1,0:T(8,128)(2,1)}, bf16[1024,256]{1,0:T(8,128)(2,1)S(1)}, u32[]{:S(2)}, u32[]{:S(2)}) collective-permute-start(bf16[1024,256]{1,0:T(8,128)(2,1)} %get-tuple-element.24), channel_id=1, source_target_pairs={{0,504},{8,0},{16,8},{24,16},{32,24},{40,32},{48,40},{56,48},{64,5... | collective-permute-start | bytes 1572872 | tf_op jit(solution)/shard_map/ppermute | solution.py:265
  100.1 0.0 all-to-all-done.1
  100.1 0.1 convert_reduce_fusion
  100.2 0.7 broadcast_in_dim.24
  100.9 11.5 %all-to-all-start.2 = ((bf16[64,16,128]{2,1,0:T(8,128)(2,1)}), bf16[64,16,128]{2,1,0:T(8,128)(2,1)S(1)}, u32[]{:S(2)}, u32[]{:S(2)}) async-start(bf16[64,16,128]{2,1,0:T(8,128)(2,1)} %broadcast_in_dim.24), calls=%async_computation.2 | async-start | bytes 524288 | tf_op jit(solution)/shard_map/all_to_all | solution.py:357
  112.4 13.7 %backward.3 = (bf16[1024,128]{1,0:T(8,128)(2,1)}, f32[8,128,128]{2,1,0:T(8,128)}, f32[8,128,128]{2,1,0:T(8,128)}) custom-call(s32[8,12]{1,0:T(8,128)} %select_reduce_fusion.places, s32[8]{0:T(128)} %copy-done.4, s32[8]{0:T(128)} %get-tuple-element.28.halo, bf16[1024,128]{1,0:T(8,128)(2,1)} %q_ref.5, bf16[1024,128]{1,0:T(8,128)(2,1)} %get-tuple-element.17.ga_ref, ...), custom_call_target="tpu_custom_call" | custom-call | flops 16000000000 | bytes 8000000 | tf_op jit(solution)/shard_map/backward/pallas_call | solution.py:247
  126.1 0.0 collective-permute-done.3
  126.1 0.0 collective-permute-done.2
  126.1 2.2 %fusion.1 = (bf16[1024,128]{1,0:T(8,128)(2,1)}, bf16[1024,128]{1,0:T(8,128)(2,1)}) fusion(f32[8,128,128]{2,1,0:T(8,128)} %get-tuple-element.26, bf16[1024,256]{1,0:T(8,128)(2,1)S(1)} %collective-permute-done.3, bf16[1024,256]{1,0:T(8,128)(2,1)S(1)} %collective-permute-done.2, f32[8,128,128]{2,1,0:T(8,128)} %get-tuple-element.23), kind=kLoop, calls=%fused_computation.2 | loop fusion | flops 1310720 | bytes 2621440 | tf_op jit(solution)/shard_map/convert_element_type | solution.py:366
  128.3 0.0 all-to-all-done.2
  128.3 0.0 copy-start.1
  128.3 0.7 copy-done.1
  129.0 1.8 %place.1 = f32[128,1024]{1,0:T(8,128)} custom-call(bf16[8,128,128]{2,1,0:T(8,128)(2,1)} %bitcast.14), custom_call_target="tpu_custom_call" | custom-call | tf_op jit(solution)/shard_map/place/pallas_call | solution.py:307
  (3 shorter events, 0.1 us)
Async XLA Ops:
  3.2 7.8 %copy-start.2 = (bf16[1024,128]{1,0:T(8,128)(2,1)S(1)}, bf16[1024,128]{1,0:T(8,128)(2,1)}, u32[]{:S(2)}) copy-start(bf16[1024,128]{1,0:T(8,128)(2,1)} %mid_k.1) | copy-start | bytes 786436
  3.2 7.8 %copy-start.3 = (bf16[1024,128]{1,0:T(8,128)(2,1)S(1)}, bf16[1024,128]{1,0:T(8,128)(2,1)}, u32[]{:S(2)}) copy-start(bf16[1024,128]{1,0:T(8,128)(2,1)} %mid_v.1) | copy-start | bytes 786436
  3.2 59.4 %all-to-all-start = ((bf16[8,1024,128]{2,1,0:T(8,128)(2,1)}), bf16[8,1024,128]{2,1,0:T(8,128)(2,1)S(1)}, u32[]{:S(2)}, u32[]{:S(2)}) async-start(bf16[8,1024,128]{2,1,0:T(8,128)(2,1)} %broadcast_in_dim.23), calls=%async_computation | async-start | bytes 4194304 | tf_op jit(solution)/shard_map/all_to_all | solution.py:316
  11.1 11.0 %collective-permute-start = (bf16[1024,256]{1,0:T(8,128)(2,1)S(1)}, bf16[1024,256]{1,0:T(8,128)(2,1)}, u32[]{:S(2)}, u32[]{:S(2)}) collective-permute-start(bf16[1024,256]{1,0:T(8,128)(2,1)S(1)} %constant_dynamic-update-slice_fusion), channel_id=1, source_target_pairs={{0,8},{8,16},{16,24},{24,32},{32,40},{40,48},{48,56},{56,64},{64,7... | collective-permute-start | bytes 1572872 | tf_op jit(solution)/shard_map/ppermute | solution.py:265
  15.9 10.9 %collective-permute-start.1 = (bf16[1024,256]{1,0:T(8,128)(2,1)S(1)}, bf16[1024,256]{1,0:T(8,128)(2,1)}, u32[]{:S(2)}, u32[]{:S(2)}) collective-permute-start(bf16[1024,256]{1,0:T(8,128)(2,1)S(1)} %constant_dynamic-update-slice_fusion), channel_id=1, source_target_pairs={{0,504},{8,0},{16,8},{24,16},{32,24},{40,32},{48,40},{56,48},{64,5... | collective-permute-start | bytes 1572872 | tf_op jit(solution)/shard_map/ppermute | solution.py:265
  18.6 8.2 %copy-start.4 = (s32[8]{0:T(128)}, s32[8]{0:T(128)S(1)}, u32[]{:S(2)}) copy-start(s32[8]{0:T(128)S(1)} %dynamic_slice.6.active) | copy-start | bytes 100
  62.6 1.3 %copy-start = (bf16[8,1024,128]{2,1,0:T(8,128)(2,1)}, bf16[8,1024,128]{2,1,0:T(8,128)(2,1)S(1)}, u32[]{:S(2)}) copy-start(bf16[8,1024,128]{2,1,0:T(8,128)(2,1)S(1)} %all-to-all-done.g_ref) | copy-start | bytes 6291460
  67.4 32.7 %all-to-all-start.1 = ((bf16[64,16,128]{2,1,0:T(8,128)(2,1)}), bf16[64,16,128]{2,1,0:T(8,128)(2,1)S(1)}, u32[]{:S(2)}, u32[]{:S(2)}) async-start(bf16[64,16,128]{2,1,0:T(8,128)(2,1)} %bitcast.15), calls=%async_computation.1 | async-start | bytes 524288 | tf_op jit(solution)/shard_map/all_to_all | solution.py:351
  95.7 30.3 %collective-permute-start.3 = (bf16[1024,256]{1,0:T(8,128)(2,1)}, bf16[1024,256]{1,0:T(8,128)(2,1)S(1)}, u32[]{:S(2)}, u32[]{:S(2)}) collective-permute-start(bf16[1024,256]{1,0:T(8,128)(2,1)} %get-tuple-element.25), channel_id=1, source_target_pairs={{0,8},{8,16},{16,24},{24,32},{32,40},{40,48},{48,56},{56,64},{64,7... | collective-permute-start | bytes 1572872 | tf_op jit(solution)/shard_map/ppermute | solution.py:265
  97.7 28.4 %collective-permute-start.2 = (bf16[1024,256]{1,0:T(8,128)(2,1)}, bf16[1024,256]{1,0:T(8,128)(2,1)S(1)}, u32[]{:S(2)}, u32[]{:S(2)}) collective-permute-start(bf16[1024,256]{1,0:T(8,128)(2,1)} %get-tuple-element.24), channel_id=1, source_target_pairs={{0,504},{8,0},{16,8},{24,16},{32,24},{40,32},{48,40},{56,48},{64,5... | collective-permute-start | bytes 1572872 | tf_op jit(solution)/shard_map/ppermute | solution.py:265
  100.9 27.4 %all-to-all-start.2 = ((bf16[64,16,128]{2,1,0:T(8,128)(2,1)}), bf16[64,16,128]{2,1,0:T(8,128)(2,1)S(1)}, u32[]{:S(2)}, u32[]{:S(2)}) async-start(bf16[64,16,128]{2,1,0:T(8,128)(2,1)} %broadcast_in_dim.24), calls=%async_computation.2 | async-start | bytes 524288 | tf_op jit(solution)/shard_map/all_to_all | solution.py:357
  128.3 0.7 copy-start.1

commit v5 on v4

--- a/solution.py
+++ b/solution.py
@@ -48,10 +48,9 @@
 
 
 def forward_kernel(
-    places, active, q_ref, mid_k, mid_v, left, right, att_ref, p_ref, kt_ref, v_ref, k_scr, vt_scr, s_scr
+    places, active, q_ref, mid_k, mid_v, left, right, att_ref, stat_ref, kt_ref, k_scr, vt_scr, s_scr
 ):
     step = pl.program_id(0)
-    factor = HD ** (-0.5)
 
     @pl.when(step == 0)
     def _():
@@ -66,10 +65,9 @@
                 k, v = source[rows, :BS], source[rows, BS:]
             k_scr[b] = k
             kt_ref[b] = k.T
-            v_ref[b] = v
             vt_scr[b] = v.T
 
-    query = spread_columns(q_ref[...].T * factor)
+    query = spread_columns(q_ref[...].T * HD ** (-0.5))
 
     def run(size):
         highest = None
@@ -88,10 +86,11 @@
             part = jnp.sum(grown.reshape(BS // 8, 8, 2 * BS), axis=0)
             total = part if total is None else total + part
         inverse = 1.0 / jnp.sum(total, axis=0, keepdims=True)
+        stat_ref[0, 0:1, :] = highest
+        stat_ref[0, 1:2, :] = inverse
         attended = None
         for s in range(0, size, 2):
             weights = s_scr[pl.ds(s * BS, 2 * BS), :] * inverse
-            p_ref[0, pl.ds(s * BS, 2 * BS), :] = weights
             pair = jnp.concatenate([vt_scr[places[step, s]], vt_scr[places[step, s + 1]]], axis=1)
             term = dot(pair, weights.astype(jnp.bfloat16))
             attended = term if attended is None else attended + term
@@ -105,7 +104,6 @@
     rows, cols = query_rows.shape
     extent = 3 * blocks
     whole = lambda *shape: pl.BlockSpec(shape, lambda i, *_: (0,) * len(shape))
-    window = jax.ShapeDtypeStruct((extent, BS, cols), jnp.bfloat16)
     return pl.pallas_call(
         forward_kernel,
         grid_spec=pltpu.PrefetchScalarGridSpec(
@@ -120,8 +118,7 @@
             ],
             out_specs=[
                 pl.BlockSpec((cols, BS), lambda i, *_: (0, i)),
-                pl.BlockSpec((1, slots * BS, 2 * BS), lambda i, *_: (i, 0, 0)),
-                whole(extent, BS, cols),
+                pl.BlockSpec((1, 8, 2 * BS), lambda i, *_: (i, 0, 0)),
                 whole(extent, BS, cols),
             ],
             scratch_shapes=[
@@ -132,9 +129,8 @@
         ),
         out_shape=[
             jax.ShapeDtypeStruct((cols, rows), jnp.bfloat16),
-            jax.ShapeDtypeStruct((blocks, slots * BS, 2 * BS), jnp.float32),
-            window,
-            window,
+            jax.ShapeDtypeStruct((blocks, 8, 2 * BS), jnp.float32),
+            jax.ShapeDtypeStruct((extent, BS, cols), jnp.bfloat16),
         ],
         compiler_params=pltpu.CompilerParams(dimension_semantics=("arbitrary",)),
         cost_estimate=cost(blocks),
@@ -142,20 +138,30 @@
     )(places, active, query_rows, key_rows, value_rows, left, right)
 
 
-def backward_kernel(own, places, active, halo, q_ref, ga_ref, att_ref, p_ref, kt_ref, v_ref, *rest):
+def backward_kernel(own, places, active, halo, q_ref, ga_ref, att_ref, stat_ref, kt_ref, first, second, *rest):
     if own:
-        base_ref, dq_ref, dk, dv = rest
+        base_ref, dq_ref, dk, dv, k_scr, v_scr = rest
     else:
-        dq_ref, left_ref, right_ref, dk, dv = rest
+        dq_ref, left_ref, right_ref, dk, dv, k_scr, v_scr = rest
     step = pl.program_id(0)
-    slots = p_ref.shape[1] // BS
-    blocks = v_ref.shape[0] // 3
+    slots = places.shape[1]
+    blocks = first.shape[0] // BS
     factor = HD ** (-0.5)
 
     @pl.when(step == 0)
     def _():
         dk[...] = jnp.zeros_like(dk)
         dv[...] = jnp.zeros_like(dv)
+        for b in range(blocks):
+            rows = pl.ds(b * BS, BS)
+            if own:
+                k_scr[b] = first[rows, :]
+                v_scr[b] = second[rows, :]
+            else:
+                k_scr[b] = first[rows, :BS]
+                v_scr[b] = first[rows, BS:]
+                k_scr[b + blocks] = second[rows, :BS]
+                v_scr[b + blocks] = second[rows, BS:]
 
     grad = ga_ref[...]
     grad_t = grad.T
@@ -169,7 +175,11 @@
     )
     grad_wide = spread_columns(grad_t)
     grad_tall = spread_rows(grad)
-    query_tall = spread_rows(q_ref[...] * factor)
+    query = q_ref[...] * factor
+    query_tall = spread_rows(query)
+    query_wide = spread_columns(query.T)
+    highest = stat_ref[0, 0:1, :]
+    inverse = stat_ref[0, 1:2, :]
     begin = halo[step] if own else 0
     used = active[step] - halo[step] if own else halo[step]
 
@@ -183,16 +193,15 @@
                 if final:
                     slot = jnp.minimum(slot, slots - 1)
                 place = places[step, slot]
-                rows = pl.ds(pl.multiple_of(slot * BS, BS), BS)
-                weights = p_ref[0, rows, :]
+                at = place - blocks if own else jnp.where(place < blocks, place, place - blocks)
+                at = jnp.clip(at, 0, dk.shape[0] - 1)
+                weights = jnp.exp(dot(k_scr[at], query_wide) - highest) * inverse
                 if final:
                     weights = jnp.where(s + j < used, weights, 0.0)
-                change = weights * (dot(v_ref[place], grad_wide) - dots)
+                change = weights * (dot(v_scr[at], grad_wide) - dots)
                 change = change.astype(jnp.bfloat16)
                 changes.append(change)
-                pair.append(kt_ref[place])
-                at = place - blocks if own else jnp.where(place < blocks, place, place - blocks)
-                at = jnp.clip(at, 0, dk.shape[0] - 1)
+                pair.append(kt_ref[at] if own else kt_ref[place])
                 dk[at] += dot(change, query_tall)
                 dv[at] += dot(weights.astype(jnp.bfloat16), grad_tall)
             term = dot(jnp.concatenate(pair, axis=1), jnp.concatenate(changes, axis=0))
@@ -217,11 +226,12 @@
                 target[rows, BS:] = dv[b].astype(target.dtype)
 
 
-def backward(tables, query_rows, grad_attended, att_t, weights, keys_t, values, base):
-    blocks, slots = tables[0].shape
+def backward(tables, query_rows, grad_attended, att_t, stats, keys_t, sources, base):
+    blocks, _ = tables[0].shape
     rows, cols = query_rows.shape
     extent = 3 * blocks
     own = bool(base)
+    held = blocks if own else 2 * blocks
     whole = lambda *shape: pl.BlockSpec(shape, lambda i, *_: (0,) * len(shape))
     one = pl.BlockSpec((BS, cols), lambda i, *_: (i, 0))
     one_t = pl.BlockSpec((cols, BS), lambda i, *_: (0, i))
@@ -229,21 +239,23 @@
         one,
         one,
         one_t,
-        pl.BlockSpec((1, slots * BS, 2 * BS), lambda i, *_: (i, 0, 0)),
-        whole(extent, BS, cols),
-        whole(extent, BS, cols),
+        pl.BlockSpec((1, 8, 2 * BS), lambda i, *_: (i, 0, 0)),
+        pl.BlockSpec((blocks, BS, cols), lambda i, *_: (1, 0, 0)) if own else whole(extent, BS, cols),
+        whole(*sources[0].shape),
+        whole(*sources[1].shape),
     ]
+    scratch = []
     if own:
         in_specs.append(one_t)
         out_specs = [one] + [whole(blocks, BS, cols)] * 2
         out_shape = [jax.ShapeDtypeStruct((rows, cols), jnp.bfloat16)]
         out_shape += [jax.ShapeDtypeStruct((blocks, BS, cols), jnp.float32)] * 2
-        scratch = []
     else:
         out_specs = [one_t] + [whole(rows, 2 * cols)] * 2
         out_shape = [jax.ShapeDtypeStruct((cols, rows), jnp.float32)]
         out_shape += [jax.ShapeDtypeStruct((rows, 2 * cols), jnp.bfloat16)] * 2
-        scratch = [pltpu.VMEM((2 * blocks, BS, cols), jnp.float32)] * 2
+        scratch = [pltpu.VMEM((held, BS, cols), jnp.float32)] * 2
+    scratch += [pltpu.VMEM((held, BS, cols), jnp.bfloat16)] * 2
     return pl.pallas_call(
         functools.partial(backward_kernel, own),
         grid_spec=pltpu.PrefetchScalarGridSpec(
@@ -257,7 +269,7 @@
         compiler_params=pltpu.CompilerParams(dimension_semantics=("arbitrary",)),
         cost_estimate=cost(blocks),
         name="backward",
-    )(*tables, query_rows, grad_attended, att_t, weights, keys_t, values, *base)
+    )(*tables, query_rows, grad_attended, att_t, stats, keys_t, *sources, *base)
 
 
 def shifted(x, axis, by):
@@ -341,21 +353,23 @@
     left = shifted(packed, "ctx", 1)
     right = shifted(packed, "ctx", -1)
     tables = slot_tables(neighbours, counts, blocks)
-    att_t, weights, keys_t, values = forward(
+    att_t, stats, keys_t = forward(
         *tables[:2], query_rows, key_rows, value_rows, left, right
     )
     grad_attended, partial = project(gathered, out_weight, att_t)
-    shared = (query_rows, grad_attended, att_t, weights, keys_t, values)
+    shared = (query_rows, grad_attended, att_t, stats, keys_t)
     members = lax.axis_size("ctx")
     pieces = partial.reshape(members, -1, partial.shape[-1])
     pieces = lax.all_to_all(pieces, "ctx", 0, 0)
-    query_part, to_left, to_right = backward(tables, *shared, ())
+    query_part, to_left, to_right = backward(tables, *shared, (left, right), ())
     from_right = shifted(to_left, "ctx", -1)
     from_left = shifted(to_right, "ctx", 1)
     piece = jnp.sum(pieces.astype(jnp.float32), axis=0) * node_count ** (-0.5)
     copies = jnp.broadcast_to(piece.astype(partial.dtype)[None], pieces.shape)
     weight_sum = lax.all_to_all(copies, "ctx", 0, 0)
-    query_grad, key_own, value_own = backward(tables, *shared, (query_part,))
+    query_grad, key_own, value_own = backward(
+        tables, *shared, (key_rows, value_rows), (query_part,)
+    )
     weight_grad = place(weight_sum.reshape(partial.shape))
     sides = [
         own.reshape(row_count, col_count)

time: 132 us -> 130 us (0.985)
  Pallas kernels: 46.8 us -> 43.2 us
  waiting for transfers between devices: 28.1 us -> 30.2 us
    all_to_all x1, waiting for transfers between devices: 22.3 us -> 24.4 us  [gather_heads(): return lax.all_to_all(copies, 'head', 0, 0)]
    pallas_call x1, Pallas kernels: 13.4 us -> 11.3 us  [forward(): pl.pallas_call(forward_kernel, grid_spec=pltpu.PrefetchScalarGridSpec(num...]
    pallas_call x2, Pallas kernels: 28.1 us -> 26.6 us  [backward(): pl.pallas_call(functools.partial(backward_kernel, own), grid_spec=pltpu.P...]
  transfers between devices with their start and end apart: 7 -> 7, of which waited for: 3 -> 3; matrix products, arithmetic and copies ran while one was open for 5% -> 5% of each run, Pallas kernels for 32% -> 30%
where the time goes in v5:
time: 130 us; the launch traced here: 128 us
  starting transfers between devices  43.2 us (33%)
  Pallas kernels  43.2 us (33%)
  waiting for transfers between devices  30.2 us (23%)
  local copies, waits for them, and re-layouts  6.31 us (5%)
  other arithmetic  4.58 us (4%)
    pallas_call x2, Pallas kernels, backward(): pl.pallas_call(functools.partial(backward_kernel, own), grid_spec=pltpu.P...  26.6 us
    all_to_all x1, waiting for transfers between devices, gather_heads(): return lax.all_to_all(copies, 'head', 0, 0)  24.4 us
    all_to_all x1, starting transfers between devices, body(): pieces = lax.all_to_all(pieces, 'ctx', 0, 0)  13.8 us
    pallas_call x1, Pallas kernels, forward(): pl.pallas_call(forward_kernel, grid_spec=pltpu.PrefetchScalarGridSpec(num...  11.3 us
    ppermute x4, starting transfers between devices, shifted(): return lax.ppermute(x, axis, [(i, (i + by) % count) for i in range(count)])  11.1 us
    all_to_all x1, starting transfers between devices, body(): weight_sum = lax.all_to_all(copies, 'ctx', 0, 0)  10.5 us
    all_to_all x1, starting transfers between devices, gather_heads(): return lax.all_to_all(copies, 'head', 0, 0)  7.77 us
    ppermute x4, waiting for transfers between devices, shifted(): return lax.ppermute(x, axis, [(i, (i + by) % count) for i in range(count)])  5.78 us
  transfers between devices with their start and end apart: 7, of which 3 were waited for; matrix products, arithmetic and copies ran while one was open for 5% of the time, Pallas kernels for 30%

profile of v5, /device:TPU:1, one launch (start us, length us, event | category | flops | bytes accessed | tf_op | source)
XLA Modules:
  0.0 128.3 jit_solution(13117216510465630974)
XLA Ops:
  0.6 2.6 %broadcast_in_dim.23 = bf16[8,1024,128]{2,1,0:T(8,128)(2,1)} broadcast(bf16[1024,128]{1,0:T(8,128)(2,1)} %param.10), dimensions={1,2} | broadcast | bytes 2359296 | tf_op jit(solution)/shard_map/broadcast_in_dim | solution.py:327
  3.2 0.0 copy-start.2
  3.2 0.0 copy-start.3
  3.2 7.8 %all-to-all-start = ((bf16[8,1024,128]{2,1,0:T(8,128)(2,1)}), bf16[8,1024,128]{2,1,0:T(8,128)(2,1)S(1)}, u32[]{:S(2)}, u32[]{:S(2)}) async-start(bf16[8,1024,128]{2,1,0:T(8,128)(2,1)} %broadcast_in_dim.23), calls=%async_computation | async-start | bytes 4194304 | tf_op jit(solution)/shard_map/all_to_all | solution.py:328
  11.0 0.0 copy-done.2
  11.0 0.0 copy-done.3
  11.0 0.1 constant_dynamic-update-slice_fusion
  11.1 4.8 %collective-permute-start = (bf16[1024,256]{1,0:T(8,128)(2,1)S(1)}, bf16[1024,256]{1,0:T(8,128)(2,1)}, u32[]{:S(2)}, u32[]{:S(2)}) collective-permute-start(bf16[1024,256]{1,0:T(8,128)(2,1)S(1)} %constant_dynamic-update-slice_fusion), channel_id=1, source_target_pairs={{0,8},{8,16},{16,24},{24,32},{32,40},{40,48},{48,56},{56,64},{64,7... | collective-permute-start | bytes 1572872 | tf_op jit(solution)/shard_map/ppermute | solution.py:277
  16.0 1.9 %collective-permute-start.1 = (bf16[1024,256]{1,0:T(8,128)(2,1)S(1)}, bf16[1024,256]{1,0:T(8,128)(2,1)}, u32[]{:S(2)}, u32[]{:S(2)}) collective-permute-start(bf16[1024,256]{1,0:T(8,128)(2,1)S(1)} %constant_dynamic-update-slice_fusion), channel_id=1, source_target_pairs={{0,504},{8,0},{16,8},{24,16},{32,24},{40,32},{48,40},{56,48},{64,5... | collective-permute-start | bytes 1572872 | tf_op jit(solution)/shard_map/ppermute | solution.py:277
  17.9 0.8 dynamic_slice.6.active
  18.7 0.0 copy-start.4
  18.7 1.3 %convert_reduce_fusion.2 = (s32[8]{0:T(128)}, pred[8,12]{0,1:T(8,128)(4,1)S(1)}, s32[8,12]{0,1:T(8,128)S(1)}) fusion(s32[8]{0:T(128)S(1)} %dynamic_slice.6.active, s32[]{:T(128)S(6)} %sub.9, s32[512,12]{0,1:T(8,128)} %param.12, s32[]{:T(128)S(6)} %select_n.12), kind=kLoop, calls=%fused_computation.11 | loop fusion | flops 1048 | bytes 936 | tf_op jit(solution)/shard_map/reduce_sum | solution.py:343
  20.0 0.1 copy.14
  20.0 0.3 convert_reduce_fusion.1
  20.4 0.7 select_reduce_fusion.places
  21.1 1.0 collective-permute-done.left.first
  22.1 4.8 %collective-permute-done.1.right.second = bf16[1024,256]{1,0:T(8,128)(2,1)} collective-permute-done((bf16[1024,256]{1,0:T(8,128)(2,1)S(1)}, bf16[1024,256]{1,0:T(8,128)(2,1)}, u32[]{:S(2)}, u32[]{:S(2)}) %collective-permute-start.1) | collective-permute-done | bytes 524320 | tf_op jit(solution)/shard_map/ppermute | solution.py:277
  26.9 0.0 copy-done.4
  26.9 11.3 %forward.1 = (bf16[128,1024]{1,0:T(8,128)(2,1)}, f32[8,8,256]{2,1,0:T(8,128)}, bf16[24,128,128]{2,1,0:T(8,128)(2,1)}) custom-call(s32[8,12]{1,0:T(8,128)} %select_reduce_fusion.places, s32[8]{0:T(128)} %copy-done.4, bf16[1024,128]{1,0:T(8,128)(2,1)} %q_ref.5, bf16[1024,128]{1,0:T(8,128)(2,1)} %first.1, bf16[1024,128]{1,0:T(8,128)(2,1)} %second.1, ...), custom_call_target="tpu_custom_call" | custom-call | flops 16000000000 | bytes 8000000 | tf_op jit(solution)/shard_map/forward/pallas_call | solution.py:107
  38.2 24.4 %all-to-all-done.g_ref = bf16[8,1024,128]{2,1,0:T(8,128)(2,1)S(1)} async-done(((bf16[8,1024,128]{2,1,0:T(8,128)(2,1)}), bf16[8,1024,128]{2,1,0:T(8,128)(2,1)S(1)}, u32[]{:S(2)}, u32[]{:S(2)}) %all-to-all-start) | async-done | bytes 2097184 | tf_op jit(solution)/shard_map/all_to_all | solution.py:328
  62.6 0.0 copy-start
  62.6 1.3 %copy-done = bf16[8,1024,128]{2,1,0:T(8,128)(2,1)} copy-done((bf16[8,1024,128]{2,1,0:T(8,128)(2,1)}, bf16[8,1024,128]{2,1,0:T(8,128)(2,1)S(1)}, u32[]{:S(2)}) %copy-start) | copy-done | bytes 2097176
  64.0 3.5 %project.1 = (bf16[1024,128]{1,0:T(8,128)(2,1)}, bf16[8,128,128]{2,1,0:T(8,128)(2,1)}) custom-call(bf16[8,1024,128]{2,1,0:T(8,128)(2,1)} %copy-done, bf16[128,1024]{1,0:T(8,128)(2,1)} %w_ref.1, bf16[128,1024]{1,0:T(8,128)(2,1)} %get-tuple-element.15.att_ref), custom_call_target="tpu_custom_call" | custom-call | flops 4000000000 | bytes 2000000 | tf_op jit(solution)/shard_map/project/pallas_call | solution.py:300
  67.4 13.8 %all-to-all-start.1 = ((bf16[64,16,128]{2,1,0:T(8,128)(2,1)}), bf16[64,16,128]{2,1,0:T(8,128)(2,1)S(1)}, u32[]{:S(2)}, u32[]{:S(2)}) async-start(bf16[64,16,128]{2,1,0:T(8,128)(2,1)} %bitcast.15), calls=%async_computation.1 | async-start | bytes 524288 | tf_op jit(solution)/shard_map/all_to_all | solution.py:363
  81.3 15.0 %backward.2 = (f32[128,1024]{1,0:T(8,128)}, bf16[1024,256]{1,0:T(8,128)(2,1)}, bf16[1024,256]{1,0:T(8,128)(2,1)}) custom-call(s32[8,12]{1,0:T(8,128)} %select_reduce_fusion.places, s32[8]{0:T(128)} %copy-done.4, s32[8]{0:T(128)} %get-tuple-element.26.halo, bf16[1024,128]{1,0:T(8,128)(2,1)} %q_ref.5, bf16[1024,128]{1,0:T(8,128)(2,1)} %get-tuple-element.16.ga_ref, ...), custom_call_target="tpu_custom_call" | custom-call | flops 16000000000 | bytes 8000000 | tf_op jit(solution)/shard_map/backward/pallas_call | solution.py:259
  96.2 1.9 %collective-permute-start.3 = (bf16[1024,256]{1,0:T(8,128)(2,1)}, bf16[1024,256]{1,0:T(8,128)(2,1)S(1)}, u32[]{:S(2)}, u32[]{:S(2)}) collective-permute-start(bf16[1024,256]{1,0:T(8,128)(2,1)} %get-tuple-element.23), channel_id=1, source_target_pairs={{0,8},{8,16},{16,24},{24,32},{32,40},{40,48},{48,56},{56,64},{64,7... | collective-permute-start | bytes 1572872 | tf_op jit(solution)/shard_map/ppermute | solution.py:277
  98.2 2.4 %collective-permute-start.2 = (bf16[1024,256]{1,0:T(8,128)(2,1)}, bf16[1024,256]{1,0:T(8,128)(2,1)S(1)}, u32[]{:S(2)}, u32[]{:S(2)}) collective-permute-start(bf16[1024,256]{1,0:T(8,128)(2,1)} %get-tuple-element.22), channel_id=1, source_target_pairs={{0,504},{8,0},{16,8},{24,16},{32,24},{40,32},{48,40},{56,48},{64,5... | collective-permute-start | bytes 1572872 | tf_op jit(solution)/shard_map/ppermute | solution.py:277
  100.6 0.0 all-to-all-done.1
  100.6 0.1 convert_reduce_fusion
  100.7 0.8 broadcast_in_dim.24
  101.4 10.5 %all-to-all-start.2 = ((bf16[64,16,128]{2,1,0:T(8,128)(2,1)}), bf16[64,16,128]{2,1,0:T(8,128)(2,1)S(1)}, u32[]{:S(2)}, u32[]{:S(2)}) async-start(bf16[64,16,128]{2,1,0:T(8,128)(2,1)} %broadcast_in_dim.24), calls=%async_computation.2 | async-start | bytes 524288 | tf_op jit(solution)/shard_map/all_to_all | solution.py:369
  112.0 11.6 %backward.3 = (bf16[1024,128]{1,0:T(8,128)(2,1)}, f32[8,128,128]{2,1,0:T(8,128)}, f32[8,128,128]{2,1,0:T(8,128)}) custom-call(s32[8,12]{1,0:T(8,128)} %select_reduce_fusion.places, s32[8]{0:T(128)} %copy-done.4, s32[8]{0:T(128)} %get-tuple-element.26.halo, bf16[1024,128]{1,0:T(8,128)(2,1)} %q_ref.5, bf16[1024,128]{1,0:T(8,128)(2,1)} %get-tuple-element.16.ga_ref, ...), custom_call_target="tpu_custom_call" | custom-call | flops 16000000000 | bytes 8000000 | tf_op jit(solution)/shard_map/backward/pallas_call | solution.py:259
  123.6 0.0 collective-permute-done.3
  123.6 0.0 collective-permute-done.2
  123.6 2.2 %fusion.1 = (bf16[1024,128]{1,0:T(8,128)(2,1)}, bf16[1024,128]{1,0:T(8,128)(2,1)}) fusion(f32[8,128,128]{2,1,0:T(8,128)} %get-tuple-element.24, bf16[1024,256]{1,0:T(8,128)(2,1)S(1)} %collective-permute-done.3, bf16[1024,256]{1,0:T(8,128)(2,1)S(1)} %collective-permute-done.2, f32[8,128,128]{2,1,0:T(8,128)} %get-tuple-element.21), kind=kLoop, calls=%fused_computation.2 | loop fusion | flops 1310720 | bytes 2621440 | tf_op jit(solution)/shard_map/convert_element_type | solution.py:380
  125.8 0.0 all-to-all-done.2
  125.8 0.0 copy-start.1
  125.8 0.7 copy-done.1
  126.5 1.8 %place.1 = f32[128,1024]{1,0:T(8,128)} custom-call(bf16[8,128,128]{2,1,0:T(8,128)(2,1)} %bitcast.14), custom_call_target="tpu_custom_call" | custom-call | tf_op jit(solution)/shard_map/place/pallas_call | solution.py:319
  (3 shorter events, 0.1 us)
Async XLA Ops:
  3.2 7.8 %copy-start.2 = (bf16[1024,128]{1,0:T(8,128)(2,1)S(1)}, bf16[1024,128]{1,0:T(8,128)(2,1)}, u32[]{:S(2)}) copy-start(bf16[1024,128]{1,0:T(8,128)(2,1)} %first.1) | copy-start | bytes 786436
  3.2 7.8 %copy-start.3 = (bf16[1024,128]{1,0:T(8,128)(2,1)S(1)}, bf16[1024,128]{1,0:T(8,128)(2,1)}, u32[]{:S(2)}) copy-start(bf16[1024,128]{1,0:T(8,128)(2,1)} %second.1) | copy-start | bytes 786436
  3.2 59.4 %all-to-all-start = ((bf16[8,1024,128]{2,1,0:T(8,128)(2,1)}), bf16[8,1024,128]{2,1,0:T(8,128)(2,1)S(1)}, u32[]{:S(2)}, u32[]{:S(2)}) async-start(bf16[8,1024,128]{2,1,0:T(8,128)(2,1)} %broadcast_in_dim.23), calls=%async_computation | async-start | bytes 4194304 | tf_op jit(solution)/shard_map/all_to_all | solution.py:328
  11.1 11.0 %collective-permute-start = (bf16[1024,256]{1,0:T(8,128)(2,1)S(1)}, bf16[1024,256]{1,0:T(8,128)(2,1)}, u32[]{:S(2)}, u32[]{:S(2)}) collective-permute-start(bf16[1024,256]{1,0:T(8,128)(2,1)S(1)} %constant_dynamic-update-slice_fusion), channel_id=1, source_target_pairs={{0,8},{8,16},{16,24},{24,32},{32,40},{40,48},{48,56},{56,64},{64,7... | collective-permute-start | bytes 1572872 | tf_op jit(solution)/shard_map/ppermute | solution.py:277
  16.0 10.9 %collective-permute-start.1 = (bf16[1024,256]{1,0:T(8,128)(2,1)S(1)}, bf16[1024,256]{1,0:T(8,128)(2,1)}, u32[]{:S(2)}, u32[]{:S(2)}) collective-permute-start(bf16[1024,256]{1,0:T(8,128)(2,1)S(1)} %constant_dynamic-update-slice_fusion), channel_id=1, source_target_pairs={{0,504},{8,0},{16,8},{24,16},{32,24},{40,32},{48,40},{56,48},{64,5... | collective-permute-start | bytes 1572872 | tf_op jit(solution)/shard_map/ppermute | solution.py:277
  18.7 8.2 %copy-start.4 = (s32[8]{0:T(128)}, s32[8]{0:T(128)S(1)}, u32[]{:S(2)}) copy-start(s32[8]{0:T(128)S(1)} %dynamic_slice.6.active) | copy-start | bytes 100
  62.6 1.3 %copy-start = (bf16[8,1024,128]{2,1,0:T(8,128)(2,1)}, bf16[8,1024,128]{2,1,0:T(8,128)(2,1)S(1)}, u32[]{:S(2)}) copy-start(bf16[8,1024,128]{2,1,0:T(8,128)(2,1)S(1)} %all-to-all-done.g_ref) | copy-start | bytes 6291460
  67.4 33.1 %all-to-all-start.1 = ((bf16[64,16,128]{2,1,0:T(8,128)(2,1)}), bf16[64,16,128]{2,1,0:T(8,128)(2,1)S(1)}, u32[]{:S(2)}, u32[]{:S(2)}) async-start(bf16[64,16,128]{2,1,0:T(8,128)(2,1)} %bitcast.15), calls=%async_computation.1 | async-start | bytes 524288 | tf_op jit(solution)/shard_map/all_to_all | solution.py:363
  96.2 27.4 %collective-permute-start.3 = (bf16[1024,256]{1,0:T(8,128)(2,1)}, bf16[1024,256]{1,0:T(8,128)(2,1)S(1)}, u32[]{:S(2)}, u32[]{:S(2)}) collective-permute-start(bf16[1024,256]{1,0:T(8,128)(2,1)} %get-tuple-element.23), channel_id=1, source_target_pairs={{0,8},{8,16},{16,24},{24,32},{32,40},{40,48},{48,56},{56,64},{64,7... | collective-permute-start | bytes 1572872 | tf_op jit(solution)/shard_map/ppermute | solution.py:277
  98.2 25.4 %collective-permute-start.2 = (bf16[1024,256]{1,0:T(8,128)(2,1)}, bf16[1024,256]{1,0:T(8,128)(2,1)S(1)}, u32[]{:S(2)}, u32[]{:S(2)}) collective-permute-start(bf16[1024,256]{1,0:T(8,128)(2,1)} %get-tuple-element.22), channel_id=1, source_target_pairs={{0,504},{8,0},{16,8},{24,16},{32,24},{40,32},{48,40},{56,48},{64,5... | collective-permute-start | bytes 1572872 | tf_op jit(solution)/shard_map/ppermute | solution.py:277
  101.4 24.3 %all-to-all-start.2 = ((bf16[64,16,128]{2,1,0:T(8,128)(2,1)}), bf16[64,16,128]{2,1,0:T(8,128)(2,1)S(1)}, u32[]{:S(2)}, u32[]{:S(2)}) async-start(bf16[64,16,128]{2,1,0:T(8,128)(2,1)} %broadcast_in_dim.24), calls=%async_computation.2 | async-start | bytes 524288 | tf_op jit(solution)/shard_map/all_to_all | solution.py:369
  125.8 0.7 copy-start.1

commit v6 on v5

--- a/solution.py
+++ b/solution.py
@@ -139,10 +139,11 @@
 
 
 def backward_kernel(own, places, active, halo, q_ref, ga_ref, att_ref, stat_ref, kt_ref, first, second, *rest):
+    gw_scr, gt_scr, qw_scr, qt_scr, dot_scr = rest[-5:]
     if own:
-        base_ref, dq_ref, dk, dv, k_scr, v_scr = rest
+        base_ref, dq_ref, dk, dv, k_scr, v_scr, dq_scr = rest[:-5]
     else:
-        dq_ref, left_ref, right_ref, dk, dv, k_scr, v_scr = rest
+        dq_ref, left_ref, right_ref, dk, dv, k_scr, v_scr = rest[:-5]
     step = pl.program_id(0)
     slots = places.shape[1]
     blocks = first.shape[0] // BS
@@ -154,6 +155,16 @@
         dv[...] = jnp.zeros_like(dv)
         for b in range(blocks):
             rows = pl.ds(b * BS, BS)
+            grad = ga_ref[rows, :]
+            grad_t = grad.T
+            products = grad_t.astype(jnp.float32) * att_ref[:, rows].astype(jnp.float32)
+            dot_scr[b, 0:1, :BS] = jnp.sum(products[:HD], axis=0, keepdims=True)
+            dot_scr[b, 0:1, BS:] = jnp.sum(products[HD:], axis=0, keepdims=True)
+            gw_scr[b] = spread_columns(grad_t)
+            gt_scr[b] = spread_rows(grad)
+            query = q_ref[rows, :] * factor
+            qw_scr[b] = spread_columns(query.T)
+            qt_scr[b] = spread_rows(query)
             if own:
                 k_scr[b] = first[rows, :]
                 v_scr[b] = second[rows, :]
@@ -163,23 +174,11 @@
                 k_scr[b + blocks] = second[rows, :BS]
                 v_scr[b + blocks] = second[rows, BS:]
 
-    grad = ga_ref[...]
-    grad_t = grad.T
-    products = grad_t.astype(jnp.float32) * att_ref[...].astype(jnp.float32)
-    dots = jnp.concatenate(
-        [
-            jnp.sum(products[:HD], axis=0, keepdims=True),
-            jnp.sum(products[HD:], axis=0, keepdims=True),
-        ],
-        axis=1,
-    )
-    grad_wide = spread_columns(grad_t)
-    grad_tall = spread_rows(grad)
-    query = q_ref[...] * factor
-    query_tall = spread_rows(query)
-    query_wide = spread_columns(query.T)
-    highest = stat_ref[0, 0:1, :]
-    inverse = stat_ref[0, 1:2, :]
+    grad_wide, grad_tall = gw_scr[step], gt_scr[step]
+    query_wide, query_tall = qw_scr[step], qt_scr[step]
+    dots = dot_scr[step, 0:1, :]
+    highest = stat_ref[step, 0:1, :]
+    inverse = stat_ref[step, 1:2, :]
     begin = halo[step] if own else 0
     used = active[step] - halo[step] if own else halo[step]
 
@@ -208,16 +207,18 @@
             total = term if total is None else total + term
         total = own_heads(total)
         if own:
-            dq_ref[...] = ((total + base_ref[...]) * factor).T.astype(jnp.bfloat16)
+            dq_scr[step] = (total + base_ref[...]) * factor
         else:
             dq_ref[...] = total
 
     by_size(used, run)
 
-    if not own:
-
-        @pl.when(step == pl.num_programs(0) - 1)
-        def _():
+    @pl.when(step == pl.num_programs(0) - 1)
+    def _():
+        if own:
+            for b in range(blocks):
+                dq_ref[pl.ds(b * BS, BS), :] = dq_scr[b].T.astype(jnp.bfloat16)
+        else:
             for b in range(2 * blocks):
                 side, at = divmod(b, blocks)
                 target = (left_ref, right_ref)[side]
@@ -233,13 +234,12 @@
     own = bool(base)
     held = blocks if own else 2 * blocks
     whole = lambda *shape: pl.BlockSpec(shape, lambda i, *_: (0,) * len(shape))
-    one = pl.BlockSpec((BS, cols), lambda i, *_: (i, 0))
     one_t = pl.BlockSpec((cols, BS), lambda i, *_: (0, i))
     in_specs = [
-        one,
-        one,
-        one_t,
-        pl.BlockSpec((1, 8, 2 * BS), lambda i, *_: (i, 0, 0)),
+        whole(rows, cols),
+        whole(rows, cols),
+        whole(cols, rows),
+        whole(*stats.shape),
         pl.BlockSpec((blocks, BS, cols), lambda i, *_: (1, 0, 0)) if own else whole(extent, BS, cols),
         whole(*sources[0].shape),
         whole(*sources[1].shape),
@@ -247,7 +247,7 @@
     scratch = []
     if own:
         in_specs.append(one_t)
-        out_specs = [one] + [whole(blocks, BS, cols)] * 2
+        out_specs = [whole(rows, cols)] + [whole(blocks, BS, cols)] * 2
         out_shape = [jax.ShapeDtypeStruct((rows, cols), jnp.bfloat16)]
         out_shape += [jax.ShapeDtypeStruct((blocks, BS, cols), jnp.float32)] * 2
     else:
@@ -256,6 +256,11 @@
         out_shape += [jax.ShapeDtypeStruct((rows, 2 * cols), jnp.bfloat16)] * 2
         scratch = [pltpu.VMEM((held, BS, cols), jnp.float32)] * 2
     scratch += [pltpu.VMEM((held, BS, cols), jnp.bfloat16)] * 2
+    if own:
+        scratch.append(pltpu.VMEM((blocks, cols, BS), jnp.float32))
+    wide = pltpu.VMEM((blocks, cols, 2 * BS), jnp.bfloat16)
+    tall = pltpu.VMEM((blocks, 2 * BS, cols), jnp.bfloat16)
+    scratch += [wide, tall, wide, tall, pltpu.VMEM((blocks, 8, 2 * BS), jnp.float32)]
     return pl.pallas_call(
         functools.partial(backward_kernel, own),
         grid_spec=pltpu.PrefetchScalarGridSpec(
@@ -277,7 +282,8 @@
     return lax.ppermute(x, axis, [(i, (i + by) % count) for i in range(count)])
 
 
-def project_kernel(g_ref, w_ref, att_ref, ga_ref, wg_ref):
+def project_kernel(g_ref, w_ref, att_ref, ga_ref, wg_ref, sums):
+    step = pl.program_id(0)
     count = g_ref.shape[0]
     att = att_ref[...]
     total = None
@@ -289,21 +295,47 @@
         )
         total = term if total is None else total + term
         grad = dot(att, part)
-        for j in range(2):
-            wg_ref[k + j] = grad[:, j * BS : (j + 1) * BS].astype(wg_ref.dtype)
+
+        @pl.when(step == 0)
+        def _():
+            sums[k // 2] = grad
+
+        @pl.when(step > 0)
+        def _():
+            sums[k // 2] += grad
+
     ga_ref[...] = total.astype(jnp.bfloat16)
+
+    @pl.when(step == pl.num_programs(0) - 1)
+    def _():
+        for k in range(count):
+            at = (k % 2) * BS
+            wg_ref[k] = sums[k // 2, :, at : at + BS].astype(wg_ref.dtype)
 
 
 def project(gathered, out_weight, att_t):
     count, rows, width = gathered.shape
     cols = out_weight.shape[0]
+    steps = 4
+    each = rows // steps
     return pl.pallas_call(
         project_kernel,
-        in_specs=[pl.BlockSpec(memory_space=pltpu.VMEM)] * 3,
+        grid=(steps,),
+        in_specs=[
+            pl.BlockSpec((count, each, width), lambda i: (0, i, 0)),
+            pl.BlockSpec((cols, count * width), lambda i: (0, 0)),
+            pl.BlockSpec((cols, each), lambda i: (0, i)),
+        ],
+        out_specs=[
+            pl.BlockSpec((each, cols), lambda i: (i, 0)),
+            pl.BlockSpec((count, cols, width), lambda i: (0, 0, 0)),
+        ],
         out_shape=[
             jax.ShapeDtypeStruct((rows, cols), jnp.bfloat16),
             jax.ShapeDtypeStruct((count, cols, width), jnp.bfloat16),
         ],
+        scratch_shapes=[pltpu.VMEM((count // 2, cols, 2 * width), jnp.float32)],
+        compiler_params=pltpu.CompilerParams(dimension_semantics=("arbitrary",)),
         cost_estimate=cost(2),
         name="project",
     )(gathered, out_weight, att_t)

time: 130 us -> 132 us (1.015)
  Pallas kernels: 43.2 us -> 45.1 us
    pallas_call x1, Pallas kernels: 3.46 us -> 5.75 us  [project(): pl.pallas_call(project_kernel, grid=(steps,), in_specs=[pl.BlockSpec((cou...]
  transfers between devices with their start and end apart: 7 -> 7, of which waited for: 3 -> 3; matrix products, arithmetic and copies ran while one was open for 5% -> 5% of each run, Pallas kernels for 30% -> 29%
where the time goes in v6:
time: 132 us; the launch traced here: 130 us
  Pallas kernels  45.1 us (34%)
  starting transfers between devices  43.2 us (33%)
  waiting for transfers between devices  30.2 us (23%)
  local copies, waits for them, and re-layouts  6.31 us (5%)
  other arithmetic  4.58 us (3%)
    pallas_call x2, Pallas kernels, backward(): pl.pallas_call(functools.partial(backward_kernel, own), grid_spec=pltpu.P...  26.3 us
    all_to_all x1, waiting for transfers between devices, gather_heads(): return lax.all_to_all(copies, 'head', 0, 0)  24.4 us
    all_to_all x1, starting transfers between devices, body(): pieces = lax.all_to_all(pieces, 'ctx', 0, 0)  13.8 us
    pallas_call x1, Pallas kernels, forward(): pl.pallas_call(forward_kernel, grid_spec=pltpu.PrefetchScalarGridSpec(num...  11.3 us
    ppermute x4, starting transfers between devices, shifted(): return lax.ppermute(x, axis, [(i, (i + by) % count) for i in range(count)])  11.1 us
    all_to_all x1, starting transfers between devices, body(): weight_sum = lax.all_to_all(copies, 'ctx', 0, 0)  10.5 us
    all_to_all x1, starting transfers between devices, gather_heads(): return lax.all_to_all(copies, 'head', 0, 0)  7.77 us
    ppermute x4, waiting for transfers between devices, shifted(): return lax.ppermute(x, axis, [(i, (i + by) % count) for i in range(count)])  5.78 us
  transfers between devices with their start and end apart: 7, of which 3 were waited for; matrix products, arithmetic and copies ran while one was open for 5% of the time, Pallas kernels for 29%

profile of v6, /device:TPU:1, one launch (start us, length us, event | category | flops | bytes accessed | tf_op | source)
XLA Modules:
  0.0 130.2 jit_solution(11881525765857926385)
XLA Ops:
  0.6 2.6 %broadcast_in_dim.23 = bf16[8,1024,128]{2,1,0:T(8,128)(2,1)} broadcast(bf16[1024,128]{1,0:T(8,128)(2,1)} %param.10), dimensions={1,2} | broadcast | bytes 2359296 | tf_op jit(solution)/shard_map/broadcast_in_dim | solution.py:359
  3.2 0.0 copy-start.2
  3.2 0.0 copy-start.3
  3.2 7.8 %all-to-all-start = ((bf16[8,1024,128]{2,1,0:T(8,128)(2,1)}), bf16[8,1024,128]{2,1,0:T(8,128)(2,1)S(1)}, u32[]{:S(2)}, u32[]{:S(2)}) async-start(bf16[8,1024,128]{2,1,0:T(8,128)(2,1)} %broadcast_in_dim.23), calls=%async_computation | async-start | bytes 4194304 | tf_op jit(solution)/shard_map/all_to_all | solution.py:360
  11.0 0.0 copy-done.2
  11.0 0.0 copy-done.3
  11.0 0.1 constant_dynamic-update-slice_fusion
  11.1 4.8 %collective-permute-start = (bf16[1024,256]{1,0:T(8,128)(2,1)S(1)}, bf16[1024,256]{1,0:T(8,128)(2,1)}, u32[]{:S(2)}, u32[]{:S(2)}) collective-permute-start(bf16[1024,256]{1,0:T(8,128)(2,1)S(1)} %constant_dynamic-update-slice_fusion), channel_id=1, source_target_pairs={{0,8},{8,16},{16,24},{24,32},{32,40},{40,48},{48,56},{56,64},{64,7... | collective-permute-start | bytes 1572872 | tf_op jit(solution)/shard_map/ppermute | solution.py:282
  16.0 1.9 %collective-permute-start.1 = (bf16[1024,256]{1,0:T(8,128)(2,1)S(1)}, bf16[1024,256]{1,0:T(8,128)(2,1)}, u32[]{:S(2)}, u32[]{:S(2)}) collective-permute-start(bf16[1024,256]{1,0:T(8,128)(2,1)S(1)} %constant_dynamic-update-slice_fusion), channel_id=1, source_target_pairs={{0,504},{8,0},{16,8},{24,16},{32,24},{40,32},{48,40},{56,48},{64,5... | collective-permute-start | bytes 1572872 | tf_op jit(solution)/shard_map/ppermute | solution.py:282
  17.9 0.8 dynamic_slice.6.active
  18.7 0.0 copy-start.4
  18.7 1.3 %convert_reduce_fusion.2 = (s32[8]{0:T(128)}, pred[8,12]{0,1:T(8,128)(4,1)S(1)}, s32[8,12]{0,1:T(8,128)S(1)}) fusion(s32[8]{0:T(128)S(1)} %dynamic_slice.6.active, s32[]{:T(128)S(6)} %sub.9, s32[512,12]{0,1:T(8,128)} %param.12, s32[]{:T(128)S(6)} %select_n.12), kind=kLoop, calls=%fused_computation.11 | loop fusion | flops 1048 | bytes 936 | tf_op jit(solution)/shard_map/reduce_sum | solution.py:375
  20.0 0.1 copy.14
  20.0 0.3 convert_reduce_fusion.1
  20.4 0.7 select_reduce_fusion.places
  21.1 1.0 collective-permute-done.left.first
  22.1 4.8 %collective-permute-done.1.right.second = bf16[1024,256]{1,0:T(8,128)(2,1)} collective-permute-done((bf16[1024,256]{1,0:T(8,128)(2,1)S(1)}, bf16[1024,256]{1,0:T(8,128)(2,1)}, u32[]{:S(2)}, u32[]{:S(2)}) %collective-permute-start.1) | collective-permute-done | bytes 524320 | tf_op jit(solution)/shard_map/ppermute | solution.py:282
  26.9 0.0 copy-done.4
  26.9 11.3 %forward.1 = (bf16[128,1024]{1,0:T(8,128)(2,1)}, f32[8,8,256]{2,1,0:T(8,128)}, bf16[24,128,128]{2,1,0:T(8,128)(2,1)}) custom-call(s32[8,12]{1,0:T(8,128)} %select_reduce_fusion.places, s32[8]{0:T(128)} %copy-done.4, bf16[1024,128]{1,0:T(8,128)(2,1)} %q_ref.5, bf16[1024,128]{1,0:T(8,128)(2,1)} %first.1, bf16[1024,128]{1,0:T(8,128)(2,1)} %second.1, ...), custom_call_target="tpu_custom_call" | custom-call | flops 16000000000 | bytes 8000000 | tf_op jit(solution)/shard_map/forward/pallas_call | solution.py:107
  38.2 24.4 %all-to-all-done.g_ref = bf16[8,1024,128]{2,1,0:T(8,128)(2,1)S(1)} async-done(((bf16[8,1024,128]{2,1,0:T(8,128)(2,1)}), bf16[8,1024,128]{2,1,0:T(8,128)(2,1)S(1)}, u32[]{:S(2)}, u32[]{:S(2)}) %all-to-all-start) | async-done | bytes 2097184 | tf_op jit(solution)/shard_map/all_to_all | solution.py:360
  62.6 0.0 copy-start
  62.6 1.3 %copy-done = bf16[8,1024,128]{2,1,0:T(8,128)(2,1)} copy-done((bf16[8,1024,128]{2,1,0:T(8,128)(2,1)}, bf16[8,1024,128]{2,1,0:T(8,128)(2,1)S(1)}, u32[]{:S(2)}) %copy-start) | copy-done | bytes 2097176
  64.0 5.7 %project.1 = (bf16[1024,128]{1,0:T(8,128)(2,1)}, bf16[8,128,128]{2,1,0:T(8,128)(2,1)}) custom-call(bf16[8,1024,128]{2,1,0:T(8,128)(2,1)} %copy-done, bf16[128,1024]{1,0:T(8,128)(2,1)} %w_ref.1, bf16[128,1024]{1,0:T(8,128)(2,1)} %get-tuple-element.15.att_ref), custom_call_target="tpu_custom_call" | custom-call | flops 4000000000 | bytes 2000000 | tf_op jit(solution)/shard_map/project/pallas_call | solution.py:321
  69.7 13.8 %all-to-all-start.1 = ((bf16[64,16,128]{2,1,0:T(8,128)(2,1)}), bf16[64,16,128]{2,1,0:T(8,128)(2,1)S(1)}, u32[]{:S(2)}, u32[]{:S(2)}) async-start(bf16[64,16,128]{2,1,0:T(8,128)(2,1)} %bitcast.15), calls=%async_computation.1 | async-start | bytes 524288 | tf_op jit(solution)/shard_map/all_to_all | solution.py:395
  83.6 14.9 %backward.2 = (f32[128,1024]{1,0:T(8,128)}, bf16[1024,256]{1,0:T(8,128)(2,1)}, bf16[1024,256]{1,0:T(8,128)(2,1)}) custom-call(s32[8,12]{1,0:T(8,128)} %select_reduce_fusion.places, s32[8]{0:T(128)} %copy-done.4, s32[8]{0:T(128)} %get-tuple-element.26.halo, bf16[1024,128]{1,0:T(8,128)(2,1)} %q_ref.5, bf16[1024,128]{1,0:T(8,128)(2,1)} %get-tuple-element.16.ga_ref, ...), custom_call_target="tpu_custom_call" | custom-call | flops 16000000000 | bytes 8000000 | tf_op jit(solution)/shard_map/backward/pallas_call | solution.py:264
  98.4 1.9 %collective-permute-start.3 = (bf16[1024,256]{1,0:T(8,128)(2,1)}, bf16[1024,256]{1,0:T(8,128)(2,1)S(1)}, u32[]{:S(2)}, u32[]{:S(2)}) collective-permute-start(bf16[1024,256]{1,0:T(8,128)(2,1)} %get-tuple-element.23), channel_id=1, source_target_pairs={{0,8},{8,16},{16,24},{24,32},{32,40},{40,48},{48,56},{56,64},{64,7... | collective-permute-start | bytes 1572872 | tf_op jit(solution)/shard_map/ppermute | solution.py:282
  100.3 2.4 %collective-permute-start.2 = (bf16[1024,256]{1,0:T(8,128)(2,1)}, bf16[1024,256]{1,0:T(8,128)(2,1)S(1)}, u32[]{:S(2)}, u32[]{:S(2)}) collective-permute-start(bf16[1024,256]{1,0:T(8,128)(2,1)} %get-tuple-element.22), channel_id=1, source_target_pairs={{0,504},{8,0},{16,8},{24,16},{32,24},{40,32},{48,40},{56,48},{64,5... | collective-permute-start | bytes 1572872 | tf_op jit(solution)/shard_map/ppermute | solution.py:282
  102.8 0.0 all-to-all-done.1
  102.8 0.1 convert_reduce_fusion
  102.9 0.8 broadcast_in_dim.24
  103.6 10.5 %all-to-all-start.2 = ((bf16[64,16,128]{2,1,0:T(8,128)(2,1)}), bf16[64,16,128]{2,1,0:T(8,128)(2,1)S(1)}, u32[]{:S(2)}, u32[]{:S(2)}) async-start(bf16[64,16,128]{2,1,0:T(8,128)(2,1)} %broadcast_in_dim.24), calls=%async_computation.2 | async-start | bytes 524288 | tf_op jit(solution)/shard_map/all_to_all | solution.py:401
  114.2 11.4 %backward.3 = (bf16[1024,128]{1,0:T(8,128)(2,1)}, f32[8,128,128]{2,1,0:T(8,128)}, f32[8,128,128]{2,1,0:T(8,128)}) custom-call(s32[8,12]{1,0:T(8,128)} %select_reduce_fusion.places, s32[8]{0:T(128)} %copy-done.4, s32[8]{0:T(128)} %get-tuple-element.26.halo, bf16[1024,128]{1,0:T(8,128)(2,1)} %q_ref.5, bf16[1024,128]{1,0:T(8,128)(2,1)} %get-tuple-element.16.ga_ref, ...), custom_call_target="tpu_custom_call" | custom-call | flops 16000000000 | bytes 8000000 | tf_op jit(solution)/shard_map/backward/pallas_call | solution.py:264
  125.6 0.0 collective-permute-done.3
  125.6 0.0 collective-permute-done.2
  125.6 2.2 %fusion.1 = (bf16[1024,128]{1,0:T(8,128)(2,1)}, bf16[1024,128]{1,0:T(8,128)(2,1)}) fusion(f32[8,128,128]{2,1,0:T(8,128)} %get-tuple-element.24, bf16[1024,256]{1,0:T(8,128)(2,1)S(1)} %collective-permute-done.3, bf16[1024,256]{1,0:T(8,128)(2,1)S(1)} %collective-permute-done.2, f32[8,128,128]{2,1,0:T(8,128)} %get-tuple-element.21), kind=kLoop, calls=%fused_computation.2 | loop fusion | flops 1310720 | bytes 2621440 | tf_op jit(solution)/shard_map/convert_element_type | solution.py:412
  127.7 0.0 all-to-all-done.2
  127.7 0.0 copy-start.1
  127.7 0.7 copy-done.1
  128.4 1.8 %place.1 = f32[128,1024]{1,0:T(8,128)} custom-call(bf16[8,128,128]{2,1,0:T(8,128)(2,1)} %bitcast.14), custom_call_target="tpu_custom_call" | custom-call | tf_op jit(solution)/shard_map/place/pallas_call | solution.py:351
  (3 shorter events, 0.1 us)
Async XLA Ops:
  3.2 7.8 %copy-start.2 = (bf16[1024,128]{1,0:T(8,128)(2,1)S(1)}, bf16[1024,128]{1,0:T(8,128)(2,1)}, u32[]{:S(2)}) copy-start(bf16[1024,128]{1,0:T(8,128)(2,1)} %first.1) | copy-start | bytes 786436
  3.2 7.8 %copy-start.3 = (bf16[1024,128]{1,0:T(8,128)(2,1)S(1)}, bf16[1024,128]{1,0:T(8,128)(2,1)}, u32[]{:S(2)}) copy-start(bf16[1024,128]{1,0:T(8,128)(2,1)} %second.1) | copy-start | bytes 786436
  3.2 59.4 %all-to-all-start = ((bf16[8,1024,128]{2,1,0:T(8,128)(2,1)}), bf16[8,1024,128]{2,1,0:T(8,128)(2,1)S(1)}, u32[]{:S(2)}, u32[]{:S(2)}) async-start(bf16[8,1024,128]{2,1,0:T(8,128)(2,1)} %broadcast_in_dim.23), calls=%async_computation | async-start | bytes 4194304 | tf_op jit(solution)/shard_map/all_to_all | solution.py:360
  11.1 11.0 %collective-permute-start = (bf16[1024,256]{1,0:T(8,128)(2,1)S(1)}, bf16[1024,256]{1,0:T(8,128)(2,1)}, u32[]{:S(2)}, u32[]{:S(2)}) collective-permute-start(bf16[1024,256]{1,0:T(8,128)(2,1)S(1)} %constant_dynamic-update-slice_fusion), channel_id=1, source_target_pairs={{0,8},{8,16},{16,24},{24,32},{32,40},{40,48},{48,56},{56,64},{64,7... | collective-permute-start | bytes 1572872 | tf_op jit(solution)/shard_map/ppermute | solution.py:282
  16.0 10.9 %collective-permute-start.1 = (bf16[1024,256]{1,0:T(8,128)(2,1)S(1)}, bf16[1024,256]{1,0:T(8,128)(2,1)}, u32[]{:S(2)}, u32[]{:S(2)}) collective-permute-start(bf16[1024,256]{1,0:T(8,128)(2,1)S(1)} %constant_dynamic-update-slice_fusion), channel_id=1, source_target_pairs={{0,504},{8,0},{16,8},{24,16},{32,24},{40,32},{48,40},{56,48},{64,5... | collective-permute-start | bytes 1572872 | tf_op jit(solution)/shard_map/ppermute | solution.py:282
  18.7 8.2 %copy-start.4 = (s32[8]{0:T(128)}, s32[8]{0:T(128)S(1)}, u32[]{:S(2)}) copy-start(s32[8]{0:T(128)S(1)} %dynamic_slice.6.active) | copy-start | bytes 100
  62.6 1.3 %copy-start = (bf16[8,1024,128]{2,1,0:T(8,128)(2,1)}, bf16[8,1024,128]{2,1,0:T(8,128)(2,1)S(1)}, u32[]{:S(2)}) copy-start(bf16[8,1024,128]{2,1,0:T(8,128)(2,1)S(1)} %all-to-all-done.g_ref) | copy-start | bytes 6291460
  69.7 33.0 %all-to-all-start.1 = ((bf16[64,16,128]{2,1,0:T(8,128)(2,1)}), bf16[64,16,128]{2,1,0:T(8,128)(2,1)S(1)}, u32[]{:S(2)}, u32[]{:S(2)}) async-start(bf16[64,16,128]{2,1,0:T(8,128)(2,1)} %bitcast.15), calls=%async_computation.1 | async-start | bytes 524288 | tf_op jit(solution)/shard_map/all_to_all | solution.py:395
  98.4 27.1 %collective-permute-start.3 = (bf16[1024,256]{1,0:T(8,128)(2,1)}, bf16[1024,256]{1,0:T(8,128)(2,1)S(1)}, u32[]{:S(2)}, u32[]{:S(2)}) collective-permute-start(bf16[1024,256]{1,0:T(8,128)(2,1)} %get-tuple-element.23), channel_id=1, source_target_pairs={{0,8},{8,16},{16,24},{24,32},{32,40},{40,48},{48,56},{56,64},{64,7... | collective-permute-start | bytes 1572872 | tf_op jit(solution)/shard_map/ppermute | solution.py:282
  100.3 25.2 %collective-permute-start.2 = (bf16[1024,256]{1,0:T(8,128)(2,1)}, bf16[1024,256]{1,0:T(8,128)(2,1)S(1)}, u32[]{:S(2)}, u32[]{:S(2)}) collective-permute-start(bf16[1024,256]{1,0:T(8,128)(2,1)} %get-tuple-element.22), channel_id=1, source_target_pairs={{0,504},{8,0},{16,8},{24,16},{32,24},{40,32},{48,40},{56,48},{64,5... | collective-permute-start | bytes 1572872 | tf_op jit(solution)/shard_map/ppermute | solution.py:282
  103.6 24.1 %all-to-all-start.2 = ((bf16[64,16,128]{2,1,0:T(8,128)(2,1)}), bf16[64,16,128]{2,1,0:T(8,128)(2,1)S(1)}, u32[]{:S(2)}, u32[]{:S(2)}) async-start(bf16[64,16,128]{2,1,0:T(8,128)(2,1)} %broadcast_in_dim.24), calls=%async_computation.2 | async-start | bytes 524288 | tf_op jit(solution)/shard_map/all_to_all | solution.py:401
  127.7 0.7 copy-start.1

commit v7 on v5

--- a/solution.py
+++ b/solution.py
@@ -10,12 +10,13 @@
 
 HD = 64
 BS = 128
-SIZES = (2, 4, 6, 8, 10, 12)
-
-
-def by_size(active, run):
+SIZES = (4, 6, 8, 10, 12)
+TWO = 2
+
+
+def by_size(active, run, sizes=SIZES):
     low = -1
-    for size in SIZES:
+    for size in sizes:
         pl.when((active > low) & (active <= size))(lambda size=size: run(size))
         low = size
 
@@ -143,12 +144,12 @@
         base_ref, dq_ref, dk, dv, k_scr, v_scr = rest
     else:
         dq_ref, left_ref, right_ref, dk, dv, k_scr, v_scr = rest
-    step = pl.program_id(0)
+    here = pl.program_id(0)
     slots = places.shape[1]
     blocks = first.shape[0] // BS
     factor = HD ** (-0.5)
 
-    @pl.when(step == 0)
+    @pl.when(here == 0)
     def _():
         dk[...] = jnp.zeros_like(dk)
         dv[...] = jnp.zeros_like(dv)
@@ -163,60 +164,62 @@
                 k_scr[b + blocks] = second[rows, :BS]
                 v_scr[b + blocks] = second[rows, BS:]
 
-    grad = ga_ref[...]
-    grad_t = grad.T
-    products = grad_t.astype(jnp.float32) * att_ref[...].astype(jnp.float32)
-    dots = jnp.concatenate(
-        [
-            jnp.sum(products[:HD], axis=0, keepdims=True),
-            jnp.sum(products[HD:], axis=0, keepdims=True),
-        ],
-        axis=1,
-    )
-    grad_wide = spread_columns(grad_t)
-    grad_tall = spread_rows(grad)
-    query = q_ref[...] * factor
-    query_tall = spread_rows(query)
-    query_wide = spread_columns(query.T)
-    highest = stat_ref[0, 0:1, :]
-    inverse = stat_ref[0, 1:2, :]
-    begin = halo[step] if own else 0
-    used = active[step] - halo[step] if own else halo[step]
+    held = []
+    for i in range(TWO):
+        step = here * TWO + i
+        rows = slice(i * BS, (i + 1) * BS)
+        grad = ga_ref[rows, :]
+        grad_t = grad.T
+        products = grad_t.astype(jnp.float32) * att_ref[:, rows].astype(jnp.float32)
+        dots = jnp.concatenate(
+            [
+                jnp.sum(products[:HD], axis=0, keepdims=True),
+                jnp.sum(products[HD:], axis=0, keepdims=True),
+            ],
+            axis=1,
+        )
+        query = q_ref[rows, :] * factor
+        wide = (spread_columns(query.T), spread_columns(grad_t))
+        tall = (spread_rows(query), spread_rows(grad))
+        begin = halo[step] if own else 0
+        used = active[step] - halo[step] if own else halo[step]
+        held.append((step, rows, dots, wide, tall, begin, used))
 
     def run(size):
-        total = None
+        totals = [None] * TWO
         for s in range(0, size, 2):
-            changes, pair = [], []
-            for j in range(2):
-                slot = begin + s + j
-                final = s + j == size - 1
-                if final:
-                    slot = jnp.minimum(slot, slots - 1)
-                place = places[step, slot]
-                at = place - blocks if own else jnp.where(place < blocks, place, place - blocks)
-                at = jnp.clip(at, 0, dk.shape[0] - 1)
-                weights = jnp.exp(dot(k_scr[at], query_wide) - highest) * inverse
-                if final:
+            for i in range(TWO):
+                step, rows, dots, wide, tall, begin, used = held[i]
+                changes, pair = [], []
+                for j in range(2):
+                    place = places[step, jnp.minimum(begin + s + j, slots - 1)]
+                    at = place - blocks if own else jnp.where(place < blocks, place, place - blocks)
+                    at = jnp.clip(at, 0, dk.shape[0] - 1)
+                    scores = dot(k_scr[at], wide[0])
+                    weights = jnp.exp(scores - stat_ref[i, 0:1, :]) * stat_ref[i, 1:2, :]
                     weights = jnp.where(s + j < used, weights, 0.0)
-                change = weights * (dot(v_scr[at], grad_wide) - dots)
-                change = change.astype(jnp.bfloat16)
-                changes.append(change)
-                pair.append(kt_ref[at] if own else kt_ref[place])
-                dk[at] += dot(change, query_tall)
-                dv[at] += dot(weights.astype(jnp.bfloat16), grad_tall)
-            term = dot(jnp.concatenate(pair, axis=1), jnp.concatenate(changes, axis=0))
-            total = term if total is None else total + term
-        total = own_heads(total)
-        if own:
-            dq_ref[...] = ((total + base_ref[...]) * factor).T.astype(jnp.bfloat16)
-        else:
-            dq_ref[...] = total
-
-    by_size(used, run)
+                    change = weights * (dot(v_scr[at], wide[1]) - dots)
+                    change = change.astype(jnp.bfloat16)
+                    changes.append(change)
+                    pair.append(kt_ref[at] if own else kt_ref[place])
+                    dk[at] += dot(change, tall[0])
+                    dv[at] += dot(weights.astype(jnp.bfloat16), tall[1])
+                term = dot(jnp.concatenate(pair, axis=1), jnp.concatenate(changes, axis=0))
+                totals[i] = term if totals[i] is None else totals[i] + term
+        for i in range(TWO):
+            rows = held[i][1]
+            total = own_heads(totals[i])
+            if own:
+                total = (total + base_ref[:, rows]) * factor
+                dq_ref[rows, :] = total.T.astype(jnp.bfloat16)
+            else:
+                dq_ref[:, rows] = total
+
+    by_size(jnp.maximum(held[0][-1], held[1][-1]), run, (2, 4, 6, 8, 12))
 
     if not own:
 
-        @pl.when(step == pl.num_programs(0) - 1)
+        @pl.when(here == pl.num_programs(0) - 1)
         def _():
             for b in range(2 * blocks):
                 side, at = divmod(b, blocks)
@@ -233,13 +236,13 @@
     own = bool(base)
     held = blocks if own else 2 * blocks
     whole = lambda *shape: pl.BlockSpec(shape, lambda i, *_: (0,) * len(shape))
-    one = pl.BlockSpec((BS, cols), lambda i, *_: (i, 0))
-    one_t = pl.BlockSpec((cols, BS), lambda i, *_: (0, i))
+    one = pl.BlockSpec((TWO * BS, cols), lambda i, *_: (i, 0))
+    one_t = pl.BlockSpec((cols, TWO * BS), lambda i, *_: (0, i))
     in_specs = [
         one,
         one,
         one_t,
-        pl.BlockSpec((1, 8, 2 * BS), lambda i, *_: (i, 0, 0)),
+        pl.BlockSpec((TWO, 8, 2 * BS), lambda i, *_: (i, 0, 0)),
         pl.BlockSpec((blocks, BS, cols), lambda i, *_: (1, 0, 0)) if own else whole(extent, BS, cols),
         whole(*sources[0].shape),
         whole(*sources[1].shape),
@@ -260,7 +263,7 @@
         functools.partial(backward_kernel, own),
         grid_spec=pltpu.PrefetchScalarGridSpec(
             num_scalar_prefetch=3,
-            grid=(blocks,),
+            grid=(blocks // TWO,),
             in_specs=in_specs,
             out_specs=out_specs,
             scratch_shapes=scratch,
@@ -353,9 +356,7 @@
     left = shifted(packed, "ctx", 1)
     right = shifted(packed, "ctx", -1)
     tables = slot_tables(neighbours, counts, blocks)
-    att_t, stats, keys_t = forward(
-        *tables[:2], query_rows, key_rows, value_rows, left, right
-    )
+    att_t, stats, keys_t = forward(*tables[:2], query_rows, key_rows, value_rows, left, right)
     grad_attended, partial = project(gathered, out_weight, att_t)
     shared = (query_rows, grad_attended, att_t, stats, keys_t)
     members = lax.axis_size("ctx")

time: 130 us -> 131 us (level)
  Pallas kernels: 43.2 us -> 44.6 us
    pallas_call x2, Pallas kernels: 26.6 us -> 28 us  [backward(): pl.pallas_call(functools.partial(backward_kernel, own), grid_spec=pltpu.P...]
where the time goes in v7:
time: 131 us; the launch traced here: 130 us
  Pallas kernels  44.6 us (34%)
  starting transfers between devices  43.2 us (33%)
  waiting for transfers between devices  30.2 us (23%)
  local copies, waits for them, and re-layouts  6.31 us (5%)
  other arithmetic  4.58 us (3%)
    pallas_call x2, Pallas kernels, backward(): pl.pallas_call(functools.partial(backward_kernel, own), grid_spec=pltpu.P...  28 us
    all_to_all x1, waiting for transfers between devices, gather_heads(): return lax.all_to_all(copies, 'head', 0, 0)  24.5 us
    all_to_all x1, starting transfers between devices, body(): pieces = lax.all_to_all(pieces, 'ctx', 0, 0)  13.8 us
    pallas_call x1, Pallas kernels, forward(): pl.pallas_call(forward_kernel, grid_spec=pltpu.PrefetchScalarGridSpec(num...  11.3 us
    ppermute x4, starting transfers between devices, shifted(): return lax.ppermute(x, axis, [(i, (i + by) % count) for i in range(count)])  11.1 us
    all_to_all x1, starting transfers between devices, body(): weight_sum = lax.all_to_all(copies, 'ctx', 0, 0)  10.5 us
    all_to_all x1, starting transfers between devices, gather_heads(): return lax.all_to_all(copies, 'head', 0, 0)  7.77 us
    ppermute x4, waiting for transfers between devices, shifted(): return lax.ppermute(x, axis, [(i, (i + by) % count) for i in range(count)])  5.78 us
  transfers between devices with their start and end apart: 7, of which 3 were waited for; matrix products, arithmetic and copies ran while one was open for 5% of the time, Pallas kernels for 30%

profile of v7, /device:TPU:1, one launch (start us, length us, event | category | flops | bytes accessed | tf_op | source)
XLA Modules:
  0.0 129.6 jit_solution(16899599064400468467)
XLA Ops:
  0.6 2.6 %broadcast_in_dim.23 = bf16[8,1024,128]{2,1,0:T(8,128)(2,1)} broadcast(bf16[1024,128]{1,0:T(8,128)(2,1)} %param.10), dimensions={1,2} | broadcast | bytes 2359296 | tf_op jit(solution)/shard_map/broadcast_in_dim | solution.py:330
  3.2 0.0 copy-start.2
  3.2 0.0 copy-start.3
  3.2 7.8 %all-to-all-start = ((bf16[8,1024,128]{2,1,0:T(8,128)(2,1)}), bf16[8,1024,128]{2,1,0:T(8,128)(2,1)S(1)}, u32[]{:S(2)}, u32[]{:S(2)}) async-start(bf16[8,1024,128]{2,1,0:T(8,128)(2,1)} %broadcast_in_dim.23), calls=%async_computation | async-start | bytes 4194304 | tf_op jit(solution)/shard_map/all_to_all | solution.py:331
  11.0 0.0 copy-done.2
  11.0 0.0 copy-done.3
  11.0 0.1 constant_dynamic-update-slice_fusion
  11.1 4.8 %collective-permute-start = (bf16[1024,256]{1,0:T(8,128)(2,1)S(1)}, bf16[1024,256]{1,0:T(8,128)(2,1)}, u32[]{:S(2)}, u32[]{:S(2)}) collective-permute-start(bf16[1024,256]{1,0:T(8,128)(2,1)S(1)} %constant_dynamic-update-slice_fusion), channel_id=1, source_target_pairs={{0,8},{8,16},{16,24},{24,32},{32,40},{40,48},{48,56},{56,64},{64,7... | collective-permute-start | bytes 1572872 | tf_op jit(solution)/shard_map/ppermute | solution.py:280
  16.0 1.9 %collective-permute-start.1 = (bf16[1024,256]{1,0:T(8,128)(2,1)S(1)}, bf16[1024,256]{1,0:T(8,128)(2,1)}, u32[]{:S(2)}, u32[]{:S(2)}) collective-permute-start(bf16[1024,256]{1,0:T(8,128)(2,1)S(1)} %constant_dynamic-update-slice_fusion), channel_id=1, source_target_pairs={{0,504},{8,0},{16,8},{24,16},{32,24},{40,32},{48,40},{56,48},{64,5... | collective-permute-start | bytes 1572872 | tf_op jit(solution)/shard_map/ppermute | solution.py:280
  17.9 0.8 dynamic_slice.6.active
  18.7 0.0 copy-start.4
  18.7 1.3 %convert_reduce_fusion.2 = (s32[8]{0:T(128)}, pred[8,12]{0,1:T(8,128)(4,1)S(1)}, s32[8,12]{0,1:T(8,128)S(1)}) fusion(s32[8]{0:T(128)S(1)} %dynamic_slice.6.active, s32[]{:T(128)S(6)} %sub.9, s32[512,12]{0,1:T(8,128)} %param.12, s32[]{:T(128)S(6)} %select_n.12), kind=kLoop, calls=%fused_computation.11 | loop fusion | flops 1048 | bytes 936 | tf_op jit(solution)/shard_map/reduce_sum | solution.py:346
  20.0 0.1 copy.14
  20.0 0.3 convert_reduce_fusion.1
  20.4 0.7 select_reduce_fusion.places
  21.1 1.0 collective-permute-done.left.first
  22.1 4.8 %collective-permute-done.1.right.second = bf16[1024,256]{1,0:T(8,128)(2,1)} collective-permute-done((bf16[1024,256]{1,0:T(8,128)(2,1)S(1)}, bf16[1024,256]{1,0:T(8,128)(2,1)}, u32[]{:S(2)}, u32[]{:S(2)}) %collective-permute-start.1) | collective-permute-done | bytes 524320 | tf_op jit(solution)/shard_map/ppermute | solution.py:280
  26.9 0.0 copy-done.4
  26.9 11.3 %forward.1 = (bf16[128,1024]{1,0:T(8,128)(2,1)}, f32[8,8,256]{2,1,0:T(8,128)}, bf16[24,128,128]{2,1,0:T(8,128)(2,1)}) custom-call(s32[8,12]{1,0:T(8,128)} %select_reduce_fusion.places, s32[8]{0:T(128)} %copy-done.4, bf16[1024,128]{1,0:T(8,128)(2,1)} %q_ref.5, bf16[1024,128]{1,0:T(8,128)(2,1)} %first.1, bf16[1024,128]{1,0:T(8,128)(2,1)} %second.1, ...), custom_call_target="tpu_custom_call" | custom-call | flops 16000000000 | bytes 8000000 | tf_op jit(solution)/shard_map/forward/pallas_call | solution.py:108
  38.2 24.5 %all-to-all-done.g_ref = bf16[8,1024,128]{2,1,0:T(8,128)(2,1)S(1)} async-done(((bf16[8,1024,128]{2,1,0:T(8,128)(2,1)}), bf16[8,1024,128]{2,1,0:T(8,128)(2,1)S(1)}, u32[]{:S(2)}, u32[]{:S(2)}) %all-to-all-start) | async-done | bytes 2097184 | tf_op jit(solution)/shard_map/all_to_all | solution.py:331
  62.6 0.0 copy-start
  62.6 1.3 %copy-done = bf16[8,1024,128]{2,1,0:T(8,128)(2,1)} copy-done((bf16[8,1024,128]{2,1,0:T(8,128)(2,1)}, bf16[8,1024,128]{2,1,0:T(8,128)(2,1)S(1)}, u32[]{:S(2)}) %copy-start) | copy-done | bytes 2097176
  64.0 3.5 %project.1 = (bf16[1024,128]{1,0:T(8,128)(2,1)}, bf16[8,128,128]{2,1,0:T(8,128)(2,1)}) custom-call(bf16[8,1024,128]{2,1,0:T(8,128)(2,1)} %copy-done, bf16[128,1024]{1,0:T(8,128)(2,1)} %w_ref.1, bf16[128,1024]{1,0:T(8,128)(2,1)} %get-tuple-element.15.att_ref), custom_call_target="tpu_custom_call" | custom-call | flops 4000000000 | bytes 2000000 | tf_op jit(solution)/shard_map/project/pallas_call | solution.py:303
  67.4 13.8 %all-to-all-start.1 = ((bf16[64,16,128]{2,1,0:T(8,128)(2,1)}), bf16[64,16,128]{2,1,0:T(8,128)(2,1)S(1)}, u32[]{:S(2)}, u32[]{:S(2)}) async-start(bf16[64,16,128]{2,1,0:T(8,128)(2,1)} %bitcast.15), calls=%async_computation.1 | async-start | bytes 524288 | tf_op jit(solution)/shard_map/all_to_all | solution.py:364
  81.3 16.4 %backward.2 = (f32[128,1024]{1,0:T(8,128)}, bf16[1024,256]{1,0:T(8,128)(2,1)}, bf16[1024,256]{1,0:T(8,128)(2,1)}) custom-call(s32[8,12]{1,0:T(8,128)} %select_reduce_fusion.places, s32[8]{0:T(128)} %copy-done.4, s32[8]{0:T(128)} %get-tuple-element.26.halo, bf16[1024,128]{1,0:T(8,128)(2,1)} %q_ref.5, bf16[1024,128]{1,0:T(8,128)(2,1)} %get-tuple-element.16.ga_ref, ...), custom_call_target="tpu_custom_call" | custom-call | flops 16000000000 | bytes 8000000 | tf_op jit(solution)/shard_map/backward/pallas_call | solution.py:262
  97.7 1.9 %collective-permute-start.3 = (bf16[1024,256]{1,0:T(8,128)(2,1)}, bf16[1024,256]{1,0:T(8,128)(2,1)S(1)}, u32[]{:S(2)}, u32[]{:S(2)}) collective-permute-start(bf16[1024,256]{1,0:T(8,128)(2,1)} %get-tuple-element.23), channel_id=1, source_target_pairs={{0,8},{8,16},{16,24},{24,32},{32,40},{40,48},{48,56},{56,64},{64,7... | collective-permute-start | bytes 1572872 | tf_op jit(solution)/shard_map/ppermute | solution.py:280
  99.6 2.4 %collective-permute-start.2 = (bf16[1024,256]{1,0:T(8,128)(2,1)}, bf16[1024,256]{1,0:T(8,128)(2,1)S(1)}, u32[]{:S(2)}, u32[]{:S(2)}) collective-permute-start(bf16[1024,256]{1,0:T(8,128)(2,1)} %get-tuple-element.22), channel_id=1, source_target_pairs={{0,504},{8,0},{16,8},{24,16},{32,24},{40,32},{48,40},{56,48},{64,5... | collective-permute-start | bytes 1572872 | tf_op jit(solution)/shard_map/ppermute | solution.py:280
  102.1 0.0 all-to-all-done.1
  102.1 0.1 convert_reduce_fusion
  102.2 0.8 broadcast_in_dim.24
  102.9 10.5 %all-to-all-start.2 = ((bf16[64,16,128]{2,1,0:T(8,128)(2,1)}), bf16[64,16,128]{2,1,0:T(8,128)(2,1)S(1)}, u32[]{:S(2)}, u32[]{:S(2)}) async-start(bf16[64,16,128]{2,1,0:T(8,128)(2,1)} %broadcast_in_dim.24), calls=%async_computation.2 | async-start | bytes 524288 | tf_op jit(solution)/shard_map/all_to_all | solution.py:370
  113.4 11.6 %backward.3 = (bf16[1024,128]{1,0:T(8,128)(2,1)}, f32[8,128,128]{2,1,0:T(8,128)}, f32[8,128,128]{2,1,0:T(8,128)}) custom-call(s32[8,12]{1,0:T(8,128)} %select_reduce_fusion.places, s32[8]{0:T(128)} %copy-done.4, s32[8]{0:T(128)} %get-tuple-element.26.halo, bf16[1024,128]{1,0:T(8,128)(2,1)} %q_ref.5, bf16[1024,128]{1,0:T(8,128)(2,1)} %get-tuple-element.16.ga_ref, ...), custom_call_target="tpu_custom_call" | custom-call | flops 16000000000 | bytes 8000000 | tf_op jit(solution)/shard_map/backward/pallas_call | solution.py:262
  124.9 0.0 collective-permute-done.3
  125.0 0.0 collective-permute-done.2
  125.0 2.2 %fusion.1 = (bf16[1024,128]{1,0:T(8,128)(2,1)}, bf16[1024,128]{1,0:T(8,128)(2,1)}) fusion(f32[8,128,128]{2,1,0:T(8,128)} %get-tuple-element.24, bf16[1024,256]{1,0:T(8,128)(2,1)S(1)} %collective-permute-done.3, bf16[1024,256]{1,0:T(8,128)(2,1)S(1)} %collective-permute-done.2, f32[8,128,128]{2,1,0:T(8,128)} %get-tuple-element.21), kind=kLoop, calls=%fused_computation.2 | loop fusion | flops 1310720 | bytes 2621440 | tf_op jit(solution)/shard_map/convert_element_type | solution.py:381
  127.1 0.0 all-to-all-done.2
  127.1 0.0 copy-start.1
  127.1 0.7 copy-done.1
  127.8 1.8 %place.1 = f32[128,1024]{1,0:T(8,128)} custom-call(bf16[8,128,128]{2,1,0:T(8,128)(2,1)} %bitcast.14), custom_call_target="tpu_custom_call" | custom-call | tf_op jit(solution)/shard_map/place/pallas_call | solution.py:322
  (3 shorter events, 0.1 us)
Async XLA Ops:
  3.2 7.8 %copy-start.2 = (bf16[1024,128]{1,0:T(8,128)(2,1)S(1)}, bf16[1024,128]{1,0:T(8,128)(2,1)}, u32[]{:S(2)}) copy-start(bf16[1024,128]{1,0:T(8,128)(2,1)} %first.1) | copy-start | bytes 786436
  3.2 7.8 %copy-start.3 = (bf16[1024,128]{1,0:T(8,128)(2,1)S(1)}, bf16[1024,128]{1,0:T(8,128)(2,1)}, u32[]{:S(2)}) copy-start(bf16[1024,128]{1,0:T(8,128)(2,1)} %second.1) | copy-start | bytes 786436
  3.2 59.4 %all-to-all-start = ((bf16[8,1024,128]{2,1,0:T(8,128)(2,1)}), bf16[8,1024,128]{2,1,0:T(8,128)(2,1)S(1)}, u32[]{:S(2)}, u32[]{:S(2)}) async-start(bf16[8,1024,128]{2,1,0:T(8,128)(2,1)} %broadcast_in_dim.23), calls=%async_computation | async-start | bytes 4194304 | tf_op jit(solution)/shard_map/all_to_all | solution.py:331
  11.1 11.0 %collective-permute-start = (bf16[1024,256]{1,0:T(8,128)(2,1)S(1)}, bf16[1024,256]{1,0:T(8,128)(2,1)}, u32[]{:S(2)}, u32[]{:S(2)}) collective-permute-start(bf16[1024,256]{1,0:T(8,128)(2,1)S(1)} %constant_dynamic-update-slice_fusion), channel_id=1, source_target_pairs={{0,8},{8,16},{16,24},{24,32},{32,40},{40,48},{48,56},{56,64},{64,7... | collective-permute-start | bytes 1572872 | tf_op jit(solution)/shard_map/ppermute | solution.py:280
  16.0 10.9 %collective-permute-start.1 = (bf16[1024,256]{1,0:T(8,128)(2,1)S(1)}, bf16[1024,256]{1,0:T(8,128)(2,1)}, u32[]{:S(2)}, u32[]{:S(2)}) collective-permute-start(bf16[1024,256]{1,0:T(8,128)(2,1)S(1)} %constant_dynamic-update-slice_fusion), channel_id=1, source_target_pairs={{0,504},{8,0},{16,8},{24,16},{32,24},{40,32},{48,40},{56,48},{64,5... | collective-permute-start | bytes 1572872 | tf_op jit(solution)/shard_map/ppermute | solution.py:280
  18.7 8.2 %copy-start.4 = (s32[8]{0:T(128)}, s32[8]{0:T(128)S(1)}, u32[]{:S(2)}) copy-start(s32[8]{0:T(128)S(1)} %dynamic_slice.6.active) | copy-start | bytes 100
  62.6 1.3 %copy-start = (bf16[8,1024,128]{2,1,0:T(8,128)(2,1)}, bf16[8,1024,128]{2,1,0:T(8,128)(2,1)S(1)}, u32[]{:S(2)}) copy-start(bf16[8,1024,128]{2,1,0:T(8,128)(2,1)S(1)} %all-to-all-done.g_ref) | copy-start | bytes 6291460
  67.4 34.6 %all-to-all-start.1 = ((bf16[64,16,128]{2,1,0:T(8,128)(2,1)}), bf16[64,16,128]{2,1,0:T(8,128)(2,1)S(1)}, u32[]{:S(2)}, u32[]{:S(2)}) async-start(bf16[64,16,128]{2,1,0:T(8,128)(2,1)} %bitcast.15), calls=%async_computation.1 | async-start | bytes 524288 | tf_op jit(solution)/shard_map/all_to_all | solution.py:364
  97.7 27.2 %collective-permute-start.3 = (bf16[1024,256]{1,0:T(8,128)(2,1)}, bf16[1024,256]{1,0:T(8,128)(2,1)S(1)}, u32[]{:S(2)}, u32[]{:S(2)}) collective-permute-start(bf16[1024,256]{1,0:T(8,128)(2,1)} %get-tuple-element.23), channel_id=1, source_target_pairs={{0,8},{8,16},{16,24},{24,32},{32,40},{40,48},{48,56},{56,64},{64,7... | collective-permute-start | bytes 1572872 | tf_op jit(solution)/shard_map/ppermute | solution.py:280
  99.6 25.3 %collective-permute-start.2 = (bf16[1024,256]{1,0:T(8,128)(2,1)}, bf16[1024,256]{1,0:T(8,128)(2,1)S(1)}, u32[]{:S(2)}, u32[]{:S(2)}) collective-permute-start(bf16[1024,256]{1,0:T(8,128)(2,1)} %get-tuple-element.22), channel_id=1, source_target_pairs={{0,504},{8,0},{16,8},{24,16},{32,24},{40,32},{48,40},{56,48},{64,5... | collective-permute-start | bytes 1572872 | tf_op jit(solution)/shard_map/ppermute | solution.py:280
  102.9 24.2 %all-to-all-start.2 = ((bf16[64,16,128]{2,1,0:T(8,128)(2,1)}), bf16[64,16,128]{2,1,0:T(8,128)(2,1)S(1)}, u32[]{:S(2)}, u32[]{:S(2)}) async-start(bf16[64,16,128]{2,1,0:T(8,128)(2,1)} %broadcast_in_dim.24), calls=%async_computation.2 | async-start | bytes 524288 | tf_op jit(solution)/shard_map/all_to_all | solution.py:370
  127.1 0.7 copy-start.1
